TPU v7x, 32 devices: a whole 2x2x4 slice. The times are simulated.
32 devices in a mesh: shard: 4 (over z), ctx: 8 (over y, x, core).
Axes of the slice: x: 2, y: 2, z: 4, core: 2. Of those that a mesh axis runs over, the one named last changes fastest.
Arguments:
- hidden: bfloat16 [4, 1024, 768], P('shard', 'ctx'), may hold values from -6 to 6
- lengths: int32 [4], P('shard'), may hold values from 256 to 1024, as said below
- row_types: int32 [4, 1024], P('shard'), may hold values 0 or 1
- query_weight: bfloat16 [4, 768, 768], P(None, 'shard'), may hold values from -0.3125 to 0.3125
- query_bias: bfloat16 [4, 768], P(None, 'shard'), may hold values from -3 to 3
- key_weight: bfloat16 [768, 768], P('shard'), may hold values from -0.21875 to 0.21875
- key_bias: bfloat16 [768], P('shard'), may hold values from -3 to 3
- value_weight: bfloat16 [768, 768], P('shard'), may hold values from -0.21875 to 0.21875
- value_bias: bfloat16 [768], P('shard'), may hold values from -0.29882812 to 0.29882812
- out_weight: bfloat16 [768, 768], P('shard'), may hold values from -3 to 3
- out_bias: bfloat16 [768], P('shard'), may hold values from -2 to 2
- norm1_gain: bfloat16 [768], P('shard'), may hold values from 0.5 to 1.5
- norm1_bias: bfloat16 [768], P('shard'), may hold values from -2 to 2
- up_weight: bfloat16 [768, 3072], P('shard'), may hold values from -0.21875 to 0.21875
- up_bias: bfloat16 [3072], P('shard'), may hold values from -2 to 2
- down_weight: bfloat16 [3072, 768], P('shard'), may hold values from -0.109375 to 0.109375
- down_bias: bfloat16 [768], P('shard'), may hold values from -2 to 2
- norm2_gain: bfloat16 [768], P('shard'), may hold values from 0.5 to 1.5
- norm2_bias: bfloat16 [768], P('shard'), may hold values from -2 to 2
- cotangent: bfloat16 [4, 1024, 768], P('shard', 'ctx'), may hold values from -6 to 6
Outputs:
- output: bfloat16 [4, 1024, 768], P('shard', 'ctx')
- input_grad: float32 [4, 1024, 768], P('shard', 'ctx')
- query_weight_grad: float32 [4, 768, 768], P(None, 'shard')
- query_bias_grad: float32 [4, 768], P(None, 'shard')
- key_weight_grad: float32 [768, 768], P('shard')
- key_bias_grad: float32 [768], P('shard')
- value_weight_grad: float32 [768, 768], P('shard')
- value_bias_grad: float32 [768], P('shard')
- out_weight_grad: float32 [768, 768], P('shard')
- out_bias_grad: float32 [768], P('shard')
- norm1_gain_grad: float32 [768], P('shard')
- norm1_bias_grad: float32 [768], P('shard')
- up_weight_grad: float32 [768, 3072], P('shard')
- up_bias_grad: float32 [3072], P('shard')
- down_weight_grad: float32 [3072, 768], P('shard')
- down_bias_grad: float32 [768], P('shard')
- norm2_gain_grad: float32 [768], P('shard')
- norm2_bias_grad: float32 [768], P('shard')
Inputs may be any that keep to these rules, and one draw needn't show every extreme that they name: `lengths`: live slots of each sequence, counted from its start; some sequence is full and some has 256. `row_types`: 0 marks a word slot, 1 an entity slot.
All inputs are finite; a program needn't handle non-finite values. No bound on the sum of `row_types` on one device may be relied on, other than what follows from the above.
Results may differ from a plain program's by a relative error of at most 0.024.
Values may be sent and summed in bfloat16 or wider, within the bound.
No kernel may reach another device: no remote copies, remote signals or barrier semaphores. Data moves between devices by JAX's collectives and lax.ppermute only.
A program may use at most 384 MiB of HBM per device.

v0:
```python
from functools import partial

import jax
import jax.numpy as jnp
from jax import lax
from jax.sharding import PartitionSpec as P

HEADS = 12
HEAD = 64


EPS = 1e-12
SCALE = 0.125
NEG = -1000000000.0


def layer_norm(summed, gain, shift):
    center = summed - jnp.mean(summed, axis=-1, keepdims=True)
    spread = jnp.mean(center * center, axis=-1, keepdims=True)
    return center * lax.rsqrt(spread + EPS) * gain + shift


def gelu_exact(inputs):
    return jax.nn.gelu(inputs, approximate=False)


def pair_queries(query_word, query_entity):
    count = query_word.shape[0]
    return jnp.concatenate(
        [query_word.reshape(count, HEADS, HEAD), query_entity.reshape(count, HEADS, HEAD)], axis=-1
    )


def pair_keys(key_rows, word_rows):
    total = key_rows.shape[0]
    heads_view = key_rows.reshape(total, HEADS, HEAD)
    blank = jnp.zeros_like(heads_view)
    marked = word_rows[:, None, None]
    return jnp.concatenate(
        [jnp.where(marked, heads_view, blank), jnp.where(marked, blank, heads_view)], axis=-1
    )


def masked_scores(paired_query, paired, key_valid):
    scores = jnp.einsum("qhc,khc->hqk", paired_query, paired, preferred_element_type=jnp.float32)
    return jnp.where(key_valid[None, None, :], scores, NEG)


def attend_forward(inputs):
    paired_query, key_rows, value_rows, word_rows, key_valid = inputs
    paired = pair_keys(key_rows, word_rows)
    scores = masked_scores(paired_query, paired, key_valid)
    top = jnp.max(scores, axis=-1, keepdims=True)
    expo = jnp.exp(scores - top)
    weight_sum = jnp.sum(expo, axis=-1, keepdims=True)
    attention = (expo / weight_sum).astype(jnp.bfloat16)
    value_heads = value_rows.reshape(value_rows.shape[0], HEADS, HEAD)
    context = jnp.einsum("hqk,khc->qhc", attention, value_heads, preferred_element_type=jnp.float32)
    context = context.reshape(context.shape[0], HEADS * HEAD).astype(jnp.bfloat16)
    return (context, (top + jnp.log(weight_sum))[..., 0])


def attend_backward(with_keys, inputs):
    paired_query, key_rows, value_rows, word_rows, key_valid, log_total, grad_context = inputs
    total = key_rows.shape[0]
    paired = pair_keys(key_rows, word_rows)
    scores = masked_scores(paired_query, paired, key_valid)
    attention = jnp.exp(scores - log_total[..., None])
    grad_heads = grad_context.reshape(grad_context.shape[0], HEADS, HEAD)
    value_heads = value_rows.reshape(total, HEADS, HEAD)
    grad_attention = jnp.einsum(
        "qhc,khc->hqk", grad_heads, value_heads, preferred_element_type=jnp.float32
    )
    inner_sum = jnp.sum(attention * grad_attention, axis=-1, keepdims=True)
    grad_scores = (attention * (grad_attention - inner_sum)).astype(jnp.bfloat16)
    grad_paired_query = jnp.einsum(
        "hqk,khc->qhc", grad_scores, paired, preferred_element_type=jnp.float32
    )
    grad_paired_keys = jnp.einsum(
        "hqk,qhc->khc", grad_scores, paired_query, preferred_element_type=jnp.float32
    )
    marked = word_rows[:, None, None]
    grad_keys = jnp.where(marked, grad_paired_keys[..., :HEAD], grad_paired_keys[..., HEAD:])
    grad_values = jnp.einsum(
        "hqk,qhc->khc",
        attention.astype(jnp.bfloat16),
        grad_heads,
        preferred_element_type=jnp.float32,
    )
    return (
        grad_paired_query,
        grad_keys.reshape(total, HEADS * HEAD),
        grad_values.reshape(total, HEADS * HEAD),
    )


def local(
    hidden,
    lengths,
    row_types,
    query_weight,
    query_bias,
    key_weight,
    key_bias,
    value_weight,
    value_bias,
    out_weight,
    out_bias,
    norm1_gain,
    norm1_bias,
    up_weight,
    up_bias,
    down_weight,
    down_bias,
    norm2_gain,
    norm2_bias,
    cotangent,
):
    (
        query_mats,
        query_shift,
        key_mat,
        key_shift,
        value_mat,
        value_shift,
        out_mat,
        out_shift,
        gain_one,
        shift_one,
        up_mat,
        up_shift,
        down_mat,
        down_shift,
        gain_two,
        shift_two,
    ) = (
        lax.all_gather(query_weight, "shard", axis=1, tiled=True),
        lax.all_gather(query_bias, "shard", axis=1, tiled=True),
        lax.all_gather(key_weight, "shard", axis=0, tiled=True),
        lax.all_gather(key_bias, "shard", axis=0, tiled=True),
        lax.all_gather(value_weight, "shard", axis=0, tiled=True),
        lax.all_gather(value_bias, "shard", axis=0, tiled=True),
        lax.all_gather(out_weight, "shard", axis=0, tiled=True),
        lax.all_gather(out_bias, "shard", axis=0, tiled=True),
        lax.all_gather(norm1_gain, "shard", axis=0, tiled=True),
        lax.all_gather(norm1_bias, "shard", axis=0, tiled=True),
        lax.all_gather(up_weight, "shard", axis=0, tiled=True),
        lax.all_gather(up_bias, "shard", axis=0, tiled=True),
        lax.all_gather(down_weight, "shard", axis=0, tiled=True),
        lax.all_gather(down_bias, "shard", axis=0, tiled=True),
        lax.all_gather(norm2_gain, "shard", axis=0, tiled=True),
        lax.all_gather(norm2_bias, "shard", axis=0, tiled=True),
    )
    seq_count, slot_count, width = hidden.shape
    total = row_types.shape[1]
    offset = lax.axis_index("ctx") * slot_count
    places = jnp.arange(total, dtype=jnp.int32)
    key_valid = places[None, :] < lengths[:, None]
    word_keys = row_types == 0
    word_rows = lax.dynamic_slice_in_dim(word_keys, offset, slot_count, 1)
    row_valid = lax.dynamic_slice_in_dim(key_valid, offset, slot_count, 1)
    word_cols = word_rows[..., None]
    valid_cols = row_valid[..., None].astype(jnp.float32)
    hidden_wide = hidden.astype(jnp.float32)
    projected = jnp.einsum("bsd,jde->jbse", hidden, query_mats, preferred_element_type=jnp.float32)
    projected = projected + query_shift.astype(jnp.float32)[:, None, None, :]
    query_word = (jnp.where(word_cols, projected[0], projected[2]) * SCALE).astype(jnp.bfloat16)
    query_entity = (jnp.where(word_cols, projected[1], projected[3]) * SCALE).astype(jnp.bfloat16)
    key_rows = (
        jnp.einsum("bsd,de->bse", hidden, key_mat, preferred_element_type=jnp.float32)
        + key_shift.astype(jnp.float32)
    ).astype(jnp.bfloat16)
    value_rows = (
        jnp.einsum("bsd,de->bse", hidden, value_mat, preferred_element_type=jnp.float32)
        + value_shift.astype(jnp.float32)
    ).astype(jnp.bfloat16)
    paired_query = jax.vmap(pair_queries)(query_word, query_entity)
    all_keys, all_values = (
        lax.all_gather(key_rows, "ctx", axis=1, tiled=True),
        lax.all_gather(value_rows, "ctx", axis=1, tiled=True),
    )
    context, log_total = lax.map(
        attend_forward, (paired_query, all_keys, all_values, word_keys, key_valid)
    )
    first_sum = (
        jnp.einsum("bsd,de->bse", context, out_mat, preferred_element_type=jnp.float32)
        + out_shift.astype(jnp.float32)
        + hidden_wide
    )
    first_norm, first_back = jax.vjp(
        layer_norm, first_sum, gain_one.astype(jnp.float32), shift_one.astype(jnp.float32)
    )
    first_low = first_norm.astype(jnp.bfloat16)
    hidden_pre = jnp.einsum(
        "bsd,df->bsf", first_low, up_mat, preferred_element_type=jnp.float32
    ) + up_shift.astype(jnp.float32)
    activated, gelu_back = jax.vjp(gelu_exact, hidden_pre)
    act_low = activated.astype(jnp.bfloat16)
    second_sum = (
        jnp.einsum("bsf,fd->bsd", act_low, down_mat, preferred_element_type=jnp.float32)
        + down_shift.astype(jnp.float32)
        + first_norm
    )
    second_norm, second_back = jax.vjp(
        layer_norm, second_sum, gain_two.astype(jnp.float32), shift_two.astype(jnp.float32)
    )
    output = (second_norm * valid_cols).astype(jnp.bfloat16)
    query_mats, key_mat, value_mat, out_mat, up_mat, down_mat = (
        lax.all_gather(query_weight, "shard", axis=1, tiled=True),
        lax.all_gather(key_weight, "shard", axis=0, tiled=True),
        lax.all_gather(value_weight, "shard", axis=0, tiled=True),
        lax.all_gather(out_weight, "shard", axis=0, tiled=True),
        lax.all_gather(up_weight, "shard", axis=0, tiled=True),
        lax.all_gather(down_weight, "shard", axis=0, tiled=True),
    )
    all_keys, all_values = (
        lax.all_gather(key_rows, "ctx", axis=1, tiled=True),
        lax.all_gather(value_rows, "ctx", axis=1, tiled=True),
    )
    grad_second, grad_gain_two, grad_shift_two = second_back(
        cotangent.astype(jnp.float32) * valid_cols
    )
    grad_down_shift = jnp.sum(grad_second, axis=(0, 1))
    grad_second_low = grad_second.astype(jnp.bfloat16)
    grad_down = jnp.einsum(
        "bsf,bsd->fd", act_low, grad_second_low, preferred_element_type=jnp.float32
    )
    grad_act = jnp.einsum(
        "bsd,fd->bsf", grad_second_low, down_mat, preferred_element_type=jnp.float32
    )
    grad_pre = gelu_back(grad_act)[0]
    grad_up_shift = jnp.sum(grad_pre, axis=(0, 1))
    grad_pre_low = grad_pre.astype(jnp.bfloat16)
    grad_up = jnp.einsum("bsd,bsf->df", first_low, grad_pre_low, preferred_element_type=jnp.float32)
    grad_first_norm = grad_second + jnp.einsum(
        "bsf,df->bsd", grad_pre_low, up_mat, preferred_element_type=jnp.float32
    )
    grad_first, grad_gain_one, grad_shift_one = first_back(grad_first_norm)
    grad_out_shift = jnp.sum(grad_first, axis=(0, 1))
    grad_first_low = grad_first.astype(jnp.bfloat16)
    grad_out = jnp.einsum(
        "bsd,bse->de", context, grad_first_low, preferred_element_type=jnp.float32
    )
    grad_context = jnp.einsum(
        "bse,de->bsd", grad_first_low, out_mat, preferred_element_type=jnp.float32
    ).astype(jnp.bfloat16)
    grad_paired, key_terms, value_terms = lax.map(
        partial(attend_backward, True),
        (paired_query, all_keys, all_values, word_keys, key_valid, log_total, grad_context),
    )
    grad_key_rows, grad_value_rows = (
        lax.psum_scatter(key_terms, "ctx", scatter_dimension=1, tiled=True),
        lax.psum_scatter(value_terms, "ctx", scatter_dimension=1, tiled=True),
    )
    grad_key_shift = jnp.sum(grad_key_rows, axis=(0, 1))
    grad_value_shift = jnp.sum(grad_value_rows, axis=(0, 1))
    grad_key_low = grad_key_rows.astype(jnp.bfloat16)
    grad_value_low = grad_value_rows.astype(jnp.bfloat16)
    grad_key = jnp.einsum("bsd,bse->de", hidden, grad_key_low, preferred_element_type=jnp.float32)
    grad_value = jnp.einsum(
        "bsd,bse->de", hidden, grad_value_low, preferred_element_type=jnp.float32
    )
    grad_query_word = grad_paired[..., :HEAD].reshape(seq_count, slot_count, width) * SCALE
    grad_query_entity = grad_paired[..., HEAD:].reshape(seq_count, slot_count, width) * SCALE
    blank = jnp.zeros_like(grad_query_word)
    grad_projected = jnp.stack(
        [
            jnp.where(word_cols, grad_query_word, blank),
            jnp.where(word_cols, grad_query_entity, blank),
            jnp.where(word_cols, blank, grad_query_word),
            jnp.where(word_cols, blank, grad_query_entity),
        ]
    )
    grad_query_shift = jnp.sum(grad_projected, axis=(1, 2))
    grad_projected_low = grad_projected.astype(jnp.bfloat16)
    grad_query = jnp.einsum(
        "bsd,jbse->jde", hidden, grad_projected_low, preferred_element_type=jnp.float32
    )
    input_grad = grad_first + jnp.einsum(
        "jbse,jde->bsd", grad_projected_low, query_mats, preferred_element_type=jnp.float32
    )
    input_grad = input_grad + jnp.einsum(
        "bse,de->bsd", grad_key_low, key_mat, preferred_element_type=jnp.float32
    )
    input_grad = input_grad + jnp.einsum(
        "bse,de->bsd", grad_value_low, value_mat, preferred_element_type=jnp.float32
    )
    (
        grad_query,
        grad_query_shift,
        grad_key,
        grad_key_shift,
        grad_value,
        grad_value_shift,
        grad_out,
        grad_out_shift,
        grad_gain_one,
        grad_shift_one,
        grad_up,
        grad_up_shift,
        grad_down,
        grad_down_shift,
        grad_gain_two,
        grad_shift_two,
    ) = (
        lax.psum_scatter(
            grad_query.astype(jnp.bfloat16), "shard", scatter_dimension=1, tiled=True
        ).astype(jnp.float32),
        lax.psum_scatter(
            grad_query_shift.astype(jnp.bfloat16), "shard", scatter_dimension=1, tiled=True
        ).astype(jnp.float32),
        lax.psum_scatter(
            grad_key.astype(jnp.bfloat16), "shard", scatter_dimension=0, tiled=True
        ).astype(jnp.float32),
        lax.psum_scatter(
            grad_key_shift.astype(jnp.bfloat16), "shard", scatter_dimension=0, tiled=True
        ).astype(jnp.float32),
        lax.psum_scatter(
            grad_value.astype(jnp.bfloat16), "shard", scatter_dimension=0, tiled=True
        ).astype(jnp.float32),
        lax.psum_scatter(
            grad_value_shift.astype(jnp.bfloat16), "shard", scatter_dimension=0, tiled=True
        ).astype(jnp.float32),
        lax.psum_scatter(
            grad_out.astype(jnp.bfloat16), "shard", scatter_dimension=0, tiled=True
        ).astype(jnp.float32),
        lax.psum_scatter(
            grad_out_shift.astype(jnp.bfloat16), "shard", scatter_dimension=0, tiled=True
        ).astype(jnp.float32),
        lax.psum_scatter(
            grad_gain_one.astype(jnp.bfloat16), "shard", scatter_dimension=0, tiled=True
        ).astype(jnp.float32),
        lax.psum_scatter(
            grad_shift_one.astype(jnp.bfloat16), "shard", scatter_dimension=0, tiled=True
        ).astype(jnp.float32),
        lax.psum_scatter(
            grad_up.astype(jnp.bfloat16), "shard", scatter_dimension=0, tiled=True
        ).astype(jnp.float32),
        lax.psum_scatter(
            grad_up_shift.astype(jnp.bfloat16), "shard", scatter_dimension=0, tiled=True
        ).astype(jnp.float32),
        lax.psum_scatter(
            grad_down.astype(jnp.bfloat16), "shard", scatter_dimension=0, tiled=True
        ).astype(jnp.float32),
        lax.psum_scatter(
            grad_down_shift.astype(jnp.bfloat16), "shard", scatter_dimension=0, tiled=True
        ).astype(jnp.float32),
        lax.psum_scatter(
            grad_gain_two.astype(jnp.bfloat16), "shard", scatter_dimension=0, tiled=True
        ).astype(jnp.float32),
        lax.psum_scatter(
            grad_shift_two.astype(jnp.bfloat16), "shard", scatter_dimension=0, tiled=True
        ).astype(jnp.float32),
    )
    reduced = lax.psum(
        (
            grad_query,
            grad_query_shift,
            grad_key,
            grad_key_shift,
            grad_value,
            grad_value_shift,
            grad_out,
            grad_out_shift,
            grad_gain_one,
            grad_shift_one,
            grad_up,
            grad_up_shift,
            grad_down,
            grad_down_shift,
            grad_gain_two,
            grad_shift_two,
        ),
        "ctx",
    )
    return (output, input_grad) + tuple(reduced)


def solution(mesh):
    placed = (
        P("shard", "ctx", None),
        P("shard"),
        P("shard", None),
        P(None, "shard", None),
        P(None, "shard"),
        P("shard", None),
        P("shard"),
        P("shard", None),
        P("shard"),
        P("shard", None),
        P("shard"),
        P("shard"),
        P("shard"),
        P("shard", None),
        P("shard"),
        P("shard", None),
        P("shard"),
        P("shard"),
        P("shard"),
        P("shard", "ctx", None),
    )
    return jax.shard_map(
        local,
        mesh=mesh,
        in_specs=placed,
        out_specs=(
            P("shard", "ctx", None),
            P("shard", "ctx", None),
            P(None, "shard", None),
            P(None, "shard"),
            P("shard", None),
            P("shard"),
            P("shard", None),
            P("shard"),
            P("shard", None),
            P("shard"),
            P("shard"),
            P("shard"),
            P("shard", None),
            P("shard"),
            P("shard", None),
            P("shard"),
            P("shard"),
            P("shard"),
        ),
        check_vma=False,
    )
```

profile of v0, /device:TPU:0, one launch (start us, length us, event | category | flops | bytes accessed | tf_op | source)
XLA Modules:
  0.0 1241.4 jit_solution(12676532006705603234)
XLA Ops:
  16.6 21.6 %all-reduce.20 = (bf16[768]{0:T(1024)(128)(2,1)S(1)}, bf16[768]{0:T(1024)(128)(2,1)S(1)}, bf16[768]{0:T(1024)(128)(2,1)S(1)}, bf16[768]{0:T(1024)(128)(2,1)S(1)}...) all-reduce(bf16[768]{0:T(1024)(128)(2,1)S(1)} %dynamic-update-slice, ...), channel_id=1, replica_groups=mesh['shard'=4,'ctx'=8] {'shard'}, use_global_device_ids=true, to_apply=%add | all-reduce | flops 5376 | bytes 21504
  45.7 28.5 %all-gather.13.cloned.1.call-done = bf16[768,768]{1,0:T(8,128)(2,1)} async-done(((bf16[192,768]{1,0:T(8,128)(2,1)}), bf16[768,768]{1,0:T(8,128)(2,1)}) %all-gather.13.cloned.1.call-update) | async-done | bytes 1179664 | tf_op jit(solution)/shard_map/all_gather | solution.py:141
  82.3 11.9 all-gather.2
  94.3 13.3 %all-gather.3 = bf16[4,1,768]{2,1,0:T(2,128)(2,1)S(1)} all-gather(bf16[1,1,768]{2,1,0:T(2,128)(2,1)S(1)} %reshape.836), channel_id=1, replica_groups=mesh['shard'=4,'ctx'=8] {'shard'}, dimensions={0}, use_global_device_ids=true | all-gather | bytes 7680 | tf_op jit(solution)/shard_map/all_gather | solution.py:148
  115.0 14.5 %all-gather.25.cloned.1.call-done = bf16[1024,768]{1,0:T(8,128)(2,1)} async-done(((bf16[128,768]{1,0:T(8,128)(2,1)}), bf16[1024,768]{1,0:T(8,128)(2,1)}) %all-gather.25.cloned.1.call-update) | async-done | bytes 1572880 | tf_op jit(solution)/shard_map/all_gather | solution.py:180
  135.6 84.7 %all-gather.15.cloned.1.call-done = bf16[4,768,768]{2,1,0:T(8,128)(2,1)} async-done(((bf16[4,192,768]{2,1,0:T(8,128)(2,1)}), bf16[4,768,768]{2,1,0:T(8,128)(2,1)}) %all-gather.15.cloned.1.call-update) | async-done | bytes 4718608 | tf_op jit(solution)/shard_map/all_gather | solution.py:137
  234.4 15.9 %all-gather.19.cloned.1.call-done = bf16[768,768]{1,0:T(8,128)(2,1)} async-done(((bf16[192,768]{1,0:T(8,128)(2,1)}), bf16[768,768]{1,0:T(8,128)(2,1)}) %all-gather.19.cloned.1.call-update) | async-done | bytes 1179664 | tf_op jit(solution)/shard_map/all_gather | solution.py:143
  253.8 86.8 %all-gather.21.cloned.1.call-done = bf16[768,3072]{1,0:T(8,128)(2,1)} async-done(((bf16[192,3072]{1,0:T(8,128)(2,1)}), bf16[768,3072]{1,0:T(8,128)(2,1)}) %all-gather.21.cloned.1.call-update) | async-done | bytes 4718608 | tf_op jit(solution)/shard_map/all_gather | solution.py:147
  340.6 8.7 multiply_convert_fusion.1
  349.3 80.7 %all-gather.23.cloned.1.call-done = bf16[3072,768]{1,0:T(8,128)(2,1)} async-done(((bf16[768,768]{1,0:T(8,128)(2,1)}), bf16[3072,768]{1,0:T(8,128)(2,1)}) %all-gather.23.cloned.1.call-update) | async-done | bytes 4718608 | tf_op jit(solution)/shard_map/all_gather | solution.py:149
  460.5 9.0 copy.126
  483.8 6.2 copy.124
  495.0 144.9 %all-reduce.27.cloned.1.call-done = bf16[4,768,768]{2,0,1:T(4,128)(2,1)} async-done(((bf16[4,768,768]{2,0,1:T(4,128)(2,1)}), bf16[4,768,768]{2,0,1:T(4,128)(2,1)}) %all-reduce.27.cloned.1.call-update) | async-done | bytes 4718608
  643.0 45.2 %reduce-scatter.17.cloned.1.call-done = f32[1,128,768]{1,2,0:T(8,128)} async-done(((f32[1,1024,768]{1,2,0:T(8,128)}), f32[1,128,768]{1,2,0:T(8,128)}) %reduce-scatter.17.cloned.1.call-update) | async-done | bytes 393232 | tf_op jit(solution)/shard_map/reduce_scatter | solution.py:253
  691.2 46.5 %reduce-scatter.15.cloned.1.call-done = f32[1,128,768]{1,2,0:T(8,128)} async-done(((f32[1,1024,768]{1,2,0:T(8,128)}), f32[1,128,768]{1,2,0:T(8,128)}) %reduce-scatter.15.cloned.1.call-update) | async-done | bytes 393232 | tf_op jit(solution)/shard_map/reduce_scatter | solution.py:252
  750.6 9.4 reduce-scatter.25.cloned.1.call-done
  760.9 29.6 %reduce-scatter.19.cloned.1.call-done = bf16[192,768]{1,0:T(8,128)(2,1)} async-done(((bf16[768,768]{1,0:T(8,128)(2,1)}), bf16[192,768]{1,0:T(8,128)(2,1)}) %reduce-scatter.19.cloned.1.call-update) | async-done | bytes 294928 | tf_op jit(solution)/shard_map/reduce_scatter | solution.py:324
  792.9 16.9 %all-reduce.19 = (bf16[768]{0:T(1024)(128)(2,1)S(1)}, bf16[768]{0:T(1024)(128)(2,1)S(1)}, bf16[768]{0:T(1024)(128)(2,1)S(1)}, bf16[768]{0:T(1024)(128)(2,1)S(1)}...) all-reduce(bf16[768]{0:T(1024)(128)(2,1)S(1)} %dynamic-update-slice, ...), channel_id=1, replica_groups=mesh['shard'=4,'ctx'=8] {'shard'}, use_global_device_ids=true, to_apply=%add.7 | all-reduce | flops 9984 | bytes 39936
  818.1 37.8 %all-reduce.25.cloned.1.call-done = f32[4,192,768]{2,0,1:T(4,128)} async-done(((f32[4,192,768]{2,0,1:T(4,128)}), f32[4,192,768]{2,0,1:T(4,128)}) %all-reduce.25.cloned.1.call-update) | async-done | bytes 2359312 | tf_op jit(solution)/shard_map/psum | solution.py:355
  859.4 27.3 %reduce-scatter.29.cloned.1.call-done = bf16[192,768]{1,0:T(8,128)(2,1)} async-done(((bf16[768,768]{1,0:T(8,128)(2,1)}), bf16[192,768]{1,0:T(8,128)(2,1)}) %reduce-scatter.29.cloned.1.call-update) | async-done | bytes 294928
  887.8 29.6 %reduce-scatter.27.cloned.1.call-done = bf16[192,768]{1,0:T(8,128)(2,1)} async-done(((bf16[768,768]{1,0:T(8,128)(2,1)}), bf16[192,768]{1,0:T(8,128)(2,1)}) %reduce-scatter.27.cloned.1.call-update) | async-done | bytes 294928
  918.5 85.0 %reduce-scatter.21.cloned.1.call-done = bf16[192,3072]{1,0:T(8,128)(2,1)} async-done(((bf16[768,3072]{1,0:T(8,128)(2,1)}), bf16[192,3072]{1,0:T(8,128)(2,1)}) %reduce-scatter.21.cloned.1.call-update) | async-done | bytes 1179664 | tf_op jit(solution)/shard_map/reduce_scatter | solution.py:336
  1003.5 88.0 %reduce-scatter.23.cloned.1.call-done = bf16[768,768]{1,0:T(8,128)(2,1)} async-done(((bf16[3072,768]{1,0:T(8,128)(2,1)}), bf16[768,768]{1,0:T(8,128)(2,1)}) %reduce-scatter.23.cloned.1.call-update) | async-done | bytes 1179664 | tf_op jit(solution)/shard_map/reduce_scatter | solution.py:342
  1091.5 140.8 %all-reduce.28 = (f32[4,192]{1,0:T(4,128)}, f32[192,768]{0,1:T(8,128)S(1)}, f32[192]{0:T(256)}, f32[192,768]{0,1:T(8,128)S(1)}, f32[192]{0:T(256)}, /*index=5*/f...) all-reduce(bf16[4,192]{1,0:T(4,128)(2,1)S(1)} %copy.135, ...), channel_id=1, replica_groups=mesh['shard'=4,'ctx'=8] {'ctx'}, use_global_device_ids=true, to_apply=%region_17.18 | all-reduce | flops 1625088 | bytes 9755136 | tf_op jit(solution)/shard_map/psum | solution.py:355
  (322 shorter events, 140.4 us)
Async XLA Ops:
  7.2 67.0 %copy-start.7 = (bf16[1,128,768]{2,1,0:T(8,128)(2,1)S(1)}, bf16[1,128,768]{2,1,0:T(8,128)(2,1)}, u32[]{:S(2)}) copy-start(bf16[1,128,768]{2,1,0:T(8,128)(2,1)} %param.20) | copy-start | bytes 589828
  7.2 36.0 %all-gather.17.cloned.1.call-start = ((), (), s32[]{:S(2)}) async-start(), calls=%async_computation.10 | async-start | bytes 1474560 | tf_op jit(solution)/shard_map/all_gather | solution.py:139
  7.9 66.3 %all-gather.13.cloned.1.call-start = ((), (), s32[]{:S(2)}) async-start(), calls=%async_computation.8 | async-start | bytes 1474560 | tf_op jit(solution)/shard_map/all_gather | solution.py:141
  8.7 101.7 %all-gather.27.cloned.1.call-start = ((), (), s32[]{:S(2)}) async-start(), calls=%async_computation.21 | async-start | bytes 1769472 | tf_op jit(solution)/shard_map/all_gather | solution.py:179
  45.6 83.8 %all-gather.25.cloned.1.call-start = ((), (), s32[]{:S(2)}) async-start(), calls=%async_computation.20 | async-start | bytes 1769472 | tf_op jit(solution)/shard_map/all_gather | solution.py:180
  76.5 143.7 %all-gather.15.cloned.1.call-start = ((), (), s32[]{:S(2)}) async-start(), calls=%async_computation.9 | async-start | bytes 5898240 | tf_op jit(solution)/shard_map/all_gather | solution.py:137
  77.1 173.2 %all-gather.19.cloned.1.call-start = ((), (), s32[]{:S(2)}) async-start(), calls=%async_computation.11 | async-start | bytes 1474560 | tf_op jit(solution)/shard_map/all_gather | solution.py:143
  77.7 262.9 %all-gather.21.cloned.1.call-start = ((), (), s32[]{:S(2)}) async-start(), calls=%async_computation.12 | async-start | bytes 5898240 | tf_op jit(solution)/shard_map/all_gather | solution.py:147
  78.5 351.5 %all-gather.23.cloned.1.call-start = ((), (), s32[]{:S(2)}) async-start(), calls=%async_computation.13 | async-start | bytes 5898240 | tf_op jit(solution)/shard_map/all_gather | solution.py:149
  79.2 560.8 %all-reduce.27.cloned.1.call-start = ((), (), s32[]{:S(2)}) async-start(), calls=%async_computation.25 | async-start | bytes 9437184
  234.4 106.2 %copy-start.41 = (f32[768]{0:T(1024)S(1)}, f32[768]{0:T(1024)}, u32[]{:S(2)}) copy-start(f32[768]{0:T(1024)} %convert_element_type.266) | copy-start | bytes 9220
  469.5 218.8 %reduce-scatter.17.cloned.1.call-start = ((), (), s32[]{:S(2)}) async-start(), calls=%async_computation.15 | async-start | bytes 3538944 | tf_op jit(solution)/shard_map/reduce_scatter | solution.py:253
  476.2 261.5 %reduce-scatter.15.cloned.1.call-start = ((), (), s32[]{:S(2)}) async-start(), calls=%async_computation.14 | async-start | bytes 3538944 | tf_op jit(solution)/shard_map/reduce_scatter | solution.py:252
  490.1 269.9 %reduce-scatter.25.cloned.1.call-start = ((), (), s32[]{:S(2)}) async-start(), calls=%async_computation.22 | async-start | bytes 245760
  492.7 297.8 %reduce-scatter.19.cloned.1.call-start = ((), (), s32[]{:S(2)}) async-start(), calls=%async_computation.17 | async-start | bytes 1474560 | tf_op jit(solution)/shard_map/reduce_scatter | solution.py:324
  494.3 361.5 %all-reduce.25.cloned.1.call-start = ((), (), s32[]{:S(2)}) async-start(), calls=%async_computation.16 | async-start | bytes 4718592 | tf_op jit(solution)/shard_map/psum | solution.py:355
  643.0 243.7 %reduce-scatter.29.cloned.1.call-start = ((), (), s32[]{:S(2)}) async-start(), calls=%async_computation.24 | async-start | bytes 1474560
  691.2 226.2 %reduce-scatter.27.cloned.1.call-start = ((), (), s32[]{:S(2)}) async-start(), calls=%async_computation.23 | async-start | bytes 1474560
  740.7 262.8 %reduce-scatter.21.cloned.1.call-start = ((), (), s32[]{:S(2)}) async-start(), calls=%async_computation.18 | async-start | bytes 5898240 | tf_op jit(solution)/shard_map/reduce_scatter | solution.py:336
  744.5 347.0 %reduce-scatter.23.cloned.1.call-start = ((), (), s32[]{:S(2)}) async-start(), calls=%async_computation.19 | async-start | bytes 5898240 | tf_op jit(solution)/shard_map/reduce_scatter | solution.py:342
  749.3 60.9 %copy-start.19 = (bf16[768,768]{1,0:T(8,128)(2,1)S(1)}, bf16[768,768]{1,0:T(8,128)(2,1)}, u32[]{:S(2)}) copy-start(bf16[768,768]{1,0:T(8,128)(2,1)} %all-gather.13.cloned.1.call-done) | copy-start | bytes 3538948
  750.5 61.4 %copy-start.18 = (bf16[768,768]{1,0:T(8,128)(2,1)S(1)}, bf16[768,768]{1,0:T(8,128)(2,1)}, u32[]{:S(2)}) copy-start(bf16[768,768]{1,0:T(8,128)(2,1)} %all-gather.17.cloned.1.call-done) | copy-start | bytes 3538948
  750.6 61.3 %copy-start.24 = (f32[1,128,768]{1,2,0:T(8,128)S(1)}, f32[1,128,768]{1,2,0:T(8,128)}, u32[]{:S(2)}) copy-start(f32[1,128,768]{1,2,0:T(8,128)} %reduce-scatter.15.cloned.1.call-done) | copy-start | bytes 1179652
  859.4 232.1 %copy-start.40 = (bf16[192,768]{1,0:T(8,128)(2,1)S(1)}, bf16[192,768]{1,0:T(8,128)(2,1)}, u32[]{:S(2)}) copy-start(bf16[192,768]{1,0:T(8,128)(2,1)} %reduce-scatter.19.cloned.1.call-done) | copy-start | bytes 884740
  (82 other events, 480.4 us)
Sparse Core Ops, SparseCore 0:
  9.6 33.5 all-gather.16
  44.8 29.3 all-gather.12
  76.7 24.7 all-gather.26
  103.8 25.5 all-gather.24
  130.8 89.3 all-gather.14
  221.7 28.6 all-gather.18
  252.0 88.6 all-gather.20
  342.2 87.7 all-gather.22
  469.6 170.3 all-reduce.26
  643.2 44.9 reduce-scatter.16
  691.6 46.0 reduce-scatter.14
  740.4 19.5 reduce-scatter.24
  762.9 27.5 reduce-scatter.18
  794.2 61.5 all-reduce.24
  858.0 28.6 reduce-scatter.28
  889.4 27.9 reduce-scatter.26
  919.5 83.8 reduce-scatter.20
  1005.6 85.7 reduce-scatter.22
where the time goes:
time: 1250 us; the launch traced here: 1240 us
  waiting for transfers between devices  863 us (69%)
  blocking collectives  204 us (16%)
  matrix products  72.7 us (6%)
  local copies, waits for them, and re-layouts  57 us (5%)
  other arithmetic  24.8 us (2%)
  between operations  18.3 us (1%)
    unnamed x22, waiting for transfers between devices  215 us
    psum x1, blocking collectives, local(): lax.psum((grad_query, grad_query_shift, grad_key, grad_key_shift, grad_va...  141 us
    reduce_scatter x1, waiting for transfers between devices, local(): lax.psum_scatter(grad_down.astype(jnp.bfloat16), 'shard', scatter_dimensi...  88 us
    all_gather x1, waiting for transfers between devices, local(): lax.all_gather(up_weight, 'shard', axis=0, tiled=True)  86.8 us
    reduce_scatter x1, waiting for transfers between devices, local(): lax.psum_scatter(grad_up.astype(jnp.bfloat16), 'shard', scatter_dimension...  85 us
    all_gather x1, waiting for transfers between devices, local(): lax.all_gather(query_weight, 'shard', axis=1, tiled=True)  84.7 us
    all_gather x1, waiting for transfers between devices, local(): lax.all_gather(down_weight, 'shard', axis=0, tiled=True)  80.7 us
    reduce_scatter x1, waiting for transfers between devices, local(): lax.psum_scatter(key_terms, 'ctx', scatter_dimension=1, tiled=True)  46.5 us
  transfers between devices with their start and end apart: 18, of which 17 were waited for; matrix products, arithmetic and copies ran while one was open for 8% of the time, Pallas kernels for 0%

commit v1 on v0

v1 whole, which is shorter than its diff:
```python
from functools import partial

import jax
import jax.numpy as jnp
from jax import lax
from jax.experimental import pallas as pl
from jax.experimental.pallas import tpu as pltpu
from jax.sharding import PartitionSpec as P

HEADS = 12
HEAD = 64
CHIPS = 4
CORES = 2
LOCAL_HEADS = HEADS // CHIPS
COLS = LOCAL_HEADS * HEAD
PAIR = 2 * HEAD
WIDE = LOCAL_HEADS * PAIR

EPS = 1e-12
SCALE = 0.125
NEG = -1000000000.0
F32 = jnp.float32
BF16 = jnp.bfloat16

SMEM = pl.BlockSpec(memory_space=pltpu.SMEM)
VMEM = pl.BlockSpec(memory_space=pltpu.VMEM)


def sds(shape, dtype):
    return jax.ShapeDtypeStruct(shape, dtype)


def dot(left, right, over_left, over_right):
    return lax.dot_general(
        left, right, (((over_left,), (over_right,)), ((), ())), preferred_element_type=F32
    )


def run(body, name, outs, scalars, *arrays, scratch=(), flops=0, vmem=48):
    many = isinstance(outs, (list, tuple))
    size = sum(a.size * a.dtype.itemsize for a in arrays)
    return pl.pallas_call(
        body,
        out_shape=outs,
        in_specs=[SMEM] + [VMEM] * len(arrays),
        out_specs=[VMEM] * len(outs) if many else VMEM,
        scratch_shapes=list(scratch),
        name=name,
        cost_estimate=pl.CostEstimate(flops=flops, bytes_accessed=size, transcendentals=0),
        compiler_params=pltpu.CompilerParams(vmem_limit_bytes=vmem << 20),
    )(scalars, *arrays)


SHARD, CHIP, CORE, SPOT, SIDE = range(5)


def prep_qkv_body(sc, qw, kw, vw, out):
    rows = kw.shape[0]
    half = rows // 2
    for chip in range(CHIPS):
        for core in range(CORES):

            @pl.when((sc[CHIP] == chip) & (sc[CORE] == core))
            def _():
                lo = chip * COLS
                first = qw[2 * core, :, lo : lo + COLS]
                second = qw[2 * core + 1, :, lo : lo + COLS]
                mix = []
                for h in range(LOCAL_HEADS):
                    mix += [
                        first[:, h * HEAD : (h + 1) * HEAD],
                        second[:, h * HEAD : (h + 1) * HEAD],
                    ]
                out[0:rows, :] = jnp.concatenate(mix, axis=1)
                src = kw if core == 0 else vw
                out[rows:, 0:COLS] = src[0:half, lo : lo + COLS]
                out[rows:, COLS:] = src[half:rows, lo : lo + COLS]


def prep_mlp_body(sc, up, down, out):
    rows, ff = up.shape
    width = down.shape[1]
    part = ff // 4
    side = part // 2
    for chip_x in range(2):

        @pl.when(sc[SIDE] == chip_x)
        def _():
            for piece in range(4):
                lo = piece * part + chip_x * side
                row = (piece // 2) * rows
                col = (piece % 2) * side
                out[row : row + rows, col : col + side] = up[:, lo : lo + side]

    out[2 * rows :, :] = down[...]


def assemble_mlp_body(shards, sc, *refs):
    pieces, (wup, wdn) = refs[: 4 * shards], refs[4 * shards :]
    rows = wup.shape[0] // shards
    part = wdn.shape[0] // shards
    width = wdn.shape[1]
    small = rows // 4
    for index, piece in enumerate(pieces):
        shift, rel = index // 4, index % 4
        owner = lax.rem(sc[SHARD] + shards - shift, shards)
        spot = sc[SPOT] ^ rel
        at = pl.multiple_of(owner * rows + spot * small, small)
        wup[pl.ds(at, small), 0:width] = piece[0:small, :]
        wup[pl.ds(at, small), width:] = piece[small : 2 * small, :]
        at = pl.multiple_of(owner * part + spot * (part // 4), part // 4)
        wdn[pl.ds(at, part // 4), :] = piece[2 * small :, :]


def assemble_out_body(shards, sc, own, other, wo):
    rows = wo.shape[0] // shards
    small = rows // 4
    for core, ref in enumerate((own, other)):
        for half in range(2):
            for shift in range(shards):
                owner = lax.rem(sc[SHARD] + shards - shift, shards)
                spot = sc[SPOT] ^ (half * 2 + core)
                at = pl.multiple_of(owner * rows + spot * small, small)
                wo[pl.ds(at, small), :] = ref[half * shards + shift]


def qkv_body(shards, sc, bias, meta, *refs):
    own_x, other_x = refs[0:4], refs[4:8]
    own_w, other_w = refs[8 : 8 + shards], refs[8 + shards : 8 + 2 * shards]
    wall, pq, pk, vv = refs[8 + 2 * shards :]
    slots = own_x[0].shape[0]
    rows = wall.shape[1] // shards
    half = rows // 2
    for which, pieces in enumerate((own_w, other_w)):
        group = sc[CORE] ^ which
        keep = (group == 0).astype(F32).astype(BF16)
        for shift in range(shards):
            piece = pieces[shift]
            owner = lax.rem(sc[SHARD] + shards - shift, shards)
            at = pl.multiple_of(owner * rows, half)
            wall[group, pl.ds(at, rows), 0:WIDE] = piece[0:rows, :]
            for part in range(2):
                mix = []
                for h in range(LOCAL_HEADS):
                    lo = part * COLS + h * HEAD
                    one = piece[rows:, lo : lo + HEAD]
                    mix += [one, one * keep]
                low = pl.multiple_of(owner * rows + part * half, half)
                wall[group, pl.ds(low, half), WIDE:] = jnp.concatenate(mix, axis=1)
    flags = meta[...].T
    lane = lax.broadcasted_iota(jnp.int32, (1, WIDE), 1)
    left = (lane % PAIR) < HEAD
    for block in range(8):
        tokens = (own_x[block] if block < 4 else other_x[block - 4])[...]
        word = flags[:, block : block + 1] > 0
        at = slice(block * slots, (block + 1) * slots)
        if block < 4:
            first = dot(tokens, wall[0], 1, 0) + bias[0:1, :]
            second = dot(tokens, wall[1], 1, 0) + bias[1:2, :]
            query = jnp.where(word, first[:, 0:WIDE], second[:, 0:WIDE]) * SCALE
            pq[at, :] = query.astype(BF16)
            key, value = first[:, WIDE:], second[:, WIDE:]
        else:
            key = dot(tokens, wall[0, :, WIDE:], 1, 0) + bias[0:1, WIDE:]
            value = dot(tokens, wall[1, :, WIDE:], 1, 0) + bias[1:2, WIDE:]
        pk[at, :] = jnp.where(left == word, key, 0.0).astype(BF16)
        vv[at, :] = value.astype(BF16)


def attend_body(step, pq, pk, vv, valid, probs, cx):
    head = pl.program_id(0)
    count = pq.shape[0]
    slots = count // 4
    keep = valid[...] > 0
    keys = pk[...]
    values = vv[...]
    for start in range(0, count, step):
        scores = dot(pq[start : start + step, :], keys, 1, 1)
        scores = jnp.where(keep, scores, NEG)
        top = jnp.max(scores, axis=-1, keepdims=True)
        expo = jnp.exp(scores - top)
        share = 1.0 / jnp.sum(expo, axis=-1, keepdims=True)
        low = (expo * share).astype(BF16)
        probs[0, start : start + step, :] = low
        mixed = dot(low, values, 1, 0)[:, 0:HEAD].astype(BF16)
        for h in range(LOCAL_HEADS):

            @pl.when(head == h)
            def _():
                for at in range(0, step, slots):
                    block = (start + at) // slots
                    mid = at + slots // 2
                    cx[block, :, h * HEAD : (h + 1) * HEAD] = mixed[at:mid]
                    cx[block, :, COLS + h * HEAD : COLS + (h + 1) * HEAD] = mixed[mid : at + slots]


def attend(pq, pk, vv, valid, slots):
    count, keys = pq.shape[0], pk.shape[0]
    step = 2 * slots if keys <= 2048 else slots
    return pl.pallas_call(
        partial(attend_body, step),
        grid=(LOCAL_HEADS,),
        in_specs=[
            pl.BlockSpec((count, PAIR), lambda h: (0, h)),
            pl.BlockSpec((keys, PAIR), lambda h: (0, h)),
            pl.BlockSpec((keys, PAIR), lambda h: (0, h)),
            pl.BlockSpec((1, keys), lambda h: (0, 0)),
        ],
        out_specs=[
            pl.BlockSpec((1, count, keys), lambda h: (h, 0, 0)),
            pl.BlockSpec((4, slots // 2, 2 * COLS), lambda h: (0, 0, 0)),
        ],
        out_shape=[
            sds((LOCAL_HEADS, count, keys), BF16),
            sds((4, slots // 2, 2 * COLS), BF16),
        ],
        name="attend",
        cost_estimate=pl.CostEstimate(
            flops=4 * LOCAL_HEADS * count * keys * PAIR,
            bytes_accessed=LOCAL_HEADS * count * keys * 2,
            transcendentals=LOCAL_HEADS * count * keys,
        ),
        compiler_params=pltpu.CompilerParams(vmem_limit_bytes=52 << 20),
    )(pq, pk, vv, valid)


def attend_back_body(step, gc0, gc1, gc2, gc3, pq, pk, vv, probs, dq, dk, dv, gcs):
    head = pl.program_id(0)
    count = pq.shape[0]
    slots = count // 4
    half = slots // 2

    @pl.when(head == 0)
    def _():
        gcs[...] = jnp.zeros_like(gcs)
        for block, ref in enumerate((gc0, gc1, gc2, gc3)):
            for h in range(LOCAL_HEADS):
                lo = block * slots
                gcs[h, lo : lo + half, 0:HEAD] = ref[:, h * HEAD : (h + 1) * HEAD]
                gcs[h, lo + half : lo + slots, 0:HEAD] = ref[
                    :, COLS + h * HEAD : COLS + (h + 1) * HEAD
                ]

    keys = pk[...]
    values = vv[...]
    for start in range(0, count, step):
        grad = gcs[head, start : start + step, :]
        low = probs[0, start : start + step, :]
        wide = low.astype(F32)
        moved = dot(grad, values, 1, 1)
        inner = jnp.sum(wide * moved, axis=-1, keepdims=True)
        ds = (wide * (moved - inner)).astype(BF16)
        query = pq[start : start + step, :]
        dq[start : start + step, :] = dot(ds, keys, 1, 0)
        key_part = dot(ds, query, 0, 0)
        value_part = dot(low, grad, 0, 0)
        if start == 0:
            dk[...] = key_part
            dv[...] = value_part
        else:
            dk[...] += key_part
            dv[...] += value_part


def attend_back(pieces, pq, pk, vv, probs, slots):
    count, keys = pq.shape[0], pk.shape[0]
    step = 2 * slots if keys <= 2048 else slots
    piece = pl.BlockSpec((slots // 2, 2 * COLS), lambda h: (0, 0))
    rows = pl.BlockSpec((count, PAIR), lambda h: (0, h))
    cols = pl.BlockSpec((keys, PAIR), lambda h: (0, h))
    return pl.pallas_call(
        partial(attend_back_body, step),
        grid=(LOCAL_HEADS,),
        in_specs=[piece] * 4
        + [rows, cols, cols, pl.BlockSpec((1, count, keys), lambda h: (h, 0, 0))],
        out_specs=[rows, cols, cols],
        out_shape=[sds((count, WIDE), F32), sds((keys, WIDE), F32), sds((keys, WIDE), F32)],
        scratch_shapes=[pltpu.VMEM((LOCAL_HEADS, count, PAIR), BF16)],
        name="attend_back",
        cost_estimate=pl.CostEstimate(
            flops=8 * LOCAL_HEADS * count * keys * PAIR,
            bytes_accessed=LOCAL_HEADS * count * keys * 2,
            transcendentals=0,
        ),
        compiler_params=pltpu.CompilerParams(vmem_limit_bytes=56 << 20),
    )(*pieces, pq, pk, vv, probs)


def unpack(piece):
    return jnp.concatenate([piece[:, 0:COLS], piece[:, COLS:]], axis=0)


def normalize(summed):
    center = summed - jnp.mean(summed, axis=-1, keepdims=True)
    spread = jnp.mean(center * center, axis=-1, keepdims=True)
    rate = lax.rsqrt(spread + EPS)
    return center * rate, rate


def norm_back(grad, unit, rate, gain):
    scaled = grad * gain
    mean_one = jnp.mean(scaled, axis=-1, keepdims=True)
    mean_two = jnp.mean(scaled * unit, axis=-1, keepdims=True)
    return rate * (scaled - mean_one - unit * mean_two)


def total(values):
    return jnp.sum(values, axis=0, keepdims=True)


OUT_B, GAIN_1, SHIFT_1, DOWN_B, GAIN_2, SHIFT_2 = range(6)


def norm_one_body(sc, vecs, cx0, cx1, cx2, cx3, wo, hidden, low, unit_out, rate_out):
    acc = hidden[...].astype(F32) + vecs[OUT_B : OUT_B + 1, :]
    for rel, ref in enumerate((cx0, cx1, cx2, cx3)):
        at = pl.multiple_of((sc[CHIP] ^ rel) * COLS, COLS)
        acc += dot(unpack(ref[...]), wo[pl.ds(at, COLS), :], 1, 0)
    unit, rate = normalize(acc)
    first = unit * vecs[GAIN_1 : GAIN_1 + 1, :] + vecs[SHIFT_1 : SHIFT_1 + 1, :]
    low[...] = first.astype(BF16)
    unit_out[...] = unit
    rate_out[...] = jnp.broadcast_to(rate, rate_out.shape)


def mlp_body(chunk, sc, bias, x0, x1, wup, wdn, act, slope, own, send):
    slots = x0.shape[0]
    tokens = jnp.concatenate([x0[...], x1[...]], axis=0)
    acc = None
    for lo in range(0, wup.shape[1], chunk):
        pre = dot(tokens, wup[:, lo : lo + chunk], 1, 0) + bias[0:1, lo : lo + chunk]
        cdf = 0.5 * (1.0 + lax.erf(pre * 0.7071067811865476))
        pdf = jnp.exp(-0.5 * pre * pre) * 0.3989422804014327
        out = (pre * cdf).astype(BF16)
        act[:, lo : lo + chunk] = out
        slope[:, lo : lo + chunk] = cdf + pre * pdf
        part = dot(out, wdn[lo : lo + chunk, :], 1, 0)
        acc = part if acc is None else acc + part
    own[...] = acc[0:slots]
    send[...] = acc[slots:].astype(BF16)


def norm_two_body(sc, vecs, meta, own, received, unit_one, cotangent, output, gs, gs_low, sums):
    valid = meta[...].T[:, 8:9]
    first = unit_one[...] * vecs[GAIN_1 : GAIN_1 + 1, :] + vecs[SHIFT_1 : SHIFT_1 + 1, :]
    acc = own[...] + received[...].astype(F32) + vecs[DOWN_B : DOWN_B + 1, :] + first
    unit, rate = normalize(acc)
    gain = vecs[GAIN_2 : GAIN_2 + 1, :]
    output[...] = ((unit * gain + vecs[SHIFT_2 : SHIFT_2 + 1, :]) * valid).astype(BF16)
    grad = cotangent[...].astype(F32) * valid
    back = norm_back(grad, unit, rate, gain)
    gs[...] = back
    gs_low[...] = back.astype(BF16)
    sums[...] = jnp.zeros_like(sums)
    sums[DOWN_B : DOWN_B + 1, :] = total(back)
    sums[GAIN_2 : GAIN_2 + 1, :] = total(grad * unit)
    sums[SHIFT_2 : SHIFT_2 + 1, :] = total(grad)


def mlp_back_body(chunk, sc, g0, g1, slope, wup, wdn, pre_low, sums, own, send):
    slots = g0.shape[0]
    grads = jnp.concatenate([g0[...], g1[...]], axis=0)
    acc = None
    sums[...] = jnp.zeros_like(sums)
    for lo in range(0, wup.shape[1], chunk):
        pre = dot(grads, wdn[lo : lo + chunk, :], 1, 1) * slope[:, lo : lo + chunk]
        sums[0:1, lo : lo + chunk] = total(pre)
        low = pre.astype(BF16)
        pre_low[:, lo : lo + chunk] = low
        part = dot(low, wup[:, lo : lo + chunk], 1, 1)
        acc = part if acc is None else acc + part
    own[...] = acc[0:slots]
    send[...] = acc[slots:].astype(BF16)


def mlp_grads_body(shards, sc, x0, x1, g0, g1, act, pre_low, keep, send):
    tokens = jnp.concatenate([x0[...], x1[...]], axis=0)
    grads = jnp.concatenate([g0[...], g1[...]], axis=0)
    width = tokens.shape[1]
    rows = width // shards
    small = rows // 4
    part = act.shape[1] // shards

    def put(values, lo, at, col):
        size = values.shape[0] // 4
        for spot in range(4):
            block = values[spot * size : (spot + 1) * size, :]
            for core in range(CORES):

                @pl.when(sc[CORE] == core)
                def _():
                    if spot % 2 == core:
                        keep[spot // 2, at, lo : lo + size, :] = block
                    else:
                        send[spot // 2, at, lo : lo + size, :] = block.astype(BF16)

    for at in range(shards):
        for col in range(2):
            up = dot(
                tokens[:, at * rows : (at + 1) * rows],
                pre_low[:, col * width : (col + 1) * width],
                0,
                0,
            )
            put(up, col * small, at, col)
        down = dot(act[:, at * part : (at + 1) * part], grads, 0, 0)
        put(down, 2 * small, at, 0)


def norm_one_back_body(
    sc, vecs, own, received, gs, unit_one, rate_one, wo, gf, gf_low, gcx, sums
):
    grad = gs[...] + own[...] + received[...].astype(F32)
    unit = unit_one[...]
    rate = rate_one[:, 0:1]
    back = norm_back(grad, unit, rate, vecs[GAIN_1 : GAIN_1 + 1, :])
    gf[...] = back
    low = back.astype(BF16)
    gf_low[...] = low
    sums[...] = jnp.zeros_like(sums)
    sums[OUT_B : OUT_B + 1, :] = total(back)
    sums[GAIN_1 : GAIN_1 + 1, :] = total(grad * unit)
    sums[SHIFT_1 : SHIFT_1 + 1, :] = total(grad)
    half = back.shape[0] // 2
    for rel in range(4):
        at = pl.multiple_of((sc[CHIP] ^ rel) * COLS, COLS)
        part = dot(low, wo[pl.ds(at, COLS), :], 1, 1).astype(BF16)
        gcx[rel, :, 0:COLS] = part[0:half]
        gcx[rel, :, COLS:] = part[half:]


def out_grads_body(sc, cx0, cx1, cx2, cx3, gf_low, keep, send):
    low = gf_low[...]
    half = keep.shape[2]
    for rel, ref in enumerate((cx0, cx1, cx2, cx3)):
        block = dot(unpack(ref[...]), low, 0, 0)
        chip = sc[CHIP] ^ rel
        for core in range(CORES):

            @pl.when(sc[CORE] == core)
            def _():
                keep[chip] = block[:, core * half : (core + 1) * half]
                other = 1 - core
                send[chip] = block[:, other * half : (other + 1) * half].astype(BF16)


def qkv_grads_body(
    shards, sc, meta, dq, dk_own, dk_rec, dv_own, dv_rec, wall, x0, x1, x2, x3,
    own, send, keep_w, send_w, sums, packed,
):
    slots = x0.shape[0]
    flags = meta[...].T
    lane = lax.broadcasted_iota(jnp.int32, (1, WIDE), 1)
    left = (lane % PAIR) < HEAD
    rows = wall.shape[1] // shards
    half = rows // 2
    acc = [0.0] * 4
    for block in range(4):
        at = slice(block * slots, (block + 1) * slots)
        word = flags[:, block : block + 1] > 0
        query = dq[at, :] * SCALE
        parts = (
            jnp.where(word, query, 0.0),
            jnp.where(word, 0.0, query),
            jnp.where(left == word, dk_own[at, :] + dk_rec[at, :].astype(F32), 0.0),
            dv_own[at, :] + dv_rec[at, :].astype(F32),
        )
        acc = [a + total(p) for a, p in zip(acc, parts)]
        packed[0, at, 0:WIDE] = parts[0].astype(BF16)
        packed[1, at, 0:WIDE] = parts[1].astype(BF16)
        packed[0, at, WIDE:] = parts[2].astype(BF16)
        packed[1, at, WIDE:] = parts[3].astype(BF16)
        back = dot(packed[0, at, :], wall[0], 1, 1) + dot(packed[1, at, :], wall[1], 1, 1)
        if block == 0:
            own[...] = back
        else:
            send[block - 1] = back.astype(BF16)
    sums[...] = jnp.zeros_like(sums)
    sums[0:1, 0:WIDE] = acc[0]
    sums[1:2, 0:WIDE] = acc[1]
    sums[0:1, WIDE:] = acc[2]
    sums[1:2, WIDE:] = acc[3]
    tokens = jnp.concatenate([x0[...], x1[...], x2[...], x3[...]], axis=0)
    for group_rel, ref in enumerate((keep_w, send_w)):
        group = sc[CORE] ^ group_rel
        for at in range(shards):
            grad = dot(tokens[:, at * rows : (at + 1) * rows], packed[group], 0, 0)
            ref[at, 0:rows, :] = grad[:, 0:WIDE].astype(ref.dtype)
            folded = jnp.concatenate(
                [
                    grad[:, WIDE + h * PAIR : WIDE + h * PAIR + HEAD]
                    + grad[:, WIDE + h * PAIR + HEAD : WIDE + (h + 1) * PAIR]
                    for h in range(LOCAL_HEADS)
                ],
                axis=1,
            ).astype(ref.dtype)
            ref[at, rows:, 0:COLS] = folded[0:half]
            ref[at, rows:, COLS:] = folded[half:]


def place_qkv_body(sc, *refs):
    pieces, (qg, kg, vg, held) = refs[:8], refs[8:]
    rows = kg.shape[0]
    half = rows // 2
    for core_rel in range(CORES):
        for rel in range(4):
            held[sc[CORE] ^ core_rel, sc[CHIP] ^ rel] = pieces[core_rel * 4 + rel][...]
    for core in range(CORES):
        for chip in range(CHIPS):
            piece = held[core, chip].astype(F32)
            lo = chip * COLS
            for which in range(2):
                qg[2 * core + which, :, lo : lo + COLS] = jnp.concatenate(
                    [
                        piece[0:rows, h * PAIR + which * HEAD : h * PAIR + (which + 1) * HEAD]
                        for h in range(LOCAL_HEADS)
                    ],
                    axis=1,
                )
            ref = kg if core == 0 else vg
            ref[0:half, lo : lo + COLS] = piece[rows:, 0:COLS]
            ref[half:, lo : lo + COLS] = piece[rows:, COLS:]


def place_mlp_body(sc, *refs):
    mlp, outs, (ug, dg, og) = refs[:8], refs[8:16], refs[16:]
    rows, ff = ug.shape
    width = dg.shape[1]
    part = ff // 4
    side = part // 2
    small = rows // 4
    low = part // 8
    for core_rel in range(CORES):
        for rel in range(4):
            core = sc[CORE] ^ core_rel
            chip = sc[CHIP] ^ rel
            chip_x, chip_y = chip & 1, chip >> 1
            spot = chip_y * 2 + core
            piece = mlp[core_rel * 4 + rel][...].astype(F32)
            at = pl.multiple_of(spot * small, small)
            for shard in range(4):
                row = (shard // 2) * small
                col = (shard % 2) * side
                lane = pl.multiple_of(shard * part + chip_x * side, side)
                ug[pl.ds(at, small), pl.ds(lane, side)] = piece[
                    row : row + small, col : col + side
                ]
            at = pl.multiple_of(chip_x * side + spot * low, low)
            dg[pl.ds(at, low), :] = piece[2 * small :, :]
            at = pl.multiple_of(chip * small, small)
            lane = pl.multiple_of(core * (width // 2), width // 2)
            og[pl.ds(at, small), pl.ds(lane, width // 2)] = outs[core_rel * 4 + rel][...].astype(
                F32
            )


def local(
    shards,
    lanes,
    hidden,
    lengths,
    row_types,
    query_weight,
    query_bias,
    key_weight,
    key_bias,
    value_weight,
    value_bias,
    out_weight,
    out_bias,
    norm1_gain,
    norm1_bias,
    up_weight,
    up_bias,
    down_weight,
    down_bias,
    norm2_gain,
    norm2_bias,
    cotangent,
):
    groups = lanes // (CHIPS * CORES)
    shard = lax.axis_index("shard")
    lane = lax.axis_index("ctx")
    core, chip, group = lane & 1, (lane >> 1) & 3, lane >> 3
    chip_x, chip_y = chip & 1, chip >> 1
    spot = chip_y * 2 + core
    scalars = jnp.stack([shard, chip, core, spot, chip_x]).astype(jnp.int32)

    def across(value, mask):
        return lax.ppermute(value, "ctx", [(i, i ^ mask) for i in range(lanes)])

    def chips(value, rel):
        return across(value, rel << 1)

    def turn(value, shift):
        return lax.ppermute(value, "shard", [(i, (i + shift) % shards) for i in range(shards)])

    def pick(stack, index):
        return lax.dynamic_index_in_dim(stack, index, 0, keepdims=False)

    def over_groups(value):
        if groups == 1:
            return value
        sets = [[g * 8 + i for g in range(groups)] for i in range(8)]
        return lax.psum(value, "ctx", axis_index_groups=sets)

    width = hidden.shape[2]
    slots = hidden.shape[1]
    rows = width // shards
    ff = up_weight.shape[1]
    part = ff // shards
    side = part // 2
    hid = hidden[0]
    cot = cotangent[0]

    mine = run(
        prep_qkv_body,
        "prep_qkv",
        sds((rows + rows // 2, WIDE), BF16),
        scalars,
        query_weight,
        key_weight,
        value_weight,
    )
    own_w = [mine] + [turn(mine, d) for d in range(1, shards)]
    own_x = [hid] + [chips(hid, rel) for rel in range(1, 4)]
    small_one = jnp.concatenate(
        [
            query_bias.reshape(-1), key_bias, value_bias, out_bias, norm1_gain, norm1_bias,
            down_bias, norm2_gain, norm2_bias, up_bias,
        ]
    ).reshape(4, width)
    small_all = [small_one] + [turn(small_one, d) for d in range(1, shards)]
    other_w = [across(piece, 1) for piece in own_w]
    other_x = [across(block, 1) for block in own_x]

    out_one = lax.dynamic_slice_in_dim(out_weight, spot * (rows // 4), rows // 4, 0)
    out_own = jnp.stack([out_one] + [turn(out_one, d) for d in range(1, shards)])
    out_own = jnp.concatenate([out_own, across(out_own, 4)], axis=0)
    wo = run(
        partial(assemble_out_body, shards),
        "assemble_out",
        sds((width, width), BF16),
        scalars,
        out_own,
        across(out_own, 1),
    )
    up_rows = lax.dynamic_slice_in_dim(up_weight, spot * (rows // 4), rows // 4, 0)
    down_rows = lax.dynamic_slice_in_dim(
        down_weight, chip_x * side + spot * (side // 4), side // 4, 0
    )
    mlp_one = run(
        prep_mlp_body,
        "prep_mlp",
        sds((rows // 2 + side // 4, width), BF16),
        scalars,
        up_rows,
        down_rows,
    )
    mlp_pieces = []
    for d in range(shards):
        here = mlp_one if d == 0 else turn(mlp_one, d)
        there = across(here, 4)
        mlp_pieces += [here, across(here, 1), there, across(there, 1)]
    wup, wdn = run(
        partial(assemble_mlp_body, shards),
        "assemble_mlp",
        [sds((width, ff // 2), BF16), sds((ff // 2, width), BF16)],
        scalars,
        *mlp_pieces,
    )

    order = (shard - jnp.arange(shards)) % shards
    table = jnp.stack(small_all)[order].astype(F32)
    qb = pick(table, chip)
    pair_bias = qb[0].reshape(2, 2, LOCAL_HEADS, HEAD).transpose(0, 2, 1, 3).reshape(2, WIDE)
    kb = jnp.repeat(qb[1, 0:COLS].reshape(LOCAL_HEADS, 1, HEAD), 2, axis=1).reshape(WIDE)
    vb = jnp.pad(
        qb[1, COLS : 2 * COLS].reshape(LOCAL_HEADS, 1, HEAD), ((0, 0), (0, 1), (0, 0))
    ).reshape(WIDE)
    bias = jnp.concatenate([pair_bias, jnp.stack([kb, vb])], axis=1)
    flat = table[:, 1:3].reshape(shards, 8, rows).transpose(1, 0, 2).reshape(8, width)
    vecs = jnp.concatenate([flat[2:8], jnp.zeros((2, width), F32)], axis=0)
    up_shift = lax.dynamic_slice_in_dim(table[:, 3], chip_x * side, side, 1).reshape(1, ff // 2)

    kinds = row_types.reshape(-1, slots)
    blocks = jnp.stack(
        [group * 8 + (chip ^ rel) * 2 + (core ^ c) for c in range(CORES) for rel in range(4)]
    )
    places = jnp.arange(slots, dtype=jnp.int32)
    word = (kinds[blocks] == 0).astype(F32)
    live = (blocks[:, None] * slots + places[None, :] < lengths[0]).astype(F32)
    meta = jnp.concatenate([word, live], axis=0)

    wall, pq, pk, vv = run(
        partial(qkv_body, shards),
        "qkv",
        [
            sds((2, width, 2 * WIDE), BF16),
            sds((4 * slots, WIDE), BF16),
            sds((8 * slots, WIDE), BF16),
            sds((8 * slots, WIDE), BF16),
        ],
        scalars,
        bias,
        meta,
        *own_x,
        *other_x,
        *own_w,
        *other_w,
        flops=2 * slots * 12 * width * 2 * WIDE,
    )
    valid = live.reshape(1, 8 * slots)
    if groups > 1:
        sets = [[g * 8 + i for g in range(groups)] for i in range(8)]
        gather = partial(lax.all_gather, axis_name="ctx", axis_index_groups=sets, tiled=True)
        pk, vv = gather(pk, axis=0), gather(vv, axis=0)
        valid = gather(valid, axis=1)
    probs, cx = attend(pq, pk, vv, valid, slots)
    cxs = [cx[0]] + [chips(cx[rel], rel) for rel in range(1, 4)]

    low_one, unit_one, rate_one = run(
        norm_one_body,
        "norm_one",
        [sds((slots, width), BF16), sds((slots, width), F32), sds((slots, 128), F32)],
        scalars,
        vecs,
        *cxs,
        wo,
        hid,
    )
    low_two = chips(low_one, 1)
    act, slope, own, send = run(
        partial(mlp_body, 384),
        "mlp",
        [
            sds((2 * slots, ff // 2), BF16),
            sds((2 * slots, ff // 2), F32),
            sds((slots, width), F32),
            sds((slots, width), BF16),
        ],
        scalars,
        up_shift,
        low_one,
        low_two,
        wup,
        wdn,
        flops=4 * slots * width * ff,
    )
    output, gs, gs_low, sums_two = run(
        norm_two_body,
        "norm_two",
        [
            sds((slots, width), BF16),
            sds((slots, width), F32),
            sds((slots, width), BF16),
            sds((8, width), F32),
        ],
        scalars,
        vecs,
        meta,
        own,
        chips(send, 1),
        unit_one,
        cot,
    )
    gs_other = chips(gs_low, 1)
    pre_low, sums_up, own, send = run(
        partial(mlp_back_body, 384),
        "mlp_back",
        [
            sds((2 * slots, ff // 2), BF16),
            sds((8, ff // 2), F32),
            sds((slots, width), F32),
            sds((slots, width), BF16),
        ],
        scalars,
        gs_low,
        gs_other,
        slope,
        wup,
        wdn,
        flops=4 * slots * width * ff,
    )
    received = chips(send, 1)
    piece_rows = rows // 2 + side // 4
    keep_mlp, send_mlp = run(
        partial(mlp_grads_body, shards),
        "mlp_grads",
        [
            sds((2, shards, piece_rows, width), F32),
            sds((2, shards, piece_rows, width), BF16),
        ],
        scalars,
        low_one,
        low_two,
        gs_low,
        gs_other,
        act,
        pre_low,
        flops=4 * slots * width * ff,
    )
    gf, gf_low, gcx, sums_one = run(
        norm_one_back_body,
        "norm_one_back",
        [
            sds((slots, width), F32),
            sds((slots, width), BF16),
            sds((4, slots // 2, 2 * COLS), BF16),
            sds((8, width), F32),
        ],
        scalars,
        vecs,
        own,
        received,
        gs,
        unit_one,
        rate_one,
        wo,
    )
    gcs = [gcx[0]] + [chips(gcx[rel], rel) for rel in range(1, 4)]
    keep_out, send_out = run(
        out_grads_body,
        "out_grads",
        [sds((CHIPS, COLS, width // 2), F32), sds((CHIPS, COLS, width // 2), BF16)],
        scalars,
        *cxs,
        gf_low,
    )

    dq, dk, dv = attend_back(gcs, pq, pk, vv, probs, slots)
    if groups > 1:
        scatter = partial(
            lax.psum_scatter, axis_name="ctx", axis_index_groups=sets, tiled=True
        )
        dk, dv = scatter(dk), scatter(dv)
    count = 4 * slots
    dk_rec = across(dk[count:].astype(BF16), 1)
    dv_rec = across(dv[count:].astype(BF16), 1)
    own, send, keep_w, send_w, sums_qkv = run(
        partial(qkv_grads_body, shards),
        "qkv_grads",
        [
            sds((slots, width), F32),
            sds((3, slots, width), BF16),
            sds((shards, rows + rows // 2, WIDE), F32),
            sds((shards, rows + rows // 2, WIDE), BF16),
            sds((8, 2 * WIDE), F32),
        ],
        scalars,
        meta,
        dq,
        dk[:count],
        dk_rec,
        dv[:count],
        dv_rec,
        wall,
        *own_x,
        scratch=[pltpu.VMEM((2, count, 2 * WIDE), BF16)],
        flops=12 * slots * width * 4 * WIDE,
    )

    def owned(parts):
        result = pick(parts, shard)
        for d in range(1, shards):
            result = result + turn(pick(parts, (shard + d) % shards).astype(BF16), d).astype(F32)
        return over_groups(result)

    def spread(value):
        low = value.astype(BF16)
        here = [low] + [chips(low, rel) for rel in range(1, 4)]
        return here + [across(block, 1) for block in here]

    done_qkv = spread(owned(keep_w + across(send_w, 1).astype(F32)))
    input_grad = gf + own
    for rel in range(1, 4):
        input_grad = input_grad + chips(send[rel - 1], rel).astype(F32)

    both = keep_mlp + across(send_mlp, 1).astype(F32)
    kept, moved = pick(both, chip_y), pick(both, 1 - chip_y).astype(BF16)
    done_mlp = spread(owned(kept + across(moved, 4).astype(F32)))

    both = (keep_out + across(send_out, 1).astype(F32)).reshape(
        CHIPS, 4, COLS // 4, width // 2
    )
    kept = lax.dynamic_index_in_dim(both, chip, 1, keepdims=False)
    for rel in range(1, 4):
        moved = lax.dynamic_index_in_dim(both, chip ^ rel, 1, keepdims=False).astype(BF16)
        kept = kept + chips(moved, rel).astype(F32)
    done_out = spread(owned(kept))

    sums = sums_one + sums_two
    mine_qb = sums_qkv[0:2, 0:WIDE].reshape(2, LOCAL_HEADS, 2, HEAD).transpose(0, 2, 1, 3)
    mine_kb = sums_qkv[0, WIDE:].reshape(LOCAL_HEADS, 2, HEAD).sum(1)
    mine_vb = sums_qkv[1, WIDE:].reshape(LOCAL_HEADS, 2, HEAD)[:, 0]
    mine_row = jnp.concatenate([mine_qb.reshape(-1), mine_kb.reshape(-1), mine_vb.reshape(-1)])
    heads_part = jnp.where(
        (jnp.arange(shards) == chip)[:, None], mine_row[None, :], 0.0
    )
    norms_part = sums[0:6].reshape(6, shards, rows).transpose(1, 0, 2).reshape(shards, 6 * rows)
    up_part = sums_up[0].reshape(shards, side)
    blank = jnp.zeros_like(up_part)
    up_part = jnp.where(
        chip_x == 0,
        jnp.concatenate([up_part, blank], axis=1),
        jnp.concatenate([blank, up_part], axis=1),
    )
    small = jnp.concatenate([heads_part, norms_part, up_part], axis=1)
    for mask in (1, 2, 4):
        small = small + across(small, mask)
    small = over_groups(small)
    step = 1
    while step < shards:
        small = small + lax.ppermute(small, "shard", [(i, i ^ step) for i in range(shards)])
        step *= 2
    small = pick(small, shard)

    qg, kg, vg = run(
        place_qkv_body,
        "place_qkv",
        [sds((4, rows, width), F32), sds((rows, width), F32), sds((rows, width), F32)],
        scalars,
        *done_qkv,
        scratch=[pltpu.VMEM((CORES, CHIPS, rows + rows // 2, WIDE), BF16)],
    )
    ug, dg, og = run(
        place_mlp_body,
        "place_mlp",
        [sds((rows, ff), F32), sds((part, width), F32), sds((rows, width), F32)],
        scalars,
        *done_mlp,
        *done_out,
    )
    pieces = [small[0 : 4 * rows].reshape(4, rows)]
    pieces += [small[i * rows : (i + 1) * rows] for i in range(4, 12)]
    qbg, kbg, vbg, obg, g1g, b1g, dbg, g2g, b2g = pieces
    ubg = small[12 * rows :]
    return (
        output[None], input_grad[None], qg, qbg, kg, kbg, vg, vbg, og, obg,
        g1g, b1g, ug, ubg, dg, dbg, g2g, b2g,
    )


def solution(mesh):
    vec, mat = P("shard"), P("shard", None)
    tokens = P("shard", "ctx", None)
    placed = (
        tokens, vec, mat, P(None, "shard", None), P(None, "shard"), mat, vec, mat, vec, mat,
        vec, vec, vec, mat, vec, mat, vec, vec, vec, tokens,
    )
    result = (
        tokens, tokens, P(None, "shard", None), P(None, "shard"), mat, vec, mat, vec, mat, vec,
        vec, vec, mat, vec, mat, vec, vec, vec,
    )
    return jax.shard_map(
        partial(local, mesh.shape["shard"], mesh.shape["ctx"]),
        mesh=mesh,
        in_specs=placed,
        out_specs=result,
        check_vma=False,
    )
```

time: 1250 us -> 335 us (0.27)
  waiting for transfers between devices: 863 us -> 124 us
  blocking collectives: 204 us -> 0 us
  starting transfers between devices: 0.72 us -> 89.6 us
  matrix products: 72.7 us -> 0 us
  Pallas kernels: 0 us -> 65.1 us
  other arithmetic: 24.8 us -> 5.88 us
  between operations: 18.3 us -> 2.15 us
    all_gather x8 -> x0, waiting for transfers between devices: 316 us -> none  [the longest x1 86.8 us: local(): lax.all_gather(up_weight, 'shard', axis=0, tiled=True)]
    reduce_scatter x5 -> x0, waiting for transfers between devices: 294 us -> none  [the longest x1 88 us: local(): lax.psum_scatter(grad_down.astype(jnp.bfloat16), 'shard', scatter_dimensi...]
    unnamed x22 -> x0, waiting for transfers between devices: 215 us -> none
    psum x1 -> x0, blocking collectives: 141 us -> none  [local(): lax.psum((grad_query, grad_query_shift, grad_key, grad_key_shift, grad_va...]
    ppermute x0 -> x94, waiting for transfers between devices: none -> 124 us  [the longest x71 78.6 us: across(): return lax.ppermute(value, 'ctx', [(i, i ^ mask) for i in range(lanes)])]
    ppermute x0 -> x94, starting transfers between devices: none -> 89.6 us  [the longest x21 43.2 us: turn(): lax.ppermute(value, 'shard', [(i, (i + shift) % shards) for i in range(sh...]
    dot_general x24 -> x0, matrix products: 72.7 us -> none  [the longest x1 8.72 us: local(): jnp.einsum('bsd,df->bsf', first_low, up_mat, preferred_element_type=jnp.f...]
    pallas_call x0 -> x17, Pallas kernels: none -> 65.1 us  [the longest x15 49.9 us: run(): pl.pallas_call(body, out_shape=outs, in_specs=[SMEM] + [VMEM] * len(array...]
  transfers between devices with their start and end apart: 18 -> 94, of which waited for: 17 -> 31; matrix products, arithmetic and copies ran while one was open for 8% -> 5% of each run, Pallas kernels for 0% -> 13%
where the time goes in v1:
time: 335 us; the launch traced here: 334 us
  waiting for transfers between devices  124 us (37%)
  starting transfers between devices  89.6 us (27%)
  Pallas kernels  65.1 us (19%)
  local copies, waits for them, and re-layouts  47.3 us (14%)
  other arithmetic  5.88 us (2%)
    ppermute x71, waiting for transfers between devices, across(): return lax.ppermute(value, 'ctx', [(i, i ^ mask) for i in range(lanes)])  78.6 us
    pallas_call x15, Pallas kernels, run(): pl.pallas_call(body, out_shape=outs, in_specs=[SMEM] + [VMEM] * len(array...  49.9 us
    ppermute x21, waiting for transfers between devices, turn(): lax.ppermute(value, 'shard', [(i, (i + shift) % shards) for i in range(sh...  45.5 us
    ppermute x21, starting transfers between devices, turn(): lax.ppermute(value, 'shard', [(i, (i + shift) % shards) for i in range(sh...  43.2 us
    ppermute x71, starting transfers between devices, across(): return lax.ppermute(value, 'ctx', [(i, i ^ mask) for i in range(lanes)])  42.2 us
    unnamed x136, local copies, waits for them, and re-layouts  27.7 us
    pallas_call x1, Pallas kernels, attend_back(): pl.pallas_call(partial(attend_back_body, step), grid=(LOCAL_HEADS,), in_s...  7.87 us
    pallas_call x1, Pallas kernels, attend(): pl.pallas_call(partial(attend_body, step), grid=(LOCAL_HEADS,), in_specs=...  7.4 us
  transfers between devices with their start and end apart: 94, of which 31 were waited for; matrix products, arithmetic and copies ran while one was open for 5% of the time, Pallas kernels for 13%

profile of v1, /device:TPU:0, one launch (start us, length us, event | category | flops | bytes accessed | tf_op | source)
XLA Modules:
  0.0 334.2 jit_solution(570867237562065106)
XLA Ops:
  1.6 6.1 %concatenate.53 = bf16[3072]{0:T(1024)(128)(2,1)S(1)} concatenate(bf16[768]{0:T(1024)(128)(2,1)S(1)} %reshape.573, bf16[192]{0:T(256)(128)(2,1)} %param.26, bf16[192]{0:T(256)(128)(2,1)} %param.28, bf16[192]{0:T(256)(128)(2,1)} %param.30, bf16[192]{0:T(256)(128)(2,1)} %param.31, bf16[192]{0:T(256)(128)(2,1)} %param.32, bf16[192]{0:T(256)(128)(2,1)} %param.36, ...), dimensions={0} | concatenate | bytes 12288 | tf_op jit(solution)/shard_map/concatenate | solution.py:627
  7.7 5.1 %collective-permute-start.2 = (bf16[4,768]{1,0:T(4,128)(2,1)S(1)}, bf16[4,768]{1,0:T(4,128)(2,1)S(1)}, u32[]{:S(2)}, u32[]{:S(2)}) collective-permute-start(bf16[4,768]{1,0:T(4,128)(2,1)S(1)} %reshape.574), channel_id=1, source_target_pairs={{0,24},{8,0},{16,8},{24,16},{1,25},{9,1},{17,9},{25,17},{2,26},{10... | collective-permute-start | bytes 18440 | tf_op jit(solution)/shard_map/ppermute | solution.py:596
  38.4 4.6 %collective-permute-done.10.refs_9_ = bf16[288,384]{1,0:T(8,128)(2,1)S(1)} collective-permute-done((bf16[288,384]{1,0:T(8,128)(2,1)S(1)}, bf16[288,384]{1,0:T(8,128)(2,1)S(1)}, u32[]{:S(2)}, u32[]{:S(2)}) %collective-permute-start.10) | collective-permute-done | bytes 221216 | tf_op jit(solution)/shard_map/ppermute | solution.py:596
  43.5 9.0 %collective-permute-done.11.refs_10_ = bf16[288,384]{1,0:T(8,128)(2,1)S(1)} collective-permute-done((bf16[288,384]{1,0:T(8,128)(2,1)S(1)}, bf16[288,384]{1,0:T(8,128)(2,1)S(1)}, u32[]{:S(2)}, u32[]{:S(2)}) %collective-permute-start.11) | collective-permute-done | bytes 221216 | tf_op jit(solution)/shard_map/ppermute | solution.py:596
  54.5 3.9 %collective-permute-done.29.refs_4_ = bf16[192,768]{1,0:T(8,128)(2,1)S(1)} collective-permute-done((bf16[192,768]{1,0:T(8,128)(2,1)S(1)}, bf16[192,768]{1,0:T(8,128)(2,1)S(1)}, u32[]{:S(2)}, u32[]{:S(2)}) %collective-permute-start.29) | collective-permute-done | bytes 294944 | tf_op jit(solution)/shard_map/ppermute | solution.py:596
  59.5 4.6 %collective-permute-start.33 = (bf16[192,768]{1,0:T(8,128)(2,1)S(1)}, bf16[192,768]{1,0:T(8,128)(2,1)}, u32[]{:S(2)}, u32[]{:S(2)}) collective-permute-start(bf16[192,768]{1,0:T(8,128)(2,1)S(1)} %prep_mlp.1.refs_0_), channel_id=1, source_target_pairs={{0,16},{8,24},{16,0},{24,8},{1,17},{9,25},{17,1},{25,9},{2,18},{10... | collective-permute-start | bytes 884744 | tf_op jit(solution)/shard_map/ppermute | solution.py:596
  68.0 4.5 %qkv.1 = (bf16[2,768,768]{2,1,0:T(8,128)(2,1)}, bf16[512,384]{1,0:T(8,128)(2,1)S(1)}, bf16[1024,384]{1,0:T(8,128)(2,1)S(1)}, bf16[1024,384]{1,0:T(8,128)(2,1)S(1)}) custom-call(s32[5]{0:T(128)S(1)} %stack.98.sc, f32[2,768]{1,0:T(2,128)S(1)} %maximum_maximum_fusion.bias, f32[16,128]{1,0:T(8,128)S(1)} %add_convert_fusion.meta, bf16[128,768]{1,0:T(8,128)(2,1)S(1)} %bitcast.164, ...), custom_call_target="tpu_custom_call" | custom-call | flops 1811939328 | bytes 3356672 | tf_op jit(solution)/shard_map/qkv/pallas_call | solution.py:42
  73.4 7.4 %attend.1 = (bf16[3,512,1024]{2,1,0:T(8,128)(2,1)}, bf16[4,64,384]{2,1,0:T(8,128)(2,1)S(1)}) custom-call(bf16[512,384]{1,0:T(8,128)(2,1)S(1)} %get-tuple-element.63.pq, bf16[1024,384]{1,0:T(8,128)(2,1)S(1)} %get-tuple-element.64.pk, bf16[1024,384]{1,0:T(8,128)(2,1)} %copy-done.60, f32[1,1024]{1,0:T(1,128)S(1)} %bitcast.168), custom_call_target="tpu_custom_call" | custom-call | flops 805306368 | bytes 3145728 | tf_op jit(solution)/shard_map/attend/pallas_call | solution.py:200
  96.7 6.3 %collective-permute-done.35.refs_10_ = bf16[192,768]{1,0:T(8,128)(2,1)} collective-permute-done((bf16[192,768]{1,0:T(8,128)(2,1)}, bf16[192,768]{1,0:T(8,128)(2,1)}, u32[]{:S(2)}, u32[]{:S(2)}) %collective-permute-start.35) | collective-permute-done | bytes 294944 | tf_op jit(solution)/shard_map/ppermute | solution.py:590
  103.0 5.1 %collective-permute-done.39.refs_14_ = bf16[192,768]{1,0:T(8,128)(2,1)} collective-permute-done((bf16[192,768]{1,0:T(8,128)(2,1)}, bf16[192,768]{1,0:T(8,128)(2,1)}, u32[]{:S(2)}, u32[]{:S(2)}) %collective-permute-start.39) | collective-permute-done | bytes 294944 | tf_op jit(solution)/shard_map/ppermute | solution.py:590
  114.6 4.3 %assemble_mlp.1 = (bf16[768,1536]{1,0:T(8,128)(2,1)}, bf16[1536,768]{1,0:T(8,128)(2,1)}) custom-call(s32[5]{0:T(128)S(1)} %stack.98.sc, bf16[192,768]{1,0:T(8,128)(2,1)S(1)} %prep_mlp.1.refs_0_, bf16[192,768]{1,0:T(8,128)(2,1)S(1)} %collective-permute-done.26.refs_1_, bf16[192,768]{1,0:T(8,128)(2,1)S(1)} %collective-permute-done.27.refs_2_, ...), custom_call_target="tpu_custom_call" | custom-call | bytes 4718592 | tf_op jit(solution)/shard_map/assemble_mlp/pallas_call | solution.py:42
  122.9 4.1 %mlp.1 = (bf16[256,1536]{1,0:T(8,128)(2,1)S(1)}, f32[256,1536]{1,0:T(8,128)S(1)}, f32[128,768]{1,0:T(8,128)S(1)}, bf16[128,768]{1,0:T(8,128)(2,1)S(1)}) custom-call(s32[5]{0:T(128)S(1)} %stack.98.sc, f32[1,1536]{1,0:T(1,128)S(1)} %bitcast.167, bf16[128,768]{1,0:T(8,128)(2,1)} %get-tuple-element.67.x0, bf16[128,768]{1,0:T(8,128)(2,1)} %collective-permute-done.25.x1, ...), custom_call_target="tpu_custom_call" | custom-call | flops 1207959552 | bytes 5117952 | tf_op jit(solution)/shard_map/mlp/pallas_call | solution.py:42
  128.4 5.5 %collective-permute-done.41.received = bf16[128,768]{1,0:T(8,128)(2,1)S(1)} collective-permute-done((bf16[128,768]{1,0:T(8,128)(2,1)S(1)}, bf16[128,768]{1,0:T(8,128)(2,1)S(1)}, u32[]{:S(2)}, u32[]{:S(2)}) %collective-permute-start.41) | collective-permute-done | bytes 196640 | tf_op jit(solution)/shard_map/ppermute | solution.py:590
  136.0 5.1 %collective-permute-done.42.g1 = bf16[128,768]{1,0:T(8,128)(2,1)S(1)} collective-permute-done((bf16[128,768]{1,0:T(8,128)(2,1)S(1)}, bf16[128,768]{1,0:T(8,128)(2,1)S(1)}, u32[]{:S(2)}, u32[]{:S(2)}) %collective-permute-start.42) | collective-permute-done | bytes 196640 | tf_op jit(solution)/shard_map/ppermute | solution.py:590
  141.2 4.5 %mlp_back.1 = (bf16[256,1536]{1,0:T(8,128)(2,1)S(1)}, f32[8,1536]{1,0:T(8,128)S(1)}, f32[128,768]{1,0:T(8,128)S(1)}, bf16[128,768]{1,0:T(8,128)(2,1)}) custom-call(s32[5]{0:T(128)S(1)} %stack.98.sc, bf16[128,768]{1,0:T(8,128)(2,1)S(1)} %get-tuple-element.74.g0, bf16[128,768]{1,0:T(8,128)(2,1)S(1)} %collective-permute-done.42.g1, ...), custom_call_target="tpu_custom_call" | custom-call | flops 1207959552 | bytes 6684672 | tf_op jit(solution)/shard_map/mlp_back/pallas_call | solution.py:42
  147.1 5.3 %collective-permute-done.43.received = bf16[128,768]{1,0:T(8,128)(2,1)S(1)} collective-permute-done((bf16[128,768]{1,0:T(8,128)(2,1)}, bf16[128,768]{1,0:T(8,128)(2,1)S(1)}, u32[]{:S(2)}, u32[]{:S(2)}) %collective-permute-start.43) | collective-permute-done | bytes 196640 | tf_op jit(solution)/shard_map/ppermute | solution.py:590
  161.9 7.9 %attend_back.1 = (f32[512,384]{1,0:T(8,128)}, f32[1024,384]{1,0:T(8,128)}, f32[1024,384]{1,0:T(8,128)}) custom-call(bf16[64,384]{1,0:T(8,128)(2,1)} %get-tuple-element.134.gc0, bf16[64,384]{1,0:T(8,128)(2,1)} %copy-done.63, bf16[64,384]{1,0:T(8,128)(2,1)} %copy-done.64, bf16[64,384]{1,0:T(8,128)(2,1)} %copy-done.65, bf16[512,384]{1,0:T(8,128)(2,1)} %copy-done.61, ...), custom_call_target="tpu_custom_call" | custom-call | flops 1610612736 | bytes 3145728 | tf_op jit(solution)/shard_map/attend_back/pallas_call | solution.py:271
  172.7 8.2 %mlp_grads.1 = (f32[2,4,192,768]{3,2,1,0:T(8,128)}, bf16[2,4,192,768]{3,2,1,0:T(8,128)(2,1)S(1)}) custom-call(s32[5]{0:T(128)S(1)} %stack.98.sc, bf16[128,768]{1,0:T(8,128)(2,1)} %get-tuple-element.67.x0, bf16[128,768]{1,0:T(8,128)(2,1)} %collective-permute-done.25.x1, bf16[128,768]{1,0:T(8,128)(2,1)S(1)} %copy-done.37, bf16[128,768]{1,0:T(8,128)(2,1)S(1)} %copy-done.39, ...), custom_call_target="tpu_custom_call" | custom-call | flops 1207959552 | bytes 2359296 | tf_op jit(solution)/shard_map/mlp_grads/pallas_call | solution.py:42
  186.3 7.5 %qkv_grads.1 = (f32[128,768]{1,0:T(8,128)S(1)}, bf16[3,128,768]{2,1,0:T(8,128)(2,1)S(1)}, f32[4,288,384]{2,1,0:T(8,128)}, bf16[4,288,384]{2,1,0:T(8,128)(2,1)S(1)}, f32[8,768]{1,0:T(8,128)S(1)}) custom-call(s32[5]{0:T(128)S(1)} %stack.98.sc, f32[16,128]{1,0:T(8,128)S(1)} %add_convert_fusion.meta, f32[512,384]{1,0:T(8,128)S(1)} %copy-done.58, ...), custom_call_target="tpu_custom_call" | custom-call | flops 1811939328 | bytes 6299648 | tf_op jit(solution)/shard_map/qkv_grads/pallas_call | solution.py:42
  231.3 18.7 %collective-permute-done.69 = bf16[4,192,768]{2,1,0:T(8,128)(2,1)S(1)} collective-permute-done((bf16[4,192,768]{2,1,0:T(8,128)(2,1)S(1)}, bf16[4,192,768]{2,1,0:T(8,128)(2,1)S(1)}, u32[]{:S(2)}, u32[]{:S(2)}) %collective-permute-start.69) | collective-permute-done | bytes 1179680 | tf_op jit(solution)/shard_map/ppermute | solution.py:590
  262.1 6.0 %collective-permute-start.70 = (bf16[192,768]{1,0:T(8,128)(2,1)S(1)}, bf16[192,768]{1,0:T(8,128)(2,1)S(1)}, u32[]{:S(2)}, u32[]{:S(2)}) collective-permute-start(bf16[192,768]{1,0:T(8,128)(2,1)S(1)} %get-tuple-element.116), channel_id=1, source_target_pairs={{0,8},{8,16},{16,24},{24,0},{1,9},{9,17},{17,25},{25,1},{2,10},{10... | collective-permute-start | bytes 884744 | tf_op jit(solution)/shard_map/ppermute | solution.py:596
  269.0 17.5 %collective-permute-done.54 = bf16[288,384]{1,0:T(8,128)(2,1)S(1)} collective-permute-done((bf16[288,384]{1,0:T(8,128)(2,1)S(1)}, bf16[288,384]{1,0:T(8,128)(2,1)S(1)}, u32[]{:S(2)}, u32[]{:S(2)}) %collective-permute-start.54) | collective-permute-done | bytes 221216 | tf_op jit(solution)/shard_map/ppermute | solution.py:596
  289.9 6.8 %collective-permute-done.71 = bf16[192,768]{1,0:T(8,128)(2,1)S(1)} collective-permute-done((bf16[192,768]{1,0:T(8,128)(2,1)S(1)}, bf16[192,768]{1,0:T(8,128)(2,1)S(1)}, u32[]{:S(2)}, u32[]{:S(2)}) %collective-permute-start.71) | collective-permute-done | bytes 294944 | tf_op jit(solution)/shard_map/ppermute | solution.py:596
  310.8 6.3 %collective-permute-done.74.refs_2_ = bf16[192,768]{1,0:T(8,128)(2,1)S(1)} collective-permute-done((bf16[192,768]{1,0:T(8,128)(2,1)S(1)}, bf16[192,768]{1,0:T(8,128)(2,1)S(1)}, u32[]{:S(2)}, u32[]{:S(2)}) %collective-permute-start.74) | collective-permute-done | bytes 294944 | tf_op jit(solution)/shard_map/ppermute | solution.py:590
  (412 shorter events, 167.8 us)
Async XLA Ops:
  13.9 20.3 %collective-permute-start.3 = (bf16[128,768]{1,0:T(8,128)(2,1)}, bf16[128,768]{1,0:T(8,128)(2,1)}, u32[]{:S(2)}, u32[]{:S(2)}) collective-permute-start(bf16[128,768]{1,0:T(8,128)(2,1)} %bitcast.160), channel_id=1, source_target_pairs={{0,2},{1,3},{2,0},{3,1},{4,6},{5,7},{6,4},{7,5},{8,10},{9,11},{10,... | collective-permute-start | bytes 589832 | tf_op jit(solution)/shard_map/ppermute | solution.py:590
  15.4 20.5 %collective-permute-start.4 = (bf16[128,768]{1,0:T(8,128)(2,1)}, bf16[128,768]{1,0:T(8,128)(2,1)}, u32[]{:S(2)}, u32[]{:S(2)}) collective-permute-start(bf16[128,768]{1,0:T(8,128)(2,1)} %bitcast.161), channel_id=1, source_target_pairs={{0,4},{1,5},{2,6},{3,7},{4,0},{5,1},{6,2},{7,3},{8,12},{9,13},{10,... | collective-permute-start | bytes 589832 | tf_op jit(solution)/shard_map/ppermute | solution.py:590
  34.2 18.3 %collective-permute-start.11 = (bf16[288,384]{1,0:T(8,128)(2,1)S(1)}, bf16[288,384]{1,0:T(8,128)(2,1)S(1)}, u32[]{:S(2)}, u32[]{:S(2)}) collective-permute-start(bf16[288,384]{1,0:T(8,128)(2,1)S(1)} %prep_qkv.1.refs_8_), channel_id=1, source_target_pairs={{0,16},{8,24},{16,0},{24,8},{1,17},{9,25},{17,1},{25,9},{2,18},{10... | collective-permute-start | bytes 663560 | tf_op jit(solution)/shard_map/ppermute | solution.py:596
  38.2 20.2 %collective-permute-start.29 = (bf16[192,768]{1,0:T(8,128)(2,1)S(1)}, bf16[192,768]{1,0:T(8,128)(2,1)S(1)}, u32[]{:S(2)}, u32[]{:S(2)}) collective-permute-start(bf16[192,768]{1,0:T(8,128)(2,1)S(1)} %prep_mlp.1.refs_0_), channel_id=1, source_target_pairs={{0,8},{8,16},{16,24},{24,0},{1,9},{9,17},{17,25},{25,1},{2,10},{10... | collective-permute-start | bytes 884744 | tf_op jit(solution)/shard_map/ppermute | solution.py:596
  59.0 21.9 %collective-permute-start.26 = (bf16[192,768]{1,0:T(8,128)(2,1)S(1)}, bf16[192,768]{1,0:T(8,128)(2,1)S(1)}, u32[]{:S(2)}, u32[]{:S(2)}) collective-permute-start(bf16[192,768]{1,0:T(8,128)(2,1)S(1)} %prep_mlp.1.refs_0_), channel_id=1, source_target_pairs={{0,1},{1,0},{2,3},{3,2},{4,5},{5,4},{6,7},{7,6},{8,9},{9,8},{10,11... | collective-permute-start | bytes 884744 | tf_op jit(solution)/shard_map/ppermute | solution.py:590
  59.5 21.5 %collective-permute-start.33 = (bf16[192,768]{1,0:T(8,128)(2,1)S(1)}, bf16[192,768]{1,0:T(8,128)(2,1)}, u32[]{:S(2)}, u32[]{:S(2)}) collective-permute-start(bf16[192,768]{1,0:T(8,128)(2,1)S(1)} %prep_mlp.1.refs_0_), channel_id=1, source_target_pairs={{0,16},{8,24},{16,0},{24,8},{1,17},{9,25},{17,1},{25,9},{2,18},{10... | collective-permute-start | bytes 884744 | tf_op jit(solution)/shard_map/ppermute | solution.py:596
  67.5 23.9 %collective-permute-start.28 = (bf16[192,768]{1,0:T(8,128)(2,1)S(1)}, bf16[192,768]{1,0:T(8,128)(2,1)S(1)}, u32[]{:S(2)}, u32[]{:S(2)}) collective-permute-start(bf16[192,768]{1,0:T(8,128)(2,1)S(1)} %collective-permute-done.27.refs_2_), channel_id=1, source_target_pairs={{0,1},{1,0},{2,3},{3,2},{4,5},{5,4},{6,7},{7,6},{8,9},{9,8},{10,11... | collective-permute-start | bytes 884744 | tf_op jit(solution)/shard_map/ppermute | solution.py:590
  67.5 26.1 %collective-permute-start.30 = (bf16[192,768]{1,0:T(8,128)(2,1)S(1)}, bf16[192,768]{1,0:T(8,128)(2,1)S(1)}, u32[]{:S(2)}, u32[]{:S(2)}) collective-permute-start(bf16[192,768]{1,0:T(8,128)(2,1)S(1)} %collective-permute-done.29.refs_4_), channel_id=1, source_target_pairs={{0,1},{1,0},{2,3},{3,2},{4,5},{5,4},{6,7},{7,6},{8,9},{9,8},{10,11... | collective-permute-start | bytes 884744 | tf_op jit(solution)/shard_map/ppermute | solution.py:590
  80.8 27.2 %collective-permute-start.24 = (bf16[8,48,768]{2,1,0:T(8,128)(2,1)S(1)}, bf16[8,48,768]{2,1,0:T(8,128)(2,1)S(1)}, u32[]{:S(2)}, u32[]{:S(2)}) collective-permute-start(bf16[8,48,768]{2,1,0:T(8,128)(2,1)S(1)} %constant_dynamic-update-slice_fusion.own), channel_id=1, source_target_pairs={{0,1},{1,0},{2,3},{3,2},{4,5},{5,4},{6,7},{7,6},{8,9},{9,8},{10,11... | collective-permute-start | bytes 1769480 | tf_op jit(solution)/shard_map/ppermute | solution.py:590
  94.3 19.7 %collective-permute-start.34 = (bf16[192,768]{1,0:T(8,128)(2,1)}, bf16[192,768]{1,0:T(8,128)(2,1)}, u32[]{:S(2)}, u32[]{:S(2)}) collective-permute-start(bf16[192,768]{1,0:T(8,128)(2,1)} %collective-permute-done.33.refs_8_), channel_id=1, source_target_pairs={{0,1},{1,0},{2,3},{3,2},{4,5},{5,4},{6,7},{7,6},{8,9},{9,8},{10,11... | collective-permute-start | bytes 884744 | tf_op jit(solution)/shard_map/ppermute | solution.py:590
  182.4 30.4 %collective-permute-start.68 = (bf16[2,4,192,768]{3,2,1,0:T(8,128)(2,1)}, bf16[2,4,192,768]{3,2,1,0:T(8,128)(2,1)}, u32[]{:S(2)}, u32[]{:S(2)}) collective-permute-start(bf16[2,4,192,768]{3,2,1,0:T(8,128)(2,1)} %copy-done.50), channel_id=1, source_target_pairs={{0,1},{1,0},{2,3},{3,2},{4,5},{5,4},{6,7},{7,6},{8,9},{9,8},{10,11... | collective-permute-start | bytes 7077896 | tf_op jit(solution)/shard_map/ppermute | solution.py:590
  203.9 26.0 %collective-permute-start.52 = (bf16[4,288,384]{2,1,0:T(8,128)(2,1)}, bf16[4,288,384]{2,1,0:T(8,128)(2,1)S(1)}, u32[]{:S(2)}, u32[]{:S(2)}) collective-permute-start(bf16[4,288,384]{2,1,0:T(8,128)(2,1)} %copy-done.51), channel_id=1, source_target_pairs={{0,1},{1,0},{2,3},{3,2},{4,5},{5,4},{6,7},{7,6},{8,9},{9,8},{10,11... | collective-permute-start | bytes 2654216 | tf_op jit(solution)/shard_map/ppermute | solution.py:590
  218.0 32.0 %collective-permute-start.69 = (bf16[4,192,768]{2,1,0:T(8,128)(2,1)S(1)}, bf16[4,192,768]{2,1,0:T(8,128)(2,1)S(1)}, u32[]{:S(2)}, u32[]{:S(2)}) collective-permute-start(bf16[4,192,768]{2,1,0:T(8,128)(2,1)S(1)} %fusion), channel_id=1, source_target_pairs={{0,4},{1,5},{2,6},{3,7},{4,0},{5,1},{6,2},{7,3},{8,12},{9,13},{10,... | collective-permute-start | bytes 3538952 | tf_op jit(solution)/shard_map/ppermute | solution.py:590
  224.8 28.6 %collective-permute-start.51 = (bf16[128,768]{1,0:T(8,128)(2,1)S(1)}, bf16[128,768]{1,0:T(8,128)(2,1)S(1)}, u32[]{:S(2)}, u32[]{:S(2)}) collective-permute-start(bf16[128,768]{1,0:T(8,128)(2,1)S(1)} %get-tuple-element.126), channel_id=1, source_target_pairs={{0,6},{1,7},{2,4},{3,5},{4,2},{5,3},{6,0},{7,1},{8,14},{9,15},{10,... | collective-permute-start | bytes 589832 | tf_op jit(solution)/shard_map/ppermute | solution.py:590
  227.3 26.8 %collective-permute-start.50 = (bf16[128,768]{1,0:T(8,128)(2,1)S(1)}, bf16[128,768]{1,0:T(8,128)(2,1)S(1)}, u32[]{:S(2)}, u32[]{:S(2)}) collective-permute-start(bf16[128,768]{1,0:T(8,128)(2,1)S(1)} %get-tuple-element.127), channel_id=1, source_target_pairs={{0,4},{1,5},{2,6},{3,7},{4,0},{5,1},{6,2},{7,3},{8,12},{9,13},{10,... | collective-permute-start | bytes 589832 | tf_op jit(solution)/shard_map/ppermute | solution.py:590
  228.9 26.7 %collective-permute-start.49 = (bf16[128,768]{1,0:T(8,128)(2,1)S(1)}, bf16[128,768]{1,0:T(8,128)(2,1)S(1)}, u32[]{:S(2)}, u32[]{:S(2)}) collective-permute-start(bf16[128,768]{1,0:T(8,128)(2,1)S(1)} %get-tuple-element.125), channel_id=1, source_target_pairs={{0,2},{1,3},{2,0},{3,1},{4,6},{5,7},{6,4},{7,5},{8,10},{9,11},{10,... | collective-permute-start | bytes 589832 | tf_op jit(solution)/shard_map/ppermute | solution.py:590
  229.9 27.2 %collective-permute-start.67 = (f32[4,3072]{1,0:T(4,128)S(1)}, f32[4,3072]{1,0:T(4,128)S(1)}, u32[]{:S(2)}, u32[]{:S(2)}) collective-permute-start(f32[4,3072]{1,0:T(4,128)S(1)} %add.321), channel_id=1, source_target_pairs={{0,16},{8,24},{16,0},{24,8},{1,17},{9,25},{17,1},{25,9},{2,18},{10... | collective-permute-start | bytes 147464 | tf_op jit(solution)/shard_map/ppermute | solution.py:914
  257.1 29.4 %collective-permute-start.54 = (bf16[288,384]{1,0:T(8,128)(2,1)S(1)}, bf16[288,384]{1,0:T(8,128)(2,1)S(1)}, u32[]{:S(2)}, u32[]{:S(2)}) collective-permute-start(bf16[288,384]{1,0:T(8,128)(2,1)S(1)} %get-tuple-element.121), channel_id=1, source_target_pairs={{0,16},{8,24},{16,0},{24,8},{1,17},{9,25},{17,1},{25,9},{2,18},{10... | collective-permute-start | bytes 663560 | tf_op jit(solution)/shard_map/ppermute | solution.py:596
  258.2 28.3 %collective-permute-start.53 = (bf16[288,384]{1,0:T(8,128)(2,1)S(1)}, bf16[288,384]{1,0:T(8,128)(2,1)S(1)}, u32[]{:S(2)}, u32[]{:S(2)}) collective-permute-start(bf16[288,384]{1,0:T(8,128)(2,1)S(1)} %get-tuple-element.119), channel_id=1, source_target_pairs={{0,8},{8,16},{16,24},{24,0},{1,9},{9,17},{17,25},{25,1},{2,10},{10... | collective-permute-start | bytes 663560 | tf_op jit(solution)/shard_map/ppermute | solution.py:596
  259.4 28.4 %collective-permute-start.72 = (bf16[192,768]{1,0:T(8,128)(2,1)S(1)}, bf16[192,768]{1,0:T(8,128)(2,1)S(1)}, u32[]{:S(2)}, u32[]{:S(2)}) collective-permute-start(bf16[192,768]{1,0:T(8,128)(2,1)S(1)} %get-tuple-element.117), channel_id=1, source_target_pairs={{0,24},{8,0},{16,8},{24,16},{1,25},{9,1},{17,9},{25,17},{2,26},{10... | collective-permute-start | bytes 884744 | tf_op jit(solution)/shard_map/ppermute | solution.py:596
  262.0 34.7 %collective-permute-start.71 = (bf16[192,768]{1,0:T(8,128)(2,1)S(1)}, bf16[192,768]{1,0:T(8,128)(2,1)S(1)}, u32[]{:S(2)}, u32[]{:S(2)}) collective-permute-start(bf16[192,768]{1,0:T(8,128)(2,1)S(1)} %get-tuple-element.118), channel_id=1, source_target_pairs={{0,16},{8,24},{16,0},{24,8},{1,17},{9,25},{17,1},{25,9},{2,18},{10... | collective-permute-start | bytes 884744 | tf_op jit(solution)/shard_map/ppermute | solution.py:596
  262.1 36.1 %collective-permute-start.70 = (bf16[192,768]{1,0:T(8,128)(2,1)S(1)}, bf16[192,768]{1,0:T(8,128)(2,1)S(1)}, u32[]{:S(2)}, u32[]{:S(2)}) collective-permute-start(bf16[192,768]{1,0:T(8,128)(2,1)S(1)} %get-tuple-element.116), channel_id=1, source_target_pairs={{0,8},{8,16},{16,24},{24,0},{1,9},{9,17},{17,25},{25,1},{2,10},{10... | collective-permute-start | bytes 884744 | tf_op jit(solution)/shard_map/ppermute | solution.py:596
  308.6 21.9 %collective-permute-start.76 = (bf16[192,768]{1,0:T(8,128)(2,1)S(1)}, bf16[192,768]{1,0:T(8,128)(2,1)S(1)}, u32[]{:S(2)}, u32[]{:S(2)}) collective-permute-start(bf16[192,768]{1,0:T(8,128)(2,1)S(1)} %fusion.3.refs_0_), channel_id=1, source_target_pairs={{0,1},{1,0},{2,3},{3,2},{4,5},{5,4},{6,7},{7,6},{8,9},{9,8},{10,11... | collective-permute-start | bytes 884744 | tf_op jit(solution)/shard_map/ppermute | solution.py:590
  310.8 19.6 %collective-permute-start.77 = (bf16[192,768]{1,0:T(8,128)(2,1)S(1)}, bf16[192,768]{1,0:T(8,128)(2,1)S(1)}, u32[]{:S(2)}, u32[]{:S(2)}) collective-permute-start(bf16[192,768]{1,0:T(8,128)(2,1)S(1)} %collective-permute-done.73.refs_1_), channel_id=1, source_target_pairs={{0,1},{1,0},{2,3},{3,2},{4,5},{5,4},{6,7},{7,6},{8,9},{9,8},{10,11... | collective-permute-start | bytes 884744 | tf_op jit(solution)/shard_map/ppermute | solution.py:590
  (136 other events, 1096.7 us)

commit v2 on v1

v2 whole, which is shorter than its diff:
```python
from functools import partial

import jax
import jax.numpy as jnp
from jax import lax
from jax.experimental import pallas as pl
from jax.experimental.pallas import tpu as pltpu
from jax.sharding import PartitionSpec as P

HEADS = 12
HEAD = 64
CHIPS = 4
CORES = 2
LOCAL_HEADS = HEADS // CHIPS
COLS = LOCAL_HEADS * HEAD
PAIR = 2 * HEAD
WIDE = LOCAL_HEADS * PAIR

EPS = 1e-12
SCALE = 0.125
NEG = -1000000000.0
F32 = jnp.float32
BF16 = jnp.bfloat16

SMEM = pl.BlockSpec(memory_space=pltpu.SMEM)
VMEM = pl.BlockSpec(memory_space=pltpu.VMEM)


def sds(shape, dtype):
    return jax.ShapeDtypeStruct(shape, dtype)


def dot(left, right, over_left, over_right):
    return lax.dot_general(
        left, right, (((over_left,), (over_right,)), ((), ())), preferred_element_type=F32
    )


def cost(micros):
    return pl.CostEstimate(flops=1, bytes_accessed=int(micros * 3e6), transcendentals=0)


MICROS = {
    "mlp": 3.5, "mlp_back": 3.5, "mlp_grads": 3.3, "out_grads": 2, "qkv_grads": 5,
    "place_qkv": 3.5, "place_mlp": 3,
}


def run(body, name, outs, scalars, *arrays, scratch=(), flops=0, vmem=24):
    many = isinstance(outs, (list, tuple))
    return pl.pallas_call(
        body,
        out_shape=outs,
        in_specs=[SMEM] + [VMEM] * len(arrays),
        out_specs=[VMEM] * len(outs) if many else VMEM,
        scratch_shapes=list(scratch),
        name=name,
        cost_estimate=cost(MICROS.get(name, 1)),
        compiler_params=pltpu.CompilerParams(vmem_limit_bytes=vmem << 20),
    )(scalars, *arrays)


SHARD, CHIP, CORE, SPOT, SIDE, TALL = range(6)


def prep_qkv_body(sc, qw, kw, vw, ow, qb, *refs):
    vectors, (ub, own, other) = refs[:8], refs[8:]
    rows = kw.shape[0]
    half = rows // 2
    wide = [ref[...].astype(F32).reshape(1, rows) for ref in vectors]
    queries = qb[...].astype(F32)
    long = ub[...].astype(F32).reshape(1, 4 * rows)
    lines = [jnp.concatenate([queries[i : i + 1], queries[i + 1 : i + 2]], axis=1) for i in (0, 2)]
    lines += [jnp.concatenate(wide[i : i + 2], axis=1) for i in range(0, 8, 2)]
    lines += [long[:, 0 : 2 * rows], long[:, 2 * rows :]]
    small = jnp.concatenate(lines, axis=0).astype(BF16)
    end = rows + half + small.shape[0]
    own[rows + half : end, :] = small
    third = ow[pl.ds(pl.multiple_of(sc[SPOT] * (rows // 4), rows // 4), rows // 4), :]
    own[end : end + rows // 4, :] = third[:, 0:WIDE]
    own[end + rows // 4 :, :] = third[:, WIDE:]
    for chip in range(CHIPS):
        for core in range(CORES):

            @pl.when((sc[CHIP] == chip) & (sc[CORE] == core))
            def _():
                lo = chip * COLS
                for out, group in ((own, core), (other, 1 - core)):
                    first = qw[2 * group, :, lo : lo + COLS]
                    second = qw[2 * group + 1, :, lo : lo + COLS]
                    mix = []
                    for h in range(LOCAL_HEADS):
                        mix += [
                            first[:, h * HEAD : (h + 1) * HEAD],
                            second[:, h * HEAD : (h + 1) * HEAD],
                        ]
                    out[0:rows, :] = jnp.concatenate(mix, axis=1)
                    src = vw if group else kw
                    out[rows : rows + half, 0:COLS] = src[0:half, lo : lo + COLS]
                    out[rows : rows + half, COLS:] = src[half:rows, lo : lo + COLS]


def prep_mlp_body(sc, up, down, out):
    rows, ff = up.shape
    part = ff // 4
    side = part // 2
    unit = side // 2
    for chip_x in range(2):

        @pl.when(sc[SIDE] == chip_x)
        def _():
            for tall in range(2):
                for piece in range(4):
                    lo = piece * part + chip_x * side + tall * unit
                    out[tall * rows : (tall + 1) * rows, piece * unit : (piece + 1) * unit] = up[
                        :, lo : lo + unit
                    ]

    out[2 * rows :, :] = down[...]


def assemble_out_body(shards, sc, whole, own, other, own_far, other_far, wo):
    rows = wo.shape[0] // shards
    small = rows // 4
    wo[pl.ds(pl.multiple_of(sc[SHARD] * rows, rows), rows), :] = whole[...]
    for rel, ref in enumerate((own, other, own_far, other_far)):
        for shift in range(1, shards):
            owner = lax.rem(sc[SHARD] + shards - shift, shards)
            at = pl.multiple_of(owner * rows + (sc[SPOT] ^ rel) * small, small)
            wo[pl.ds(at, small), :] = ref[shift - 1]


def assemble_mlp_body(shards, sc, up, down, *refs):
    pieces, (wup, wdn) = refs[:-2], refs[-2:]
    rows = wup.shape[0] // shards
    part = wdn.shape[0] // shards
    width = wdn.shape[1]
    unit = part // 2
    small = rows // 4
    at = pl.multiple_of(sc[SHARD] * rows, rows)
    for chip_x in range(2):

        @pl.when(sc[SIDE] == chip_x)
        def _():
            for tall in range(2):
                for piece in range(4):
                    lo = piece * 2 * part + chip_x * part + tall * unit
                    to = tall * width + piece * unit
                    wup[pl.ds(at, rows), to : to + unit] = up[:, lo : lo + unit]

    for tall in range(2):
        at = pl.multiple_of(tall * width + sc[SHARD] * unit, unit)
        lo = pl.multiple_of(sc[SIDE] * part + tall * unit, unit)
        wdn[pl.ds(at, unit), :] = down[pl.ds(lo, unit), :]
    for index, ref in enumerate(pieces):
        rel, shift = index // (shards - 1), index % (shards - 1) + 1
        spot = sc[SPOT] ^ (rel // 2 + rel % 2 * 2)
        owner = lax.rem(sc[SHARD] + shards - shift, shards)
        at = pl.multiple_of(owner * rows + spot * small, small)
        wup[pl.ds(at, small), 0:width] = ref[0:small, :]
        wup[pl.ds(at, small), width:] = ref[small : 2 * small, :]
        at = (spot // 2) * width + owner * unit + (spot % 2) * (unit // 2)
        at = pl.multiple_of(at, unit // 2)
        wdn[pl.ds(at, unit // 2), :] = ref[2 * small :, :]


def split_pairs(line):
    pieces = [
        jnp.concatenate(
            [line[:, h * PAIR + t * HEAD : h * PAIR + (t + 1) * HEAD] for h in range(LOCAL_HEADS)],
            axis=1,
        )
        for t in range(2)
    ]
    return jnp.concatenate(pieces, axis=1)


def join_pairs(left, right):
    mix = []
    for h in range(LOCAL_HEADS):
        mix += [left[:, h * HEAD : (h + 1) * HEAD], right[:, h * HEAD : (h + 1) * HEAD]]
    return jnp.concatenate(mix, axis=1)


def qkv_body(shards, sc, meta, mine, other_mine, own_x, other_x, *refs):
    own_w = [mine] + list(refs[: shards - 1])
    other_w = [other_mine] + list(refs[shards - 1 : 2 * shards - 2])
    wall, pq, pk, vv, vecs, upb, out_own, out_other, held = refs[2 * shards - 2 :]
    slots = own_x.shape[1]
    small = out_own.shape[1]
    width = wall.shape[1]
    rows = width // shards
    half = rows // 2
    unit = rows
    for which in range(CORES):
        group = sc[CORE] ^ which
        keep = (group == 0).astype(F32).astype(BF16)
        for shift in range(shards):
            ref = (other_w if which else own_w)[shift]
            if shift > 0:
                third = out_other if which else out_own
                end = ref.shape[0] - 2 * small
                third[shift - 1, :, 0:WIDE] = ref[end : end + small, :]
                third[shift - 1, :, WIDE:] = ref[end + small :, :]
            owner = lax.rem(sc[SHARD] + shards - shift, shards)
            at = pl.multiple_of(owner * rows, half)
            wall[group, pl.ds(at, rows), 0:WIDE] = ref[0:rows, :]
            if which == 0:
                held[owner] = ref[rows + half : ref.shape[0] - 2 * small, :].astype(F32)
            for part in range(2):
                mix = []
                for h in range(LOCAL_HEADS):
                    lo = part * COLS + h * HEAD
                    one = ref[rows : rows + half, lo : lo + HEAD]
                    mix += [one, one * keep]
                low = pl.multiple_of(owner * rows + part * half, half)
                wall[group, pl.ds(low, half), WIDE:] = jnp.concatenate(mix, axis=1)
    vecs[...] = jnp.zeros_like(vecs)
    for shard in range(shards):
        lo = shard * rows
        for row in range(6):
            line = 3 + row // 2
            col = (row % 2) * rows
            vecs[row : row + 1, lo : lo + rows] = held[shard, line : line + 1, col : col + rows]
        for chip_x in range(2):

            @pl.when(sc[SIDE] == chip_x)
            def _():
                for tall in range(2):
                    to = tall * width + shard * unit
                    upb[0:1, to : to + unit] = held[
                        shard, 6 + chip_x : 7 + chip_x, tall * unit : (tall + 1) * unit
                    ]

    table = held[sc[CHIP]]
    bias = [join_pairs(table[i : i + 1, 0:COLS], table[i : i + 1, COLS:]) for i in range(2)]
    key_bias = join_pairs(table[2:3, 0:COLS], table[2:3, 0:COLS])
    value_bias = join_pairs(table[2:3, COLS:], jnp.zeros((1, COLS), F32))
    flags = meta[...].T
    lane = lax.broadcasted_iota(jnp.int32, (1, WIDE), 1)
    left = (lane % PAIR) < HEAD
    for block in range(8):
        tokens = (own_x if block < 4 else other_x)[sc[CHIP] ^ (block % 4)]
        word = flags[:, block : block + 1] > 0
        at = slice(block * slots, (block + 1) * slots)
        if block < 4:
            first = dot(tokens, wall[0], 1, 0)
            second = dot(tokens, wall[1], 1, 0)
            query = jnp.where(word, first[:, 0:WIDE] + bias[0], second[:, 0:WIDE] + bias[1]) * SCALE
            pq[at, :] = query.astype(BF16)
            key, value = first[:, WIDE:], second[:, WIDE:]
        else:
            key = dot(tokens, wall[0, :, WIDE:], 1, 0)
            value = dot(tokens, wall[1, :, WIDE:], 1, 0)
        pk[at, :] = jnp.where(left == word, key + key_bias, 0.0).astype(BF16)
        vv[at, :] = (value + value_bias).astype(BF16)


def attend_body(step, pq, pk, vv, valid, probs, cx):
    head = pl.program_id(0)
    count = pq.shape[0]
    slots = count // 4
    keep = valid[...] > 0
    keys = pk[...]
    values = vv[...]
    for start in range(0, count, step):
        scores = dot(pq[start : start + step, :], keys, 1, 1)
        scores = jnp.where(keep, scores, NEG)
        top = jnp.max(scores, axis=-1, keepdims=True)
        expo = jnp.exp(scores - top)
        share = 1.0 / jnp.sum(expo, axis=-1, keepdims=True)
        low = (expo * share).astype(BF16)
        probs[0, start : start + step, :] = low
        mixed = dot(low, values, 1, 0)[:, 0:HEAD].astype(BF16)
        for h in range(LOCAL_HEADS):

            @pl.when(head == h)
            def _():
                for at in range(0, step, slots):
                    block = (start + at) // slots
                    mid = at + slots // 2
                    cx[block, :, h * HEAD : (h + 1) * HEAD] = mixed[at:mid]
                    cx[block, :, COLS + h * HEAD : COLS + (h + 1) * HEAD] = mixed[mid : at + slots]


def attend(pq, pk, vv, valid, slots):
    count, keys = pq.shape[0], pk.shape[0]
    step = 2 * slots if keys <= 2048 else slots
    limit = 14 if keys <= 2048 else 56
    return pl.pallas_call(
        partial(attend_body, step),
        grid=(LOCAL_HEADS,),
        in_specs=[
            pl.BlockSpec((count, PAIR), lambda h: (0, h)),
            pl.BlockSpec((keys, PAIR), lambda h: (0, h)),
            pl.BlockSpec((keys, PAIR), lambda h: (0, h)),
            pl.BlockSpec((1, keys), lambda h: (0, 0)),
        ],
        out_specs=[
            pl.BlockSpec((1, count, keys), lambda h: (h, 0, 0)),
            pl.BlockSpec((4, slots // 2, 2 * COLS), lambda h: (0, 0, 0)),
        ],
        out_shape=[
            sds((LOCAL_HEADS, count, keys), BF16),
            sds((4, slots // 2, 2 * COLS), BF16),
        ],
        name="attend",
        cost_estimate=cost(5.5),
        compiler_params=pltpu.CompilerParams(vmem_limit_bytes=limit << 20),
    )(pq, pk, vv, valid)


def attend_back_body(step, split, gc0, gc1, gc2, gc3, pq, pk, vv, probs, dq, *refs):
    head = pl.program_id(0)
    count = pq.shape[0]
    slots = count // 4
    half = slots // 2
    if split:
        dk_own, dv_own, dkv_other, gcs, dk, dv = refs
    else:
        dk, dv, gcs = refs

    @pl.when(head == 0)
    def _():
        gcs[...] = jnp.zeros_like(gcs)
        for block, ref in enumerate((gc0, gc1, gc2, gc3)):
            for h in range(LOCAL_HEADS):
                lo = block * slots
                gcs[h, lo : lo + half, 0:HEAD] = ref[:, h * HEAD : (h + 1) * HEAD]
                gcs[h, lo + half : lo + slots, 0:HEAD] = ref[
                    :, COLS + h * HEAD : COLS + (h + 1) * HEAD
                ]

    keys = pk[...]
    values = vv[...]
    for start in range(0, count, step):
        grad = gcs[head, start : start + step, :]
        low = probs[0, start : start + step, :]
        wide = low.astype(F32)
        moved = dot(grad, values, 1, 1)
        inner = jnp.sum(wide * moved, axis=-1, keepdims=True)
        ds = (wide * (moved - inner)).astype(BF16)
        query = pq[start : start + step, :]
        dq[start : start + step, :] = dot(ds, keys, 1, 0)
        key_part = dot(ds, query, 0, 0)
        value_part = dot(low, grad, 0, 0)
        if start == 0:
            dk[...] = key_part
            dv[...] = value_part
        else:
            dk[...] += key_part
            dv[...] += value_part
    if split:
        dk_own[...] = dk[0:count, :]
        dv_own[...] = dv[0:count, :]
        dkv_other[0] = dk[count:, :].astype(BF16)
        dkv_other[1] = dv[count:, :].astype(BF16)


def attend_back(pieces, pq, pk, vv, probs, slots, split):
    count, keys = pq.shape[0], pk.shape[0]
    step = 2 * slots if keys <= 2048 else slots
    limit = 20 if keys <= 2048 else 58
    piece = pl.BlockSpec((slots // 2, 2 * COLS), lambda h: (0, 0))
    rows = pl.BlockSpec((count, PAIR), lambda h: (0, h))
    cols = pl.BlockSpec((keys, PAIR), lambda h: (0, h))
    scratch = [pltpu.VMEM((LOCAL_HEADS, count, PAIR), BF16)]
    if split:
        specs = [rows, rows, rows, pl.BlockSpec((2, count, PAIR), lambda h: (0, 0, h))]
        shapes = [sds((count, WIDE), F32)] * 3 + [sds((2, count, WIDE), BF16)]
        scratch += [pltpu.VMEM((keys, PAIR), F32), pltpu.VMEM((keys, PAIR), F32)]
    else:
        specs = [rows, cols, cols]
        shapes = [sds((count, WIDE), F32), sds((keys, WIDE), F32), sds((keys, WIDE), F32)]
    return pl.pallas_call(
        partial(attend_back_body, step, split),
        grid=(LOCAL_HEADS,),
        in_specs=[piece] * 4
        + [rows, cols, cols, pl.BlockSpec((1, count, keys), lambda h: (h, 0, 0))],
        out_specs=specs,
        out_shape=shapes,
        scratch_shapes=scratch,
        name="attend_back",
        cost_estimate=cost(6),
        compiler_params=pltpu.CompilerParams(vmem_limit_bytes=limit << 20),
    )(*pieces, pq, pk, vv, probs)


def unpack(piece):
    return jnp.concatenate([piece[:, 0:COLS], piece[:, COLS:]], axis=0)


def normalize(summed):
    center = summed - jnp.mean(summed, axis=-1, keepdims=True)
    spread = jnp.mean(center * center, axis=-1, keepdims=True)
    rate = lax.rsqrt(spread + EPS)
    return center * rate, rate


def norm_back(grad, unit, rate, gain):
    scaled = grad * gain
    mean_one = jnp.mean(scaled, axis=-1, keepdims=True)
    mean_two = jnp.mean(scaled * unit, axis=-1, keepdims=True)
    return rate * (scaled - mean_one - unit * mean_two)


def total(values):
    return jnp.sum(values, axis=0, keepdims=True)


OUT_B, GAIN_1, SHIFT_1, DOWN_B, GAIN_2, SHIFT_2 = range(6)


def norm_one_body(sc, vecs, cx0, cx1, cx2, cx3, wo, hidden, low, unit_out, rate_out):
    acc = hidden[...].astype(F32) + vecs[OUT_B : OUT_B + 1, :]
    for rel, ref in enumerate((cx0, cx1, cx2, cx3)):
        at = pl.multiple_of((sc[CHIP] ^ rel) * COLS, COLS)
        acc += dot(unpack(ref[...]), wo[pl.ds(at, COLS), :], 1, 0)
    unit, rate = normalize(acc)
    first = unit * vecs[GAIN_1 : GAIN_1 + 1, :] + vecs[SHIFT_1 : SHIFT_1 + 1, :]
    low[...] = first.astype(BF16)
    unit_out[...] = unit
    rate_out[...] = jnp.broadcast_to(rate, rate_out.shape)


def mlp_body(chunk, sc, bias, x0, x1, wup, wdn, act, act_send, slope, own, send):
    slots = x0.shape[0]
    width = x0.shape[1]
    tokens = jnp.concatenate([x0[...], x1[...]], axis=0)
    acc = None
    for lo in range(0, wup.shape[1], chunk):
        pre = dot(tokens, wup[:, lo : lo + chunk], 1, 0) + bias[0:1, lo : lo + chunk]
        cdf = 0.5 * (1.0 + lax.erf(pre * 0.7071067811865476))
        pdf = jnp.exp(-0.5 * pre * pre) * 0.3989422804014327
        out = (pre * cdf).astype(BF16)
        slope[:, lo : lo + chunk] = cdf + pre * pdf
        to_quarter(sc, out, lo, width, act, act_send)
        part = dot(out, wdn[lo : lo + chunk, :], 1, 0)
        acc = part if acc is None else acc + part
    own[...] = acc[0:slots]
    send[...] = acc[slots:].astype(BF16)


def to_quarter(sc, values, lo, width, keep, send):
    tall, at = lo // width, lo % width

    @pl.when(sc[TALL] == tall)
    def _():
        keep[:, at : at + values.shape[1]] = values

    @pl.when(sc[TALL] != tall)
    def _():
        send[:, at : at + values.shape[1]] = values


def norm_two_body(sc, vecs, meta, own, received, unit_one, cotangent, output, gs, gs_low, sums):
    valid = meta[...].T[:, 8:9]
    first = unit_one[...] * vecs[GAIN_1 : GAIN_1 + 1, :] + vecs[SHIFT_1 : SHIFT_1 + 1, :]
    acc = own[...] + received[...].astype(F32) + vecs[DOWN_B : DOWN_B + 1, :] + first
    unit, rate = normalize(acc)
    gain = vecs[GAIN_2 : GAIN_2 + 1, :]
    output[...] = ((unit * gain + vecs[SHIFT_2 : SHIFT_2 + 1, :]) * valid).astype(BF16)
    grad = cotangent[...].astype(F32) * valid
    back = norm_back(grad, unit, rate, gain)
    gs[...] = back
    gs_low[...] = back.astype(BF16)
    sums[...] = jnp.zeros_like(sums)
    sums[DOWN_B : DOWN_B + 1, :] = total(back)
    sums[GAIN_2 : GAIN_2 + 1, :] = total(grad * unit)
    sums[SHIFT_2 : SHIFT_2 + 1, :] = total(grad)


def mlp_back_body(chunk, sc, g0, g1, slope, wup, wdn, low_keep, low_send, sums, own, send):
    slots = g0.shape[0]
    width = g0.shape[1]
    grads = jnp.concatenate([g0[...], g1[...]], axis=0)
    acc = None
    sums[...] = jnp.zeros_like(sums)
    for lo in range(0, wup.shape[1], chunk):
        pre = dot(grads, wdn[lo : lo + chunk, :], 1, 1) * slope[:, lo : lo + chunk]
        sums[0:1, lo : lo + chunk] = total(pre)
        low = pre.astype(BF16)
        to_quarter(sc, low, lo, width, low_keep, low_send)
        part = dot(low, wup[:, lo : lo + chunk], 1, 1)
        acc = part if acc is None else acc + part
    own[...] = acc[0:slots]
    send[...] = acc[slots:].astype(BF16)


def mlp_grads_body(
    shards, sc, x0, x1, x2, x3, g0, g1, g2, g3, act, act_r, low, low_r, keep, send
):
    tokens = jnp.concatenate([x0[...], x1[...], x2[...], x3[...]], axis=0)
    grads = jnp.concatenate([g0[...], g1[...], g2[...], g3[...]], axis=0)
    hidden = jnp.concatenate([act[...], act_r[...]], axis=0)
    back = jnp.concatenate([low[...], low_r[...]], axis=0)
    rows = tokens.shape[1] // shards
    for at in range(shards):
        lo = at * rows
        up = dot(tokens[:, lo : lo + rows], back, 0, 0)
        down = dot(hidden[:, lo : lo + rows], grads, 0, 0)

        @pl.when(sc[CORE] == 0)
        def _():
            keep[at] = up
            send[at] = down.astype(BF16)

        @pl.when(sc[CORE] == 1)
        def _():
            keep[at] = down
            send[at] = up.astype(BF16)


def fan_body(shards, sc, keep, received, own, *sends):
    at = sc[SHARD]
    own[...] = keep[at] + received[at].astype(F32)
    for shift in range(1, shards):
        at = lax.rem(sc[SHARD] + shift, shards)
        sends[shift - 1][...] = (keep[at] + received[at].astype(F32)).astype(BF16)


def out_fan_body(sc, keep, received, own, *sends):
    small = own.shape[1]
    for rel in range(4):
        at = pl.multiple_of((sc[CHIP] ^ rel) * small, small)
        value = keep[:, pl.ds(at, small), :] + received[:, pl.ds(at, small), :].astype(F32)
        if rel == 0:
            own[...] = value
        else:
            sends[rel - 1][...] = value.astype(BF16)


def qkv_fan_body(shards, sc, keep, received, own, *sends):
    main = received.shape[1]
    for shift in range(shards):
        at = lax.rem(sc[SHARD] + shift, shards)
        ref = own if shift == 0 else sends[shift - 1]
        ref[0:main, :] = (keep[at, 0:main, :] + received[at].astype(F32)).astype(ref.dtype)
        ref[main:, :] = keep[at, main:, :].astype(ref.dtype)


def out_shards_body(shards, sc, own_all, r1, r2, r3, own, *sends):
    for shift in range(shards):
        at = lax.rem(sc[SHARD] + shift, shards)
        value = own_all[at] + r1[at].astype(F32) + r2[at].astype(F32) + r3[at].astype(F32)
        ref = own if shift == 0 else sends[shift - 1]
        ref[...] = value.astype(ref.dtype)


def gather_sum_body(sc, own, *refs):
    acc = own[...]
    for ref in refs[:-1]:
        acc += ref[...].astype(F32)
    refs[-1][...] = acc.astype(refs[-1].dtype)


def two_sums_body(count, sc, *refs):
    out = refs[-1]
    at = 0
    for part in (refs[:count], refs[count:-1]):
        acc = part[0][...]
        for ref in part[1:]:
            acc += ref[...].astype(F32)
        out[at : at + acc.shape[0], :] = acc.astype(out.dtype)
        at += acc.shape[0]


def input_grad_body(sc, base, own, r1, r2, r3, out):
    out[...] = (
        base[...] + own[...] + r1[...].astype(F32) + r2[...].astype(F32) + r3[...].astype(F32)
    )


def norm_one_back_body(
    sc, vecs, own, received, gs, unit_one, rate_one, wo, gf, gf_low, gcx, sums
):
    grad = gs[...] + own[...] + received[...].astype(F32)
    unit = unit_one[...]
    rate = rate_one[:, 0:1]
    back = norm_back(grad, unit, rate, vecs[GAIN_1 : GAIN_1 + 1, :])
    gf[...] = back
    low = back.astype(BF16)
    gf_low[...] = low
    sums[...] = jnp.zeros_like(sums)
    sums[OUT_B : OUT_B + 1, :] = total(back)
    sums[GAIN_1 : GAIN_1 + 1, :] = total(grad * unit)
    sums[SHIFT_1 : SHIFT_1 + 1, :] = total(grad)
    half = back.shape[0] // 2
    for rel in range(4):
        at = pl.multiple_of((sc[CHIP] ^ rel) * COLS, COLS)
        part = dot(low, wo[pl.ds(at, COLS), :], 1, 1).astype(BF16)
        gcx[rel, :, 0:COLS] = part[0:half]
        gcx[rel, :, COLS:] = part[half:]


def out_grads_body(sc, cx0, cx1, cx2, cx3, gf_low, keep, send):
    low = gf_low[...]
    half = keep.shape[2]
    for rel, ref in enumerate((cx0, cx1, cx2, cx3)):
        block = dot(unpack(ref[...]), low, 0, 0)
        chip = sc[CHIP] ^ rel
        for core in range(CORES):

            @pl.when(sc[CORE] == core)
            def _():
                keep[chip] = block[:, core * half : (core + 1) * half]
                other = 1 - core
                send[chip] = block[:, other * half : (other + 1) * half].astype(BF16)


def qkv_grads_body(
    shards, sc, meta, dq, dk_own, dv_own, dkv_rec, wall, sums_one, sums_two, sums_up,
    x, own, send, keep_w, send_w, packed,
):
    slots = x.shape[1]
    flags = meta[...].T
    lane = lax.broadcasted_iota(jnp.int32, (1, WIDE), 1)
    left = (lane % PAIR) < HEAD
    width = wall.shape[1]
    rows = width // shards
    half = rows // 2
    acc = [0.0] * 4
    for block in range(4):
        at = slice(block * slots, (block + 1) * slots)
        word = flags[:, block : block + 1] > 0
        query = dq[at, :] * SCALE
        parts = (
            jnp.where(word, query, 0.0),
            jnp.where(word, 0.0, query),
            jnp.where(left == word, dk_own[at, :] + dkv_rec[0, at, :].astype(F32), 0.0),
            dv_own[at, :] + dkv_rec[1, at, :].astype(F32),
        )
        acc = [a + total(p) for a, p in zip(acc, parts)]
        packed[0, at, 0:WIDE] = parts[0].astype(BF16)
        packed[1, at, 0:WIDE] = parts[1].astype(BF16)
        packed[0, at, WIDE:] = parts[2].astype(BF16)
        packed[1, at, WIDE:] = parts[3].astype(BF16)
    tokens = jnp.concatenate([x[sc[CHIP] ^ rel] for rel in range(4)], axis=0)
    for group_rel, ref in enumerate((keep_w, send_w)):
        group = sc[CORE] ^ group_rel
        for at in range(shards):
            grad = dot(tokens[:, at * rows : (at + 1) * rows], packed[group], 0, 0)
            ref[at, 0:rows, :] = grad[:, 0:WIDE].astype(ref.dtype)
            folded = jnp.concatenate(
                [
                    grad[:, WIDE + h * PAIR : WIDE + h * PAIR + HEAD]
                    + grad[:, WIDE + h * PAIR + HEAD : WIDE + (h + 1) * PAIR]
                    for h in range(LOCAL_HEADS)
                ],
                axis=1,
            ).astype(ref.dtype)
            ref[at, rows : rows + half, 0:COLS] = folded[0:half]
            ref[at, rows : rows + half, COLS:] = folded[half:]
    for block in range(4):
        at = slice(block * slots, (block + 1) * slots)
        back = dot(packed[0, at, :], wall[0], 1, 1) + dot(packed[1, at, :], wall[1], 1, 1)
        if block == 0:
            own[...] = back
        else:
            send[block - 1] = back.astype(BF16)
    keys = split_pairs(acc[2])
    values = split_pairs(acc[3])
    heads = [
        split_pairs(acc[0]),
        split_pairs(acc[1]),
        jnp.concatenate([keys[:, 0:COLS] + keys[:, COLS:], values[:, 0:COLS]], axis=1),
    ]
    norms = sums_one[...] + sums_two[...]
    for at in range(shards):
        mine = (sc[CHIP] == at).astype(F32)
        lo = at * rows
        lines = [line * mine for line in heads]
        for row in range(0, 6, 2):
            lines.append(
                jnp.concatenate(
                    [norms[row : row + 1, lo : lo + rows], norms[row + 1 : row + 2, lo : lo + rows]],
                    axis=1,
                )
            )
        units = jnp.concatenate(
            [sums_up[0:1, t * width + lo : t * width + lo + rows] for t in range(2)], axis=1
        )
        side = sc[SIDE].astype(F32)
        lines += [units * (1.0 - side), units * side]
        keep_w[at, rows + half :, :] = jnp.concatenate(lines, axis=0)


def place_qkv_body(sc, p0, p1, p2, p3, others, qg, kg, vg, og, qb, *refs):
    vectors, (ub, held) = refs[:8], refs[8:]
    rows = kg.shape[0]
    half = rows // 2
    small = rows // 4
    lines = 0.0
    for core_rel in range(CORES):
        for rel in range(4):
            value = (p0, p1, p2, p3)[rel][...] if core_rel == 0 else others[rel]
            lines += value[rows + half : rows + half + 8, :].astype(F32)
            held[sc[CORE] ^ core_rel, sc[CHIP] ^ rel] = value
    for core in range(CORES):
        for chip in range(CHIPS):
            piece = held[core, chip].astype(F32)
            lo = chip * COLS
            for which in range(2):
                qg[2 * core + which, :, lo : lo + COLS] = jnp.concatenate(
                    [
                        piece[0:rows, h * PAIR + which * HEAD : h * PAIR + (which + 1) * HEAD]
                        for h in range(LOCAL_HEADS)
                    ],
                    axis=1,
                )
            ref = kg if core == 0 else vg
            ref[0:half, lo : lo + COLS] = piece[rows : rows + half, 0:COLS]
            ref[half:, lo : lo + COLS] = piece[rows : rows + half, COLS:]
            og[chip * small : (chip + 1) * small, core * 2 * COLS : (core + 1) * 2 * COLS] = piece[
                rows + half + 8 :, :
            ]
    for which in range(4):
        qb[which : which + 1, :] = lines[
            which // 2 : which // 2 + 1, (which % 2) * COLS : (which % 2 + 1) * COLS
        ]
    for index, ref in enumerate(vectors):
        ref[...] = lines[2 + index // 2, (index % 2) * rows : (index % 2 + 1) * rows]
    ub[...] = jnp.concatenate([lines[6], lines[7]], axis=0)


def place_mlp_body(sc, p0, p1, p2, p3, others, ug, dg, held):
    rows, ff = ug.shape
    part = ff // 4
    side = part // 2
    unit = side // 2
    for core_rel in range(CORES):
        for rel in range(4):
            value = (p0, p1, p2, p3)[rel][...] if core_rel == 0 else others[rel]
            held[sc[CORE] ^ core_rel, sc[CHIP] ^ rel] = value
    for chip in range(CHIPS):
        lo = (chip & 1) * side + (chip >> 1) * unit
        piece = held[0, chip].astype(F32)
        for shard in range(4):
            at = shard * part + lo
            ug[:, at : at + unit] = piece[:, shard * unit : (shard + 1) * unit]
        dg[lo : lo + unit, :] = held[1, chip].astype(F32)


def local(
    shards,
    lanes,
    hidden,
    lengths,
    row_types,
    query_weight,
    query_bias,
    key_weight,
    key_bias,
    value_weight,
    value_bias,
    out_weight,
    out_bias,
    norm1_gain,
    norm1_bias,
    up_weight,
    up_bias,
    down_weight,
    down_bias,
    norm2_gain,
    norm2_bias,
    cotangent,
):
    groups = lanes // (CHIPS * CORES)
    shard = lax.axis_index("shard")
    lane = lax.axis_index("ctx")
    core, chip, group = lane & 1, (lane >> 1) & 3, lane >> 3
    chip_x, chip_y = chip & 1, chip >> 1
    spot = chip_y * 2 + core
    scalars = jnp.stack([shard, chip, core, spot, chip_x, chip_y]).astype(jnp.int32)
    sets = [[g * 8 + i for g in range(groups)] for i in range(8)]

    def across(value, mask, name):
        with jax.named_scope(f"{name}_{mask}"):
            return lax.ppermute(value, "ctx", [(i, i ^ mask) for i in range(lanes)])

    def chips(value, rel, name):
        return across(value, rel << 1, name)

    def turn(value, shift, name):
        with jax.named_scope(f"{name}_z{shift}"):
            return lax.ppermute(value, "shard", [(i, (i + shift) % shards) for i in range(shards)])

    def after(value, *others):
        return lax.optimization_barrier((value,) + others)[0]

    width = hidden.shape[2]
    slots = hidden.shape[1]
    rows = width // shards
    ff = up_weight.shape[1]
    part = ff // shards
    side = part // 2
    hid = hidden[0]
    cot = cotangent[0]
    small_rows = 8
    main = rows + rows // 2

    mine, other_mine = run(
        prep_qkv_body,
        "prep_qkv",
        [sds((main + small_rows + rows // 2, WIDE), BF16), sds((main, WIDE), BF16)],
        scalars,
        query_weight, key_weight, value_weight, out_weight, query_bias,
        key_bias, value_bias, out_bias, norm1_gain, norm1_bias,
        down_bias, norm2_gain, norm2_bias, up_bias,
        vmem=60,
    )
    own_w = [turn(mine, d, "qkvw") for d in range(1, shards)]
    quarter = rows // 4
    mlp_one = run(
        prep_mlp_body,
        "prep_mlp",
        sds((2 * quarter + side // 4, width), BF16),
        scalars,
        lax.dynamic_slice_in_dim(up_weight, spot * quarter, quarter, 0),
        lax.dynamic_slice_in_dim(down_weight, chip_x * side + spot * (side // 4), side // 4, 0),
    )
    mlp_z = [turn(after(mlp_one, mine), d, "mlpw") for d in range(1, shards)]
    planes = [[g * 8 + 2 * j + c for j in range(CHIPS)] for g in range(groups) for c in range(CORES)]
    own_x = lax.all_gather(after(hid, mlp_one), "ctx", axis_index_groups=planes)
    other_x = across(own_x, 1, "hid")
    other_w = [across(piece, 1, "qkvw") for piece in own_w]

    kinds = row_types.reshape(-1, slots)
    blocks = [group * 8 + (chip ^ rel) * 2 + (core ^ c) for c in range(CORES) for rel in range(4)]
    places = jnp.arange(slots, dtype=jnp.int32)
    word = jnp.concatenate([lax.dynamic_slice_in_dim(kinds, b, 1, 0) for b in blocks], axis=0)
    starts = jnp.stack(blocks)[:, None] * slots
    live = (starts + places[None, :] < lengths[0]).astype(F32)
    meta = jnp.concatenate([(word == 0).astype(F32), live], axis=0)

    wall, pq, pk, vv, vecs, up_shift, out_own, out_other = run(
        partial(qkv_body, shards),
        "qkv",
        [
            sds((2, width, 2 * WIDE), BF16),
            sds((4 * slots, WIDE), BF16),
            sds((8 * slots, WIDE), BF16),
            sds((8 * slots, WIDE), BF16),
            sds((8, width), F32),
            sds((1, ff // 2), F32),
            sds((shards - 1, quarter, width), BF16),
            sds((shards - 1, quarter, width), BF16),
        ],
        scalars,
        meta, mine, other_mine, own_x, other_x, *own_w, *other_w,
        scratch=[pltpu.VMEM((shards, small_rows, WIDE), F32)],
    )
    out_far = across(out_own, 4, "outw")
    valid = live.reshape(1, 8 * slots)
    if groups > 1:
        gather = partial(lax.all_gather, axis_name="ctx", axis_index_groups=sets, tiled=True)
        pk, vv = gather(pk, axis=0), gather(vv, axis=0)
        valid = gather(valid, axis=1)
    probs, cx = attend(pq, pk, vv, valid, slots)
    cxs = [cx[0]] + [chips(cx[rel], rel, "cx") for rel in range(1, 4)]
    *cxs, out_far = lax.optimization_barrier((*cxs, out_far))
    wo = run(
        partial(assemble_out_body, shards),
        "assemble_out",
        sds((width, width), BF16),
        scalars,
        out_weight, out_own, out_other, out_far, across(out_far, 1, "outw"),
    )
    mlp_z = after(mlp_z, cx)
    mlp_far = [across(piece, 4, "mlpw") for piece in mlp_z]
    pieces = mlp_z + mlp_far
    wup, wdn = run(
        partial(assemble_mlp_body, shards),
        "assemble_mlp",
        [sds((width, ff // 2), BF16), sds((ff // 2, width), BF16)],
        scalars,
        up_weight, down_weight, *pieces, *[across(piece, 1, "mlpw") for piece in pieces],
    )

    low_one, unit_one, rate_one = run(
        norm_one_body,
        "norm_one",
        [sds((slots, width), BF16), sds((slots, width), F32), sds((slots, 128), F32)],
        scalars,
        vecs, *cxs, wo, hid,
    )
    low_two = chips(low_one, 1, "mlpx")
    low_two, far_one = lax.optimization_barrier((low_two, across(low_one, 4, "mlpy_x1")))
    far_two = across(low_two, 4, "mlpy_x2")
    act, act_send, slope, own, send = run(
        partial(mlp_body, 384),
        "mlp",
        [
            sds((2 * slots, ff // 4), BF16),
            sds((2 * slots, ff // 4), BF16),
            sds((2 * slots, ff // 2), F32),
            sds((slots, width), F32),
            sds((slots, width), BF16),
        ],
        scalars,
        up_shift, low_one, low_two, wup, wdn,
    )
    received, far_two = lax.optimization_barrier((chips(send, 1, "mlpp"), far_two))
    act_far = across(act_send, 4, "mlpy_a")
    output, gs, gs_low, sums_two = run(
        norm_two_body,
        "norm_two",
        [
            sds((slots, width), BF16),
            sds((slots, width), F32),
            sds((slots, width), BF16),
            sds((8, width), F32),
        ],
        scalars,
        vecs, meta, own, received, unit_one, cot,
    )
    gs_other, gs_far_one, act_far = lax.optimization_barrier(
        (chips(gs_low, 1, "mlpg"), across(gs_low, 4, "mlpy_g1"), act_far)
    )
    gs_far_two = across(gs_other, 4, "mlpy_g2")
    low_keep, low_send, sums_up, own, send = run(
        partial(mlp_back_body, 384),
        "mlp_back",
        [
            sds((2 * slots, ff // 4), BF16),
            sds((2 * slots, ff // 4), BF16),
            sds((8, ff // 2), F32),
            sds((slots, width), F32),
            sds((slots, width), BF16),
        ],
        scalars,
        gs_low, gs_other, slope, wup, wdn,
    )
    received, gs_far_two = lax.optimization_barrier((chips(send, 1, "mlpb"), gs_far_two))
    low_far = across(low_send, 4, "mlpy_l")
    gf, gf_low, gcx, sums_one = run(
        norm_one_back_body,
        "norm_one_back",
        [
            sds((slots, width), F32),
            sds((slots, width), BF16),
            sds((4, slots // 2, 2 * COLS), BF16),
            sds((8, width), F32),
        ],
        scalars,
        vecs, own, received, gs, unit_one, rate_one, wo,
    )
    gcs = [gcx[0]] + [chips(gcx[rel], rel, "gcx") for rel in range(1, 4)]
    keep_mlp, send_mlp = run(
        partial(mlp_grads_body, shards),
        "mlp_grads",
        [sds((shards, rows, width), F32), sds((shards, rows, width), BF16)],
        scalars,
        low_one, low_two, far_one, far_two, gs_low, gs_other, gs_far_one, gs_far_two,
        act, act_far, low_keep, low_far,
    )
    *gcs, keep_mlp, send_mlp = lax.optimization_barrier((*gcs, keep_mlp, send_mlp))
    keep_out, send_out = run(
        out_grads_body,
        "out_grads",
        [sds((CHIPS, COLS, width // 2), F32), sds((CHIPS, COLS, width // 2), BF16)],
        scalars,
        *cxs,
        gf_low,
    )

    kind = BF16 if groups == 1 else F32

    def spread(low, name, late=()):
        if groups > 1:
            low = lax.psum(low, "ctx", axis_index_groups=sets).astype(BF16)
        here = [low] + [chips(low, rel, name) for rel in range(1, 4)]
        return here + [across(after(jnp.stack(here), *late), 1, name)]

    if groups == 1:
        dq, dk_own, dv_own, dkv = attend_back(gcs, pq, pk, vv, probs, slots, True)
    else:
        count = 4 * slots
        scatter = partial(lax.psum_scatter, axis_name="ctx", axis_index_groups=sets, tiled=True)
        dq, dk, dv = attend_back(gcs, pq, pk, vv, probs, slots, False)
        dk, dv = scatter(dk), scatter(dv)
        dk_own, dv_own = dk[:count], dv[:count]
        dkv = jnp.stack([dk[count:], dv[count:]]).astype(BF16)
    mlp_parts = run(
        partial(fan_body, shards),
        "fan_mlp",
        [sds((rows, width), F32)] + [sds((rows, width), BF16)] * (shards - 1),
        scalars,
        keep_mlp,
        across(send_mlp, 1, "gm"),
    )
    dkv, *mlp_parts = lax.optimization_barrier((dkv, *mlp_parts))
    mlp_recs = [turn(value, d + 1, "gm") for d, value in enumerate(mlp_parts[1:])]
    dkv_rec, keep_out, send_out = lax.optimization_barrier(
        (across(dkv, 1, "dkv"), keep_out, send_out)
    )
    own, send, keep_w, send_w = run(
        partial(qkv_grads_body, shards),
        "qkv_grads",
        [
            sds((slots, width), F32),
            sds((3, slots, width), BF16),
            sds((shards, main + small_rows, WIDE), F32),
            sds((shards, main, WIDE), BF16),
        ],
        scalars,
        meta, dq, dk_own, dv_own, dkv_rec, wall, sums_one, sums_two, sums_up, own_x,
        scratch=[pltpu.VMEM((2, 4 * slots, 2 * WIDE), BF16)],
    )
    qkv_parts = run(
        partial(qkv_fan_body, shards),
        "fan_qkv",
        [sds((main + small_rows, WIDE), F32)]
        + [sds((main + small_rows, WIDE), BF16)] * (shards - 1),
        scalars,
        keep_w,
        across(send_w, 1, "gq"),
    )
    qkv_recs = [turn(value, d + 1, "gq") for d, value in enumerate(qkv_parts[1:])]

    out_parts = run(
        out_fan_body,
        "fan_out",
        [sds((CHIPS, quarter, width // 2), F32)] + [sds((CHIPS, quarter, width // 2), BF16)] * 3,
        scalars,
        keep_out,
        across(send_out, 1, "go"),
    )
    out_recs = [chips(after(out_parts[rel], qkv_parts), rel, "go") for rel in range(1, 4)]
    out_shards = run(
        partial(out_shards_body, shards),
        "shards_out",
        [sds((quarter, width // 2), F32)] + [sds((quarter, width // 2), BF16)] * (shards - 1),
        scalars,
        out_parts[0],
        *out_recs,
    )
    out_recs = [turn(value, d + 1, "go") for d, value in enumerate(out_shards[1:])]

    mlp_recs = after(mlp_recs, qkv_parts)
    low = run(
        gather_sum_body, "sum_mlp", sds((rows, width), kind), scalars, mlp_parts[0], *mlp_recs
    )
    done_mlp = spread(low, "gm")
    input_grad = run(
        input_grad_body,
        "input_grad",
        sds((slots, width), F32),
        scalars,
        gf,
        own,
        *[chips(send[rel - 1], rel, "ig") for rel in range(1, 4)],
    )
    ug, dg = run(
        place_mlp_body,
        "place_mlp",
        [sds((rows, ff), F32), sds((part, width), F32)],
        scalars,
        *done_mlp,
        scratch=[pltpu.VMEM((CORES, CHIPS, rows, width), BF16)],
    )
    size = main + small_rows + quarter
    qkv_recs, out_recs = after((qkv_recs, out_recs), input_grad)
    low = run(
        partial(two_sums_body, shards),
        "sum_qkv",
        sds((size, WIDE), kind),
        scalars,
        qkv_parts[0], *qkv_recs, out_shards[0], *out_recs,
    )
    done_qkv = spread(low, "gq", (ug, dg))

    vec = sds((rows,), F32)
    qg, kg, vg, og, qbg, kbg, vbg, obg, g1g, b1g, dbg, g2g, b2g, ubg = run(
        place_qkv_body,
        "place_qkv",
        [
            sds((4, rows, width), F32), sds((rows, width), F32), sds((rows, width), F32),
            sds((rows, width), F32), sds((4, rows), F32), vec, vec, vec, vec, vec, vec, vec, vec,
            sds((4 * rows,), F32),
        ],
        scalars,
        *done_qkv,
        scratch=[pltpu.VMEM((CORES, CHIPS, size, WIDE), BF16)],
    )
    return (
        output[None], input_grad[None], qg, qbg, kg, kbg, vg, vbg, og, obg,
        g1g, b1g, ug, ubg, dg, dbg, g2g, b2g,
    )


def solution(mesh):
    vec, mat = P("shard"), P("shard", None)
    tokens = P("shard", "ctx", None)
    placed = (
        tokens, vec, mat, P(None, "shard", None), P(None, "shard"), mat, vec, mat, vec, mat,
        vec, vec, vec, mat, vec, mat, vec, vec, vec, tokens,
    )
    result = (
        tokens, tokens, P(None, "shard", None), P(None, "shard"), mat, vec, mat, vec, mat, vec,
        vec, vec, mat, vec, mat, vec, vec, vec,
    )
    return jax.shard_map(
        partial(local, mesh.shape["shard"], mesh.shape["ctx"]),
        mesh=mesh,
        in_specs=placed,
        out_specs=result,
        check_vma=False,
    )
```

time: 335 us -> 275 us (0.82)
  local copies, waits for them, and re-layouts: 47.3 us -> 2.79 us
  blocking collectives: 0 us -> 11.1 us
  Pallas kernels: 65.1 us -> 56.6 us
  starting transfers between devices: 89.6 us -> 82.6 us
  other arithmetic: 5.88 us -> 0.41 us
  waiting for transfers between devices: 124 us -> 119 us
    unnamed x136 -> x18, local copies, waits for them, and re-layouts: 27.7 us -> 1.93 us
    all_gather x0 -> x1, blocking collectives: none -> 11.1 us  [local(): own_x = lax.all_gather(after(hid, mlp_one), 'ctx', axis_index_groups=planes)]
    ppermute x71 -> x49, waiting for transfers between devices: 78.6 us -> 71.4 us  [across(): return lax.ppermute(value, 'ctx', [(i, i ^ mask) for i in range(lanes)])]
    slice x17 -> x0, local copies, waits for them, and re-layouts: 6.31 us -> none  [the longest x1 1.19 us: local(): dv[:count]]
    concatenate x4 -> x1, local copies, waits for them, and re-layouts: 6.21 us -> 0.03 us  [local(): jnp.concatenate([lax.dynamic_slice_in_dim(kinds, b, 1, 0) for b in blocks...]
    pallas_call x15 -> x22, Pallas kernels: 49.9 us -> 45.2 us  [run(): pl.pallas_call(body, out_shape=outs, in_specs=[SMEM] + [VMEM] * len(array...]
    add x11 -> x0, other arithmetic: 4.41 us -> none  [the longest x1 3.69 us: local(): both = keep_mlp + across(send_mlp, 1).astype(F32)]
    ppermute x2 -> x0, starting transfers between devices: 4.19 us -> none  [local(): lax.ppermute(small, 'shard', [(i, i ^ step) for i in range(shards)])]
  transfers between devices with their start and end apart: 94 -> 64, of which waited for: 31 -> 25; matrix products, arithmetic and copies ran while one was open for 5% -> 0% of each run, Pallas kernels for 13% -> 13%
where the time goes in v2:
time: 275 us; the launch traced here: 274 us
  waiting for transfers between devices  119 us (43%)
  starting transfers between devices  82.6 us (30%)
  Pallas kernels  56.6 us (21%)
  blocking collectives  11.1 us (4%)
  local copies, waits for them, and re-layouts  2.79 us (1%)
    ppermute x49, waiting for transfers between devices, across(): return lax.ppermute(value, 'ctx', [(i, i ^ mask) for i in range(lanes)])  71.4 us
    ppermute x15, waiting for transfers between devices, turn(): lax.ppermute(value, 'shard', [(i, (i + shift) % shards) for i in range(sh...  47.5 us
    pallas_call x22, Pallas kernels, run(): pl.pallas_call(body, out_shape=outs, in_specs=[SMEM] + [VMEM] * len(array...  45.2 us
    ppermute x49, starting transfers between devices, across(): return lax.ppermute(value, 'ctx', [(i, i ^ mask) for i in range(lanes)])  42.5 us
    ppermute x15, starting transfers between devices, turn(): lax.ppermute(value, 'shard', [(i, (i + shift) % shards) for i in range(sh...  40.1 us
    all_gather x1, blocking collectives, local(): own_x = lax.all_gather(after(hid, mlp_one), 'ctx', axis_index_groups=planes)  11.1 us
    pallas_call x1, Pallas kernels, attend_back(): pl.pallas_call(partial(attend_back_body, step, split), grid=(LOCAL_HEADS,...  5.84 us
  transfers between devices with their start and end apart: 64, of which 25 were waited for; matrix products, arithmetic and copies ran while one was open for 0% of the time, Pallas kernels for 13%

profile of v2, /device:TPU:0, one launch (start us, length us, event | category | flops | bytes accessed | tf_op | source)
XLA Modules:
  0.0 274.3 jit_solution(16577136962481612784)
XLA Ops:
  4.1 5.1 %collective-permute-start.3 = (bf16[392,384]{1,0:T(8,128)(2,1)}, bf16[392,384]{1,0:T(8,128)(2,1)}, u32[]{:S(2)}, u32[]{:S(2)}) collective-permute-start(bf16[392,384]{1,0:T(8,128)(2,1)} %get-tuple-element.143.mine), channel_id=1, source_target_pairs={{0,24},{8,0},{16,8},{24,16},{1,25},{9,1},{17,9},{25,17},{2,26},{10... | collective-permute-start | bytes 903176 | tf_op jit(solution)/shard_map/qkvw_z3/ppermute | solution.py:786
  14.5 11.1 %all-gather = bf16[512,768]{1,0:T(8,128)(2,1)S(1)} all-gather(bf16[128,768]{1,0:T(8,128)(2,1)S(1)} %bitcast.64), channel_id=2, replica_groups={{0,2,4,6},{1,3,5,7},{8,10,12,14},{9,11,13,15},{16,18,20,22},{17,19,21,2..., dimensions={0}, use_global_device_ids=true | all-gather | bytes 983040 | tf_op jit(solution)/shard_map/all_gather | solution.py:824
  26.9 9.3 %collective-permute-done.2.refs_1_ = bf16[392,384]{1,0:T(8,128)(2,1)} collective-permute-done((bf16[392,384]{1,0:T(8,128)(2,1)}, bf16[392,384]{1,0:T(8,128)(2,1)}, u32[]{:S(2)}, u32[]{:S(2)}) %collective-permute-start.2) | collective-permute-done | bytes 301088 | tf_op jit(solution)/shard_map/qkvw_z2/ppermute | solution.py:786
  36.4 7.8 %collective-permute-start.15 = (bf16[192,768]{1,0:T(8,128)(2,1)}, bf16[192,768]{1,0:T(8,128)(2,1)S(1)}, u32[]{:S(2)}, u32[]{:S(2)}) collective-permute-start(bf16[192,768]{1,0:T(8,128)(2,1)} %prep_mlp.1), channel_id=1, source_target_pairs={{0,16},{8,24},{16,0},{24,8},{1,17},{9,25},{17,1},{25,9},{2,18},{10... | collective-permute-start | bytes 884744 | tf_op jit(solution)/shard_map/mlpw_z2/ppermute | solution.py:786
  48.0 4.7 %qkv.1 = (bf16[2,768,768]{2,1,0:T(8,128)(2,1)S(1)}, bf16[512,384]{1,0:T(8,128)(2,1)S(1)}, bf16[1024,384]{1,0:T(8,128)(2,1)S(1)}, bf16[1024,384]{1,0:T(8,128)(2,1...) custom-call(s32[6]{0:T(128)S(1)} %copy-done.5, ...), custom_call_target="tpu_custom_call" | custom-call | flops 1 | bytes 3000000 | tf_op jit(solution)/shard_map/qkv/pallas_call | solution.py:51
  52.8 5.5 %attend.1 = (bf16[3,512,1024]{2,1,0:T(8,128)(2,1)S(1)}, bf16[4,64,384]{2,1,0:T(8,128)(2,1)S(1)}) custom-call(bf16[512,384]{1,0:T(8,128)(2,1)S(1)} %get-tuple-element.148.pq, bf16[1024,384]{1,0:T(8,128)(2,1)S(1)} %get-tuple-element.149.pk, bf16[1024,384]{1,0:T(8,128)(2,1)S(1)} %get-tuple-element.150.vv, f32[1,1024]{1,0:T(1,128)S(1)} %bitcast.67), custom_call_target="tpu_custom_call" | custom-call | flops 1 | bytes 16500000 | tf_op jit(solution)/shard_map/attend/pallas_call | solution.py:290
  58.3 5.3 %collective-permute-done.15.refs_1_ = bf16[192,768]{1,0:T(8,128)(2,1)S(1)} collective-permute-done((bf16[192,768]{1,0:T(8,128)(2,1)}, bf16[192,768]{1,0:T(8,128)(2,1)S(1)}, u32[]{:S(2)}, u32[]{:S(2)}) %collective-permute-start.15) | collective-permute-done | bytes 294944 | tf_op jit(solution)/shard_map/mlpw_z2/ppermute | solution.py:786
  72.2 7.7 %collective-permute-done.8.cx2 = bf16[64,384]{1,0:T(8,128)(2,1)S(1)} collective-permute-done((bf16[64,384]{1,0:T(8,128)(2,1)S(1)}, bf16[64,384]{1,0:T(8,128)(2,1)S(1)}, u32[]{:S(2)}, u32[]{:S(2)}) %collective-permute-start.8) | collective-permute-done | bytes 49184 | tf_op jit(solution)/shard_map/cx_4/ppermute | solution.py:779
  82.4 7.3 %collective-permute-done.18.refs_4_ = bf16[192,768]{1,0:T(8,128)(2,1)S(1)} collective-permute-done((bf16[192,768]{1,0:T(8,128)(2,1)S(1)}, bf16[192,768]{1,0:T(8,128)(2,1)S(1)}, u32[]{:S(2)}, u32[]{:S(2)}) %collective-permute-start.18) | collective-permute-done | bytes 294944 | tf_op jit(solution)/shard_map/mlpw_4/ppermute | solution.py:779
  89.7 5.0 %collective-permute-done.19.refs_5_ = bf16[192,768]{1,0:T(8,128)(2,1)S(1)} collective-permute-done((bf16[192,768]{1,0:T(8,128)(2,1)}, bf16[192,768]{1,0:T(8,128)(2,1)S(1)}, u32[]{:S(2)}, u32[]{:S(2)}) %collective-permute-start.19) | collective-permute-done | bytes 294944 | tf_op jit(solution)/shard_map/mlpw_4/ppermute | solution.py:779
  119.6 4.7 %collective-permute-done.29.g2 = bf16[128,768]{1,0:T(8,128)(2,1)S(1)} collective-permute-done((bf16[128,768]{1,0:T(8,128)(2,1)S(1)}, bf16[128,768]{1,0:T(8,128)(2,1)S(1)}, u32[]{:S(2)}, u32[]{:S(2)}) %collective-permute-start.29) | collective-permute-done | bytes 196640 | tf_op jit(solution)/shard_map/mlpy_g1_4/ppermute | solution.py:779
  145.4 5.8 %attend_back.1 = (f32[512,384]{1,0:T(8,128)S(1)}, f32[512,384]{1,0:T(8,128)S(1)}, f32[512,384]{1,0:T(8,128)S(1)}, bf16[2,512,384]{2,1,0:T(8,128)(2,1)S(1)}) custom-call(bf16[64,384]{1,0:T(8,128)(2,1)S(1)} %get-tuple-element.193.gc0, bf16[64,384]{1,0:T(8,128)(2,1)S(1)} %collective-permute-done.33.gc1, bf16[64,384]{1,0:T(8,128)(2,1)S(1)} %collective-permute-done.34.gc2, ...), custom_call_target="tpu_custom_call" | custom-call | flops 1 | bytes 18000000 | tf_op jit(solution)/shard_map/attend_back/pallas_call | solution.py:375
  154.9 5.1 %qkv_grads.1 = (f32[128,768]{1,0:T(8,128)S(1)}, bf16[3,128,768]{2,1,0:T(8,128)(2,1)S(1)}, f32[4,296,384]{2,1,0:T(8,128)S(1)}, bf16[4,288,384]{2,1,0:T(8,128)(2,1)S(1)}) custom-call(s32[6]{0:T(128)S(1)} %copy-done.5, f32[16,128]{1,0:T(8,128)S(1)} %add_convert_fusion.meta, f32[512,384]{1,0:T(8,128)S(1)} %get-tuple-element.198.dq, ...), custom_call_target="tpu_custom_call" | custom-call | flops 1 | bytes 15000000 | tf_op jit(solution)/shard_map/qkv_grads/pallas_call | solution.py:51
  160.1 3.7 %collective-permute-start.58 = (bf16[192,768]{1,0:T(8,128)(2,1)S(1)}, bf16[192,768]{1,0:T(8,128)(2,1)S(1)}, u32[]{:S(2)}, u32[]{:S(2)}) collective-permute-start(bf16[192,768]{1,0:T(8,128)(2,1)S(1)} %get-tuple-element.247), channel_id=1, source_target_pairs={{0,24},{8,0},{16,8},{24,16},{1,25},{9,1},{17,9},{25,17},{2,26},{10... | collective-permute-start | bytes 884744 | tf_op jit(solution)/shard_map/gm_z3/ppermute | solution.py:786
  164.6 7.3 %collective-permute-done.56.refs_0_ = bf16[192,768]{1,0:T(8,128)(2,1)S(1)} collective-permute-done((bf16[192,768]{1,0:T(8,128)(2,1)S(1)}, bf16[192,768]{1,0:T(8,128)(2,1)S(1)}, u32[]{:S(2)}, u32[]{:S(2)}) %collective-permute-start.56) | collective-permute-done | bytes 294944 | tf_op jit(solution)/shard_map/gm_z1/ppermute | solution.py:786
  171.9 11.7 %collective-permute-done.57.refs_1_ = bf16[192,768]{1,0:T(8,128)(2,1)S(1)} collective-permute-done((bf16[192,768]{1,0:T(8,128)(2,1)S(1)}, bf16[192,768]{1,0:T(8,128)(2,1)S(1)}, u32[]{:S(2)}, u32[]{:S(2)}) %collective-permute-start.57) | collective-permute-done | bytes 294944 | tf_op jit(solution)/shard_map/gm_z2/ppermute | solution.py:786
  187.8 7.3 %collective-permute-done.61.p3 = bf16[192,768]{1,0:T(8,128)(2,1)S(1)} collective-permute-done((bf16[192,768]{1,0:T(8,128)(2,1)S(1)}, bf16[192,768]{1,0:T(8,128)(2,1)S(1)}, u32[]{:S(2)}, u32[]{:S(2)}) %collective-permute-start.61) | collective-permute-done | bytes 294944 | tf_op jit(solution)/shard_map/gm_6/ppermute | solution.py:779
  195.2 4.2 %collective-permute-done.60.p2 = bf16[192,768]{1,0:T(8,128)(2,1)S(1)} collective-permute-done((bf16[192,768]{1,0:T(8,128)(2,1)S(1)}, bf16[192,768]{1,0:T(8,128)(2,1)S(1)}, u32[]{:S(2)}, u32[]{:S(2)}) %collective-permute-start.60) | collective-permute-done | bytes 294944 | tf_op jit(solution)/shard_map/gm_4/ppermute | solution.py:779
  210.2 5.2 %collective-permute-done.40.r2 = bf16[128,768]{1,0:T(8,128)(2,1)S(1)} collective-permute-done((bf16[128,768]{1,0:T(8,128)(2,1)S(1)}, bf16[128,768]{1,0:T(8,128)(2,1)S(1)}, u32[]{:S(2)}, u32[]{:S(2)}) %collective-permute-start.40) | collective-permute-done | bytes 196640 | tf_op jit(solution)/shard_map/ig_4/ppermute | solution.py:779
  216.8 6.9 %collective-permute-start.43 = (bf16[296,384]{1,0:T(8,128)(2,1)S(1)}, bf16[296,384]{1,0:T(8,128)(2,1)S(1)}, u32[]{:S(2)}, u32[]{:S(2)}) collective-permute-start(bf16[296,384]{1,0:T(8,128)(2,1)S(1)} %get-tuple-element.222), channel_id=1, source_target_pairs={{0,8},{8,16},{16,24},{24,0},{1,9},{9,17},{17,25},{25,1},{2,10},{10... | collective-permute-start | bytes 681992 | tf_op jit(solution)/shard_map/gq_z1/ppermute | solution.py:786
  229.1 9.9 %collective-permute-done.50.refs_5_ = bf16[48,384]{1,0:T(8,128)(2,1)S(1)} collective-permute-done((bf16[48,384]{1,0:T(8,128)(2,1)S(1)}, bf16[48,384]{1,0:T(8,128)(2,1)S(1)}, u32[]{:S(2)}, u32[]{:S(2)}) %collective-permute-start.50) | collective-permute-done | bytes 36896 | tf_op jit(solution)/shard_map/go_z1/ppermute | solution.py:786
  239.0 7.3 %collective-permute-start.51 = (bf16[48,384]{1,0:T(8,128)(2,1)S(1)}, bf16[48,384]{1,0:T(8,128)(2,1)S(1)}, u32[]{:S(2)}, u32[]{:S(2)}) collective-permute-start(bf16[48,384]{1,0:T(8,128)(2,1)S(1)} %get-tuple-element.235), channel_id=1, source_target_pairs={{0,16},{8,24},{16,0},{24,8},{1,17},{9,25},{17,1},{25,9},{2,18},{10... | collective-permute-start | bytes 110600 | tf_op jit(solution)/shard_map/go_z2/ppermute | solution.py:786
  256.5 5.1 %collective-permute-done.55.p3 = bf16[344,384]{1,0:T(8,128)(2,1)S(1)} collective-permute-done((bf16[344,384]{1,0:T(8,128)(2,1)S(1)}, bf16[344,384]{1,0:T(8,128)(2,1)S(1)}, u32[]{:S(2)}, u32[]{:S(2)}) %collective-permute-start.55) | collective-permute-done | bytes 264224 | tf_op jit(solution)/shard_map/gq_6/ppermute | solution.py:779
  270.4 3.8 %place_qkv.1 = (f32[4,192,768]{2,1,0:T(8,128)}, f32[192,768]{1,0:T(8,128)}, f32[192,768]{1,0:T(8,128)}, f32[192,768]{1,0:T(8,128)}, f32[4,192]{1,0:T(4,128)}, /*...) custom-call(s32[6]{0:T(128)S(1)} %copy-done.5, ...), custom_call_target="tpu_custom_call" | custom-call | flops 1 | bytes 10500000 | tf_op jit(solution)/shard_map/place_qkv/pallas_call | solution.py:51
  (162 shorter events, 115.5 us)
Async XLA Ops:
  4.1 22.4 %collective-permute-start.3 = (bf16[392,384]{1,0:T(8,128)(2,1)}, bf16[392,384]{1,0:T(8,128)(2,1)}, u32[]{:S(2)}, u32[]{:S(2)}) collective-permute-start(bf16[392,384]{1,0:T(8,128)(2,1)} %get-tuple-element.143.mine), channel_id=1, source_target_pairs={{0,24},{8,0},{16,8},{24,16},{1,25},{9,1},{17,9},{25,17},{2,26},{10... | collective-permute-start | bytes 903176 | tf_op jit(solution)/shard_map/qkvw_z3/ppermute | solution.py:786
  9.2 27.1 %collective-permute-start.2 = (bf16[392,384]{1,0:T(8,128)(2,1)}, bf16[392,384]{1,0:T(8,128)(2,1)}, u32[]{:S(2)}, u32[]{:S(2)}) collective-permute-start(bf16[392,384]{1,0:T(8,128)(2,1)} %get-tuple-element.143.mine), channel_id=1, source_target_pairs={{0,16},{8,24},{16,0},{24,8},{1,17},{9,25},{17,1},{25,9},{2,18},{10... | collective-permute-start | bytes 903176 | tf_op jit(solution)/shard_map/qkvw_z2/ppermute | solution.py:786
  9.2 27.1 %collective-permute-start.1 = (bf16[392,384]{1,0:T(8,128)(2,1)}, bf16[392,384]{1,0:T(8,128)(2,1)}, u32[]{:S(2)}, u32[]{:S(2)}) collective-permute-start(bf16[392,384]{1,0:T(8,128)(2,1)} %get-tuple-element.143.mine), channel_id=1, source_target_pairs={{0,8},{8,16},{16,24},{24,0},{1,9},{9,17},{17,25},{25,1},{2,10},{10... | collective-permute-start | bytes 903176 | tf_op jit(solution)/shard_map/qkvw_z1/ppermute | solution.py:786
  11.7 46.6 %collective-permute-start.16 = (bf16[192,768]{1,0:T(8,128)(2,1)}, bf16[192,768]{1,0:T(8,128)(2,1)}, u32[]{:S(2)}, u32[]{:S(2)}) collective-permute-start(bf16[192,768]{1,0:T(8,128)(2,1)} %prep_mlp.1), channel_id=1, source_target_pairs={{0,24},{8,0},{16,8},{24,16},{1,25},{9,1},{17,9},{25,17},{2,26},{10... | collective-permute-start | bytes 884744 | tf_op jit(solution)/shard_map/mlpw_z3/ppermute | solution.py:786
  25.6 20.5 %collective-permute-start = (bf16[4,128,768]{2,1,0:T(8,128)(2,1)S(1)}, bf16[4,128,768]{2,1,0:T(8,128)(2,1)}, u32[]{:S(2)}, u32[]{:S(2)}) collective-permute-start(bf16[4,128,768]{2,1,0:T(8,128)(2,1)S(1)} %bitcast.53), channel_id=1, source_target_pairs={{0,1},{1,0},{2,3},{3,2},{4,5},{5,4},{6,7},{7,6},{8,9},{9,8},{10,11... | collective-permute-start | bytes 2359304 | tf_op jit(solution)/shard_map/hid_1/ppermute | solution.py:779
  26.4 17.8 %collective-permute-start.6 = (bf16[392,384]{1,0:T(8,128)(2,1)}, bf16[392,384]{1,0:T(8,128)(2,1)}, u32[]{:S(2)}, u32[]{:S(2)}) collective-permute-start(bf16[392,384]{1,0:T(8,128)(2,1)} %collective-permute-done.3.refs_2_), channel_id=1, source_target_pairs={{0,1},{1,0},{2,3},{3,2},{4,5},{5,4},{6,7},{7,6},{8,9},{9,8},{10,11... | collective-permute-start | bytes 903176 | tf_op jit(solution)/shard_map/qkvw_1/ppermute | solution.py:779
  36.4 27.2 %collective-permute-start.15 = (bf16[192,768]{1,0:T(8,128)(2,1)}, bf16[192,768]{1,0:T(8,128)(2,1)S(1)}, u32[]{:S(2)}, u32[]{:S(2)}) collective-permute-start(bf16[192,768]{1,0:T(8,128)(2,1)} %prep_mlp.1), channel_id=1, source_target_pairs={{0,16},{8,24},{16,0},{24,8},{1,17},{9,25},{17,1},{25,9},{2,18},{10... | collective-permute-start | bytes 884744 | tf_op jit(solution)/shard_map/mlpw_z2/ppermute | solution.py:786
  44.2 19.3 %collective-permute-start.14 = (bf16[192,768]{1,0:T(8,128)(2,1)}, bf16[192,768]{1,0:T(8,128)(2,1)S(1)}, u32[]{:S(2)}, u32[]{:S(2)}) collective-permute-start(bf16[192,768]{1,0:T(8,128)(2,1)} %prep_mlp.1), channel_id=1, source_target_pairs={{0,8},{8,16},{16,24},{24,0},{1,9},{9,17},{17,25},{25,1},{2,10},{10... | collective-permute-start | bytes 884744 | tf_op jit(solution)/shard_map/mlpw_z1/ppermute | solution.py:786
  63.5 18.3 %collective-permute-start.20 = (bf16[192,768]{1,0:T(8,128)(2,1)S(1)}, bf16[192,768]{1,0:T(8,128)(2,1)S(1)}, u32[]{:S(2)}, u32[]{:S(2)}) collective-permute-start(bf16[192,768]{1,0:T(8,128)(2,1)S(1)} %collective-permute-done.14.refs_0_), channel_id=1, source_target_pairs={{0,1},{1,0},{2,3},{3,2},{4,5},{5,4},{6,7},{7,6},{8,9},{9,8},{10,11... | collective-permute-start | bytes 884744 | tf_op jit(solution)/shard_map/mlpw_1/ppermute | solution.py:779
  63.6 18.8 %collective-permute-start.17 = (bf16[192,768]{1,0:T(8,128)(2,1)S(1)}, bf16[192,768]{1,0:T(8,128)(2,1)S(1)}, u32[]{:S(2)}, u32[]{:S(2)}) collective-permute-start(bf16[192,768]{1,0:T(8,128)(2,1)S(1)} %collective-permute-done.14.refs_0_), channel_id=1, source_target_pairs={{0,4},{1,5},{2,6},{3,7},{4,0},{5,1},{6,2},{7,3},{8,12},{9,13},{10,... | collective-permute-start | bytes 884744 | tf_op jit(solution)/shard_map/mlpw_4/ppermute | solution.py:779
  65.1 16.8 %collective-permute-start.10 = (bf16[3,48,768]{2,1,0:T(8,128)(2,1)S(1)}, bf16[3,48,768]{2,1,0:T(8,128)(2,1)S(1)}, u32[]{:S(2)}, u32[]{:S(2)}) collective-permute-start(bf16[3,48,768]{2,1,0:T(8,128)(2,1)S(1)} %get-tuple-element.152.own), channel_id=1, source_target_pairs={{0,4},{1,5},{2,6},{3,7},{4,0},{5,1},{6,2},{7,3},{8,12},{9,13},{10,... | collective-permute-start | bytes 663560 | tf_op jit(solution)/shard_map/outw_4/ppermute | solution.py:779
  81.9 15.1 %collective-permute-start.21 = (bf16[192,768]{1,0:T(8,128)(2,1)S(1)}, bf16[192,768]{1,0:T(8,128)(2,1)S(1)}, u32[]{:S(2)}, u32[]{:S(2)}) collective-permute-start(bf16[192,768]{1,0:T(8,128)(2,1)S(1)} %collective-permute-done.15.refs_1_), channel_id=1, source_target_pairs={{0,1},{1,0},{2,3},{3,2},{4,5},{5,4},{6,7},{7,6},{8,9},{9,8},{10,11... | collective-permute-start | bytes 884744 | tf_op jit(solution)/shard_map/mlpw_1/ppermute | solution.py:779
  82.4 16.2 %collective-permute-start.22 = (bf16[192,768]{1,0:T(8,128)(2,1)}, bf16[192,768]{1,0:T(8,128)(2,1)S(1)}, u32[]{:S(2)}, u32[]{:S(2)}) collective-permute-start(bf16[192,768]{1,0:T(8,128)(2,1)} %collective-permute-done.16.refs_2_), channel_id=1, source_target_pairs={{0,1},{1,0},{2,3},{3,2},{4,5},{5,4},{6,7},{7,6},{8,9},{9,8},{10,11... | collective-permute-start | bytes 884744 | tf_op jit(solution)/shard_map/mlpw_1/ppermute | solution.py:779
  110.8 13.6 %collective-permute-start.30 = (bf16[256,768]{1,0:T(8,128)(2,1)S(1)}, bf16[256,768]{1,0:T(8,128)(2,1)S(1)}, u32[]{:S(2)}, u32[]{:S(2)}) collective-permute-start(bf16[256,768]{1,0:T(8,128)(2,1)S(1)} %get-tuple-element.173), channel_id=1, source_target_pairs={{0,4},{1,5},{2,6},{3,7},{4,0},{5,1},{6,2},{7,3},{8,12},{9,13},{10,... | collective-permute-start | bytes 1179656 | tf_op jit(solution)/shard_map/mlpy_a_4/ppermute | solution.py:779
  160.1 23.5 %collective-permute-start.57 = (bf16[192,768]{1,0:T(8,128)(2,1)S(1)}, bf16[192,768]{1,0:T(8,128)(2,1)S(1)}, u32[]{:S(2)}, u32[]{:S(2)}) collective-permute-start(bf16[192,768]{1,0:T(8,128)(2,1)S(1)} %get-tuple-element.246), channel_id=1, source_target_pairs={{0,16},{8,24},{16,0},{24,8},{1,17},{9,25},{17,1},{25,9},{2,18},{10... | collective-permute-start | bytes 884744 | tf_op jit(solution)/shard_map/gm_z2/ppermute | solution.py:786
  160.1 23.5 %collective-permute-start.58 = (bf16[192,768]{1,0:T(8,128)(2,1)S(1)}, bf16[192,768]{1,0:T(8,128)(2,1)S(1)}, u32[]{:S(2)}, u32[]{:S(2)}) collective-permute-start(bf16[192,768]{1,0:T(8,128)(2,1)S(1)} %get-tuple-element.247), channel_id=1, source_target_pairs={{0,24},{8,0},{16,8},{24,16},{1,25},{9,1},{17,9},{25,17},{2,26},{10... | collective-permute-start | bytes 884744 | tf_op jit(solution)/shard_map/gm_z3/ppermute | solution.py:786
  187.8 14.8 %collective-permute-start.46 = (bf16[4,192,384]{2,1,0:T(8,128)(2,1)S(1)}, bf16[4,192,384]{2,1,0:T(8,128)(2,1)S(1)}, u32[]{:S(2)}, u32[]{:S(2)}) collective-permute-start(bf16[4,192,384]{2,1,0:T(8,128)(2,1)S(1)} %get-tuple-element.226), channel_id=1, source_target_pairs={{0,1},{1,0},{2,3},{3,2},{4,5},{5,4},{6,7},{7,6},{8,9},{9,8},{10,11... | collective-permute-start | bytes 1769480 | tf_op jit(solution)/shard_map/go_1/ppermute | solution.py:779
  199.6 64.8 %collective-permute-start.62 = (bf16[4,192,768]{2,1,0:T(8,128)(2,1)S(1)}, bf16[4,192,768]{2,1,0:T(8,128)(2,1)S(1)}, u32[]{:S(2)}, u32[]{:S(2)}) collective-permute-start(bf16[4,192,768]{2,1,0:T(8,128)(2,1)S(1)} %pad_maximum_fusion), channel_id=1, source_target_pairs={{0,1},{1,0},{2,3},{3,2},{4,5},{5,4},{6,7},{7,6},{8,9},{9,8},{10,11... | collective-permute-start | bytes 3538952 | tf_op jit(solution)/shard_map/gm_1/ppermute | solution.py:779
  201.5 13.9 %collective-permute-start.40 = (bf16[128,768]{1,0:T(8,128)(2,1)S(1)}, bf16[128,768]{1,0:T(8,128)(2,1)S(1)}, u32[]{:S(2)}, u32[]{:S(2)}) collective-permute-start(bf16[128,768]{1,0:T(8,128)(2,1)S(1)} %get-tuple-element.269), channel_id=1, source_target_pairs={{0,4},{1,5},{2,6},{3,7},{4,0},{5,1},{6,2},{7,3},{8,12},{9,13},{10,... | collective-permute-start | bytes 589832 | tf_op jit(solution)/shard_map/ig_4/ppermute | solution.py:779
  204.0 19.6 %collective-permute-start.48 = (bf16[4,48,384]{2,1,0:T(8,128)(2,1)S(1)}, bf16[4,48,384]{2,1,0:T(8,128)(2,1)S(1)}, u32[]{:S(2)}, u32[]{:S(2)}) collective-permute-start(bf16[4,48,384]{2,1,0:T(8,128)(2,1)S(1)} %get-tuple-element.231), channel_id=1, source_target_pairs={{0,4},{1,5},{2,6},{3,7},{4,0},{5,1},{6,2},{7,3},{8,12},{9,13},{10,... | collective-permute-start | bytes 442376 | tf_op jit(solution)/shard_map/go_4/ppermute | solution.py:779
  208.5 15.9 %collective-permute-start.49 = (bf16[4,48,384]{2,1,0:T(8,128)(2,1)S(1)}, bf16[4,48,384]{2,1,0:T(8,128)(2,1)S(1)}, u32[]{:S(2)}, u32[]{:S(2)}) collective-permute-start(bf16[4,48,384]{2,1,0:T(8,128)(2,1)S(1)} %get-tuple-element.233), channel_id=1, source_target_pairs={{0,6},{1,7},{2,4},{3,5},{4,2},{5,3},{6,0},{7,1},{8,14},{9,15},{10,... | collective-permute-start | bytes 442376 | tf_op jit(solution)/shard_map/go_6/ppermute | solution.py:779
  216.8 35.5 %collective-permute-start.43 = (bf16[296,384]{1,0:T(8,128)(2,1)S(1)}, bf16[296,384]{1,0:T(8,128)(2,1)S(1)}, u32[]{:S(2)}, u32[]{:S(2)}) collective-permute-start(bf16[296,384]{1,0:T(8,128)(2,1)S(1)} %get-tuple-element.222), channel_id=1, source_target_pairs={{0,8},{8,16},{16,24},{24,0},{1,9},{9,17},{17,25},{25,1},{2,10},{10... | collective-permute-start | bytes 681992 | tf_op jit(solution)/shard_map/gq_z1/ppermute | solution.py:786
  223.7 28.6 %collective-permute-start.44 = (bf16[296,384]{1,0:T(8,128)(2,1)S(1)}, bf16[296,384]{1,0:T(8,128)(2,1)S(1)}, u32[]{:S(2)}, u32[]{:S(2)}) collective-permute-start(bf16[296,384]{1,0:T(8,128)(2,1)S(1)} %get-tuple-element.223), channel_id=1, source_target_pairs={{0,16},{8,24},{16,0},{24,8},{1,17},{9,25},{17,1},{25,9},{2,18},{10... | collective-permute-start | bytes 681992 | tf_op jit(solution)/shard_map/gq_z2/ppermute | solution.py:786
  224.4 27.9 %collective-permute-start.45 = (bf16[296,384]{1,0:T(8,128)(2,1)S(1)}, bf16[296,384]{1,0:T(8,128)(2,1)S(1)}, u32[]{:S(2)}, u32[]{:S(2)}) collective-permute-start(bf16[296,384]{1,0:T(8,128)(2,1)S(1)} %get-tuple-element.224), channel_id=1, source_target_pairs={{0,24},{8,0},{16,8},{24,16},{1,25},{9,1},{17,9},{25,17},{2,26},{10... | collective-permute-start | bytes 681992 | tf_op jit(solution)/shard_map/gq_z3/ppermute | solution.py:786
  (49 other events, 443.2 us)

commit v3 on v2

--- a/solution.py
+++ b/solution.py
@@ -60,7 +60,7 @@
     )(scalars, *arrays)
 
 
-SHARD, CHIP, CORE, SPOT, SIDE, TALL = range(6)
+SHARD, CHIP, CORE, SPOT, SIDE, TALL, PLACE = range(7)
 
 
 def prep_qkv_body(sc, qw, kw, vw, ow, qb, *refs):
@@ -76,7 +76,7 @@
     small = jnp.concatenate(lines, axis=0).astype(BF16)
     end = rows + half + small.shape[0]
     own[rows + half : end, :] = small
-    third = ow[pl.ds(pl.multiple_of(sc[SPOT] * (rows // 4), rows // 4), rows // 4), :]
+    third = ow[pl.ds(pl.multiple_of(sc[PLACE] * (rows // 4), rows // 4), rows // 4), :]
     own[end : end + rows // 4, :] = third[:, 0:WIDE]
     own[end + rows // 4 :, :] = third[:, WIDE:]
     for chip in range(CHIPS):
@@ -125,8 +125,8 @@
     wo[pl.ds(pl.multiple_of(sc[SHARD] * rows, rows), rows), :] = whole[...]
     for rel, ref in enumerate((own, other, own_far, other_far)):
         for shift in range(1, shards):
-            owner = lax.rem(sc[SHARD] + shards - shift, shards)
-            at = pl.multiple_of(owner * rows + (sc[SPOT] ^ rel) * small, small)
+            owner = sc[SHARD] ^ shift
+            at = pl.multiple_of(owner * rows + (sc[PLACE] ^ rel) * small, small)
             wo[pl.ds(at, small), :] = ref[shift - 1]
 
 
@@ -155,7 +155,7 @@
     for index, ref in enumerate(pieces):
         rel, shift = index // (shards - 1), index % (shards - 1) + 1
         spot = sc[SPOT] ^ (rel // 2 + rel % 2 * 2)
-        owner = lax.rem(sc[SHARD] + shards - shift, shards)
+        owner = sc[SHARD] ^ shift
         at = pl.multiple_of(owner * rows + spot * small, small)
         wup[pl.ds(at, small), 0:width] = ref[0:small, :]
         wup[pl.ds(at, small), width:] = ref[small : 2 * small, :]
@@ -202,7 +202,7 @@
                 end = ref.shape[0] - 2 * small
                 third[shift - 1, :, 0:WIDE] = ref[end : end + small, :]
                 third[shift - 1, :, WIDE:] = ref[end + small :, :]
-            owner = lax.rem(sc[SHARD] + shards - shift, shards)
+            owner = sc[SHARD] ^ shift
             at = pl.multiple_of(owner * rows, half)
             wall[group, pl.ds(at, rows), 0:WIDE] = ref[0:rows, :]
             if which == 0:
@@ -240,7 +240,7 @@
     lane = lax.broadcasted_iota(jnp.int32, (1, WIDE), 1)
     left = (lane % PAIR) < HEAD
     for block in range(8):
-        tokens = (own_x if block < 4 else other_x)[sc[CHIP] ^ (block % 4)]
+        tokens = (own_x if block < 4 else other_x)[block % 4]
         word = flags[:, block : block + 1] > 0
         at = slice(block * slots, (block + 1) * slots)
         if block < 4:
@@ -511,12 +511,38 @@
             send[at] = up.astype(BF16)
 
 
-def fan_body(shards, sc, keep, received, own, *sends):
-    at = sc[SHARD]
-    own[...] = keep[at] + received[at].astype(F32)
-    for shift in range(1, shards):
-        at = lax.rem(sc[SHARD] + shift, shards)
-        sends[shift - 1][...] = (keep[at] + received[at].astype(F32)).astype(BF16)
+def fan_body(shards, sc, keep, received, *outs):
+    for shift in range(shards):
+        at = sc[SHARD] ^ shift
+        value = keep[at] + received[at].astype(F32)
+        outs[shift][...] = value.astype(outs[shift].dtype)
+
+
+def relay_body(sc, value, received, out):
+    out[...] = (value[...] + received[...].astype(F32)).astype(BF16)
+
+
+def relay_second_body(sc, value, received, out):
+    out[...] = (value[...] + received[1].astype(F32)).astype(BF16)
+
+
+def qkv_fan_body(shards, sc, keep, received, planes, *outs):
+    main = received.shape[1]
+    small, half = planes.shape[1:]
+    end = keep.shape[1]
+    for shift in range(shards):
+        at = sc[SHARD] ^ shift
+        ref = outs[shift]
+        ref[0:main, :] = (keep[at, 0:main, :] + received[at].astype(F32)).astype(ref.dtype)
+        ref[main:end, :] = keep[at, main:, :].astype(ref.dtype)
+        ref[end:, :] = planes[at].astype(ref.dtype)
+
+
+def gather_sum_body(sc, own, *refs):
+    acc = own[...]
+    for ref in refs[:-1]:
+        acc += ref[...].astype(F32)
+    refs[-1][...] = acc.astype(refs[-1].dtype)
 
 
 def out_fan_body(sc, keep, received, own, *sends):
@@ -530,45 +556,12 @@
             sends[rel - 1][...] = value.astype(BF16)
 
 
-def qkv_fan_body(shards, sc, keep, received, own, *sends):
-    main = received.shape[1]
-    for shift in range(shards):
-        at = lax.rem(sc[SHARD] + shift, shards)
-        ref = own if shift == 0 else sends[shift - 1]
-        ref[0:main, :] = (keep[at, 0:main, :] + received[at].astype(F32)).astype(ref.dtype)
-        ref[main:, :] = keep[at, main:, :].astype(ref.dtype)
-
-
-def out_shards_body(shards, sc, own_all, r1, r2, r3, own, *sends):
-    for shift in range(shards):
-        at = lax.rem(sc[SHARD] + shift, shards)
-        value = own_all[at] + r1[at].astype(F32) + r2[at].astype(F32) + r3[at].astype(F32)
-        ref = own if shift == 0 else sends[shift - 1]
-        ref[...] = value.astype(ref.dtype)
-
-
-def gather_sum_body(sc, own, *refs):
-    acc = own[...]
-    for ref in refs[:-1]:
-        acc += ref[...].astype(F32)
-    refs[-1][...] = acc.astype(refs[-1].dtype)
-
-
-def two_sums_body(count, sc, *refs):
-    out = refs[-1]
-    at = 0
-    for part in (refs[:count], refs[count:-1]):
-        acc = part[0][...]
-        for ref in part[1:]:
-            acc += ref[...].astype(F32)
-        out[at : at + acc.shape[0], :] = acc.astype(out.dtype)
-        at += acc.shape[0]
-
-
-def input_grad_body(sc, base, own, r1, r2, r3, out):
-    out[...] = (
-        base[...] + own[...] + r1[...].astype(F32) + r2[...].astype(F32) + r3[...].astype(F32)
-    )
+def plane_sum_body(sc, own, r1, r2, r3, out):
+    out[...] = own[...] + r1[...].astype(F32) + r2[...].astype(F32) + r3[...].astype(F32)
+
+
+def input_grad_body(sc, base, own, near, far, out):
+    out[...] = base[...] + own[...] + near[0].astype(F32) + far[...].astype(F32)
 
 
 def norm_one_back_body(
@@ -610,7 +603,7 @@
 
 def qkv_grads_body(
     shards, sc, meta, dq, dk_own, dv_own, dkv_rec, wall, sums_one, sums_two, sums_up,
-    x, own, send, keep_w, send_w, packed,
+    x, own, own_far, send, keep_w, send_w, packed,
 ):
     slots = x.shape[1]
     flags = meta[...].T
@@ -635,7 +628,7 @@
         packed[1, at, 0:WIDE] = parts[1].astype(BF16)
         packed[0, at, WIDE:] = parts[2].astype(BF16)
         packed[1, at, WIDE:] = parts[3].astype(BF16)
-    tokens = jnp.concatenate([x[sc[CHIP] ^ rel] for rel in range(4)], axis=0)
+    tokens = jnp.concatenate([x[rel] for rel in range(4)], axis=0)
     for group_rel, ref in enumerate((keep_w, send_w)):
         group = sc[CORE] ^ group_rel
         for at in range(shards):
@@ -656,8 +649,10 @@
         back = dot(packed[0, at, :], wall[0], 1, 1) + dot(packed[1, at, :], wall[1], 1, 1)
         if block == 0:
             own[...] = back
+        elif block == 2:
+            own_far[...] = back
         else:
-            send[block - 1] = back.astype(BF16)
+            send[block // 2] = back.astype(BF16)
     keys = split_pairs(acc[2])
     values = split_pairs(acc[3])
     heads = [
@@ -771,7 +766,7 @@
     core, chip, group = lane & 1, (lane >> 1) & 3, lane >> 3
     chip_x, chip_y = chip & 1, chip >> 1
     spot = chip_y * 2 + core
-    scalars = jnp.stack([shard, chip, core, spot, chip_x, chip_y]).astype(jnp.int32)
+    scalars = jnp.stack([shard, chip, core, spot, chip_x, chip_y, chip_x * 2 + core]).astype(jnp.int32)
     sets = [[g * 8 + i for g in range(groups)] for i in range(8)]
 
     def across(value, mask, name):
@@ -783,7 +778,19 @@
 
     def turn(value, shift, name):
         with jax.named_scope(f"{name}_z{shift}"):
-            return lax.ppermute(value, "shard", [(i, (i + shift) % shards) for i in range(shards)])
+            return lax.ppermute(value, "shard", [(i, i ^ shift) for i in range(shards)])
+
+    def collect(value, name):
+        far = turn(value, 2, name)
+        far, near = lax.optimization_barrier((far, turn(value, 1, name)))
+        return [near, far, turn(far, 1, name)]
+
+    def reduce(parts, name, *others):
+        _, near, far, last = parts
+        last = after(turn(last, 1, name), *others)
+        near = turn(near, 1, name)
+        far = run(relay_body, "relay", sds(far.shape, BF16), scalars, far, last)
+        return [near, turn(far, 2, name)], far
 
     def after(value, *others):
         return lax.optimization_barrier((value,) + others)[0]
@@ -809,21 +816,20 @@
         down_bias, norm2_gain, norm2_bias, up_bias,
         vmem=60,
     )
-    own_w = [turn(mine, d, "qkvw") for d in range(1, shards)]
+    own_w = collect(mine, "qkvw")
     quarter = rows // 4
     mlp_one = run(
         prep_mlp_body,
         "prep_mlp",
         sds((2 * quarter + side // 4, width), BF16),
         scalars,
-        lax.dynamic_slice_in_dim(up_weight, spot * quarter, quarter, 0),
+        after(lax.dynamic_slice_in_dim(up_weight, spot * quarter, quarter, 0), own_w[1]),
         lax.dynamic_slice_in_dim(down_weight, chip_x * side + spot * (side // 4), side // 4, 0),
     )
-    mlp_z = [turn(after(mlp_one, mine), d, "mlpw") for d in range(1, shards)]
-    planes = [[g * 8 + 2 * j + c for j in range(CHIPS)] for g in range(groups) for c in range(CORES)]
-    own_x = lax.all_gather(after(hid, mlp_one), "ctx", axis_index_groups=planes)
+    own_x = jnp.stack([hid] + [chips(hid, rel, "hid") for rel in range(1, 4)])
+    mlp_z = collect(mlp_one, "mlpw")
     other_x = across(own_x, 1, "hid")
-    other_w = [across(piece, 1, "qkvw") for piece in own_w]
+    other_w = [across(after(piece, other_x), 1, "qkvw") for piece in own_w]
 
     kinds = row_types.reshape(-1, slots)
     blocks = [group * 8 + (chip ^ rel) * 2 + (core ^ c) for c in range(CORES) for rel in range(4)]
@@ -850,14 +856,19 @@
         meta, mine, other_mine, own_x, other_x, *own_w, *other_w,
         scratch=[pltpu.VMEM((shards, small_rows, WIDE), F32)],
     )
-    out_far = across(out_own, 4, "outw")
+    out_far = chips(out_own, 1, "outw")
     valid = live.reshape(1, 8 * slots)
     if groups > 1:
         gather = partial(lax.all_gather, axis_name="ctx", axis_index_groups=sets, tiled=True)
         pk, vv = gather(pk, axis=0), gather(vv, axis=0)
         valid = gather(valid, axis=1)
-    probs, cx = attend(pq, pk, vv, valid, slots)
+    mlp_far = [across(piece, 4, "mlpw") for piece in mlp_z]
+    mlp_core = [across(piece, 1, "mlpw") for piece in mlp_z[:2]]
+    probs, cx = attend(after(pq, mlp_core), pk, vv, valid, slots)
+    cx = after(cx, out_far, mlp_far[0])
     cxs = [cx[0]] + [chips(cx[rel], rel, "cx") for rel in range(1, 4)]
+    mlp_core += [across(piece, 1, "mlpw") for piece in (mlp_z[2], mlp_far[0], mlp_far[1])]
+    cxs = after(cxs, mlp_core)
     *cxs, out_far = lax.optimization_barrier((*cxs, out_far))
     wo = run(
         partial(assemble_out_body, shards),
@@ -866,27 +877,26 @@
         scalars,
         out_weight, out_own, out_other, out_far, across(out_far, 1, "outw"),
     )
-    mlp_z = after(mlp_z, cx)
-    mlp_far = [across(piece, 4, "mlpw") for piece in mlp_z]
+    low_one, unit_one, rate_one = run(
+        norm_one_body,
+        "norm_one",
+        [sds((slots, width), BF16), sds((slots, width), F32), sds((slots, 128), F32)],
+        scalars,
+        vecs, *cxs, wo, hid,
+    )
+    low_two = chips(low_one, 1, "mlpx")
+    low_two, far_one = lax.optimization_barrier((low_two, across(low_one, 4, "mlpy_x1")))
+    far_two = chips(far_one, 1, "mlpy_x2")
     pieces = mlp_z + mlp_far
+    mlp_core.append(across(after(mlp_far[2], low_two), 1, "mlpw"))
     wup, wdn = run(
         partial(assemble_mlp_body, shards),
         "assemble_mlp",
         [sds((width, ff // 2), BF16), sds((ff // 2, width), BF16)],
         scalars,
-        up_weight, down_weight, *pieces, *[across(piece, 1, "mlpw") for piece in pieces],
-    )
-
-    low_one, unit_one, rate_one = run(
-        norm_one_body,
-        "norm_one",
-        [sds((slots, width), BF16), sds((slots, width), F32), sds((slots, 128), F32)],
-        scalars,
-        vecs, *cxs, wo, hid,
-    )
-    low_two = chips(low_one, 1, "mlpx")
-    low_two, far_one = lax.optimization_barrier((low_two, across(low_one, 4, "mlpy_x1")))
-    far_two = across(low_two, 4, "mlpy_x2")
+        up_weight, down_weight, *pieces, *mlp_core,
+    )
+
     act, act_send, slope, own, send = run(
         partial(mlp_body, 384),
         "mlp",
@@ -917,7 +927,7 @@
     gs_other, gs_far_one, act_far = lax.optimization_barrier(
         (chips(gs_low, 1, "mlpg"), across(gs_low, 4, "mlpy_g1"), act_far)
     )
-    gs_far_two = across(gs_other, 4, "mlpy_g2")
+    gs_far_two = chips(gs_far_one, 1, "mlpy_g2")
     low_keep, low_send, sums_up, own, send = run(
         partial(mlp_back_body, 384),
         "mlp_back",
@@ -952,16 +962,15 @@
         [sds((shards, rows, width), F32), sds((shards, rows, width), BF16)],
         scalars,
         low_one, low_two, far_one, far_two, gs_low, gs_other, gs_far_one, gs_far_two,
-        act, act_far, low_keep, low_far,
-    )
-    *gcs, keep_mlp, send_mlp = lax.optimization_barrier((*gcs, keep_mlp, send_mlp))
+        act, act_far, after(low_keep, gf_low), low_far,
+    )
     keep_out, send_out = run(
         out_grads_body,
         "out_grads",
         [sds((CHIPS, COLS, width // 2), F32), sds((CHIPS, COLS, width // 2), BF16)],
         scalars,
         *cxs,
-        gf_low,
+        after(gf_low, send_mlp),
     )
 
     kind = BF16 if groups == 1 else F32
@@ -972,6 +981,26 @@
         here = [low] + [chips(low, rel, name) for rel in range(1, 4)]
         return here + [across(after(jnp.stack(here), *late), 1, name)]
 
+    def fan(size):
+        return [sds(size, F32), sds(size, BF16), sds(size, F32), sds(size, BF16)]
+
+    mlp_parts = run(
+        partial(fan_body, shards),
+        "fan_mlp",
+        fan((rows, width)),
+        scalars,
+        keep_mlp,
+        across(send_mlp, 1, "gm"),
+    )
+    out_parts = run(
+        out_fan_body,
+        "fan_out",
+        [sds((CHIPS, quarter, width // 2), F32)] + [sds((CHIPS, quarter, width // 2), BF16)] * 3,
+        scalars,
+        keep_out,
+        across(send_out, 1, "go"),
+    )
+    gcs, _, (out_own, *out_sends) = lax.optimization_barrier((gcs, mlp_parts[1], out_parts))
     if groups == 1:
         dq, dk_own, dv_own, dkv = attend_back(gcs, pq, pk, vv, probs, slots, True)
     else:
@@ -981,25 +1010,22 @@
         dk, dv = scatter(dk), scatter(dv)
         dk_own, dv_own = dk[:count], dv[:count]
         dkv = jnp.stack([dk[count:], dv[count:]]).astype(BF16)
-    mlp_parts = run(
-        partial(fan_body, shards),
-        "fan_mlp",
-        [sds((rows, width), F32)] + [sds((rows, width), BF16)] * (shards - 1),
-        scalars,
-        keep_mlp,
-        across(send_mlp, 1, "gm"),
-    )
-    dkv, *mlp_parts = lax.optimization_barrier((dkv, *mlp_parts))
-    mlp_recs = [turn(value, d + 1, "gm") for d, value in enumerate(mlp_parts[1:])]
-    dkv_rec, keep_out, send_out = lax.optimization_barrier(
-        (across(dkv, 1, "dkv"), keep_out, send_out)
-    )
-    own, send, keep_w, send_w = run(
+    planes = run(
+        plane_sum_body,
+        "plane_out",
+        sds((shards, quarter, width // 2), F32),
+        scalars,
+        after(out_own, dq),
+        *[chips(out_sends[rel - 1], rel, "go") for rel in range(1, 4)],
+    )
+    dkv_rec = across(after(dkv, planes), 1, "dkv")
+    own, own_far, send, keep_w, send_w = run(
         partial(qkv_grads_body, shards),
         "qkv_grads",
         [
             sds((slots, width), F32),
-            sds((3, slots, width), BF16),
+            sds((slots, width), F32),
+            sds((2, slots, width), BF16),
             sds((shards, main + small_rows, WIDE), F32),
             sds((shards, main, WIDE), BF16),
         ],
@@ -1007,50 +1033,36 @@
         meta, dq, dk_own, dv_own, dkv_rec, wall, sums_one, sums_two, sums_up, own_x,
         scratch=[pltpu.VMEM((2, 4 * slots, 2 * WIDE), BF16)],
     )
+    mlp_recs, gm_far = reduce(mlp_parts, "gm", own)
+    size = main + small_rows + quarter
     qkv_parts = run(
         partial(qkv_fan_body, shards),
         "fan_qkv",
-        [sds((main + small_rows, WIDE), F32)]
-        + [sds((main + small_rows, WIDE), BF16)] * (shards - 1),
+        fan((size, WIDE)),
         scalars,
         keep_w,
-        across(send_w, 1, "gq"),
-    )
-    qkv_recs = [turn(value, d + 1, "gq") for d, value in enumerate(qkv_parts[1:])]
-
-    out_parts = run(
-        out_fan_body,
-        "fan_out",
-        [sds((CHIPS, quarter, width // 2), F32)] + [sds((CHIPS, quarter, width // 2), BF16)] * 3,
-        scalars,
-        keep_out,
-        across(send_out, 1, "go"),
-    )
-    out_recs = [chips(after(out_parts[rel], qkv_parts), rel, "go") for rel in range(1, 4)]
-    out_shards = run(
-        partial(out_shards_body, shards),
-        "shards_out",
-        [sds((quarter, width // 2), F32)] + [sds((quarter, width // 2), BF16)] * (shards - 1),
-        scalars,
-        out_parts[0],
-        *out_recs,
-    )
-    out_recs = [turn(value, d + 1, "go") for d, value in enumerate(out_shards[1:])]
-
-    mlp_recs = after(mlp_recs, qkv_parts)
-    low = run(
-        gather_sum_body, "sum_mlp", sds((rows, width), kind), scalars, mlp_parts[0], *mlp_recs
-    )
-    done_mlp = spread(low, "gm")
+        across(after(send_w, gm_far), 1, "gq"),
+        planes,
+    )
+    qkv_recs, gq_far = reduce(qkv_parts, "gq")
+
+    near = chips(send, 1, "ig")
+    far = run(
+        relay_second_body, "relay_ig", sds((slots, width), BF16), scalars, own_far, near
+    )
     input_grad = run(
         input_grad_body,
         "input_grad",
         sds((slots, width), F32),
         scalars,
-        gf,
-        own,
-        *[chips(send[rel - 1], rel, "ig") for rel in range(1, 4)],
-    )
+        gf, own, near, chips(far, 2, "ig"),
+    )
+
+    mlp_recs = after(mlp_recs, gq_far, far)
+    low = run(
+        gather_sum_body, "sum_mlp", sds((rows, width), kind), scalars, mlp_parts[0], *mlp_recs
+    )
+    done_mlp = spread(low, "gm", (input_grad, qkv_recs))
     ug, dg = run(
         place_mlp_body,
         "place_mlp",
@@ -1059,14 +1071,8 @@
         *done_mlp,
         scratch=[pltpu.VMEM((CORES, CHIPS, rows, width), BF16)],
     )
-    size = main + small_rows + quarter
-    qkv_recs, out_recs = after((qkv_recs, out_recs), input_grad)
     low = run(
-        partial(two_sums_body, shards),
-        "sum_qkv",
-        sds((size, WIDE), kind),
-        scalars,
-        qkv_parts[0], *qkv_recs, out_shards[0], *out_recs,
+        gather_sum_body, "sum_qkv", sds((size, WIDE), kind), scalars, qkv_parts[0], *qkv_recs
     )
     done_qkv = spread(low, "gq", (ug, dg))
 

time: 275 us -> 225 us (0.82)
  starting transfers between devices: 82.6 us -> 59.5 us
  waiting for transfers between devices: 119 us -> 99.6 us
  blocking collectives: 11.1 us -> 0 us
    ppermute x15 -> x12, starting transfers between devices: 40.1 us -> 18.1 us  [turn(): return lax.ppermute(value, 'shard', [(i, i ^ shift) for i in range(shards)])]
    all_gather x1 -> x0, blocking collectives: 11.1 us -> none  [local(): own_x = lax.all_gather(after(hid, mlp_one), 'ctx', axis_index_groups=planes)]
    ppermute x15 -> x12, waiting for transfers between devices: 47.5 us -> 36.6 us  [turn(): return lax.ppermute(value, 'shard', [(i, i ^ shift) for i in range(shards)])]
    ppermute x49 -> x51, waiting for transfers between devices: 71.4 us -> 63 us  [across(): return lax.ppermute(value, 'ctx', [(i, i ^ mask) for i in range(lanes)])]
    pallas_call x22 -> x25, Pallas kernels: 45.2 us -> 47.2 us  [run(): pl.pallas_call(body, out_shape=outs, in_specs=[SMEM] + [VMEM] * len(array...]
    ppermute x49 -> x51, starting transfers between devices: 42.5 us -> 41.4 us  [across(): return lax.ppermute(value, 'ctx', [(i, i ^ mask) for i in range(lanes)])]
  transfers between devices with their start and end apart: 64 -> 63, of which waited for: 25 -> 32; matrix products, arithmetic and copies ran while one was open for 0% -> 1% of each run, Pallas kernels for 13% -> 19%
where the time goes in v3:
time: 225 us; the launch traced here: 224 us
  waiting for transfers between devices  99.6 us (44%)
  starting transfers between devices  59.5 us (26%)
  Pallas kernels  58.5 us (26%)
  local copies, waits for them, and re-layouts  3.41 us (2%)
    ppermute x51, waiting for transfers between devices, across(): return lax.ppermute(value, 'ctx', [(i, i ^ mask) for i in range(lanes)])  63 us
    pallas_call x25, Pallas kernels, run(): pl.pallas_call(body, out_shape=outs, in_specs=[SMEM] + [VMEM] * len(array...  47.2 us
    ppermute x51, starting transfers between devices, across(): return lax.ppermute(value, 'ctx', [(i, i ^ mask) for i in range(lanes)])  41.4 us
    ppermute x12, waiting for transfers between devices, turn(): return lax.ppermute(value, 'shard', [(i, i ^ shift) for i in range(shards)])  36.6 us
    ppermute x12, starting transfers between devices, turn(): return lax.ppermute(value, 'shard', [(i, i ^ shift) for i in range(shards)])  18.1 us
    pallas_call x1, Pallas kernels, attend_back(): pl.pallas_call(partial(attend_back_body, step, split), grid=(LOCAL_HEADS,...  5.82 us
    pallas_call x1, Pallas kernels, attend(): pl.pallas_call(partial(attend_body, step), grid=(LOCAL_HEADS,), in_specs=...  5.47 us
  transfers between devices with their start and end apart: 63, of which 32 were waited for; matrix products, arithmetic and copies ran while one was open for 1% of the time, Pallas kernels for 19%

profile of v3, /device:TPU:0, one launch (start us, length us, event | category | flops | bytes accessed | tf_op | source)
XLA Modules:
  0.0 224.5 jit_solution(16864108316400178097)
XLA Ops:
  0.7 4.0 %collective-permute-start.2 = (bf16[128,768]{1,0:T(8,128)(2,1)}, bf16[128,768]{1,0:T(8,128)(2,1)S(1)}, u32[]{:S(2)}, u32[]{:S(2)}) collective-permute-start(bf16[128,768]{1,0:T(8,128)(2,1)} %bitcast.58), channel_id=1, source_target_pairs={{0,6},{1,7},{2,4},{3,5},{4,2},{5,3},{6,0},{7,1},{8,14},{9,15},{10,... | collective-permute-start | bytes 589832 | tf_op jit(solution)/shard_map/hid_6/ppermute | solution.py:774
  5.9 2.8 %prep_qkv.1 = (bf16[392,384]{1,0:T(8,128)(2,1)}, bf16[288,384]{1,0:T(8,128)(2,1)}) custom-call(s32[7]{0:T(128)} %stack.100.sc, bf16[4,192,768]{2,1,0:T(8,128)(2,1)} %qw.1, bf16[192,768]{1,0:T(8,128)(2,1)} %kw.1, bf16[192,768]{1,0:T(8,128)(2,1)} %vw.1, bf16[192,768]{1,0:T(8,128)(2,1)} %whole.1, bf16[4,192]{1,0:T(4,128)(2,1)} %qb.1, bf16[192]{0:T(256)(128)(2,1)} %refs_0_.1, ...), custom_call_target="tpu_custom_call" | custom-call | flops 1 | bytes 3000000 | tf_op jit(solution)/shard_map/prep_qkv/pallas_call | solution.py:51
  16.9 6.7 %collective-permute-done.5.refs_0_ = bf16[392,384]{1,0:T(8,128)(2,1)} collective-permute-done((bf16[392,384]{1,0:T(8,128)(2,1)}, bf16[392,384]{1,0:T(8,128)(2,1)}, u32[]{:S(2)}, u32[]{:S(2)}) %collective-permute-start.5) | collective-permute-done | bytes 301088 | tf_op jit(solution)/shard_map/qkvw_z1/ppermute | solution.py:781
  30.7 11.2 %collective-permute-done.6.refs_2_ = bf16[392,384]{1,0:T(8,128)(2,1)} collective-permute-done((bf16[392,384]{1,0:T(8,128)(2,1)}, bf16[392,384]{1,0:T(8,128)(2,1)}, u32[]{:S(2)}, u32[]{:S(2)}) %collective-permute-start.6) | collective-permute-done | bytes 301088 | tf_op jit(solution)/shard_map/qkvw_z1/ppermute | solution.py:781
  50.6 4.9 %qkv.1 = (bf16[2,768,768]{2,1,0:T(8,128)(2,1)S(1)}, bf16[512,384]{1,0:T(8,128)(2,1)S(1)}, bf16[1024,384]{1,0:T(8,128)(2,1)S(1)}, bf16[1024,384]{1,0:T(8,128)(2,1...) custom-call(s32[7]{0:T(128)S(1)} %copy-done.4, ...), custom_call_target="tpu_custom_call" | custom-call | flops 1 | bytes 3000000 | tf_op jit(solution)/shard_map/qkv/pallas_call | solution.py:51
  59.0 5.5 %attend.1 = (bf16[3,512,1024]{2,1,0:T(8,128)(2,1)S(1)}, bf16[4,64,384]{2,1,0:T(8,128)(2,1)S(1)}) custom-call(bf16[512,384]{1,0:T(8,128)(2,1)S(1)} %get-tuple-element.154.pq, bf16[1024,384]{1,0:T(8,128)(2,1)S(1)} %get-tuple-element.155.pk, bf16[1024,384]{1,0:T(8,128)(2,1)S(1)} %get-tuple-element.156.vv, f32[1,1024]{1,0:T(1,128)S(1)} %bitcast.63), custom_call_target="tpu_custom_call" | custom-call | flops 1 | bytes 16500000 | tf_op jit(solution)/shard_map/attend/pallas_call | solution.py:290
  77.0 8.3 %collective-permute-done.26.x2 = bf16[128,768]{1,0:T(8,128)(2,1)S(1)} collective-permute-done((bf16[128,768]{1,0:T(8,128)(2,1)S(1)}, bf16[128,768]{1,0:T(8,128)(2,1)S(1)}, u32[]{:S(2)}, u32[]{:S(2)}) %collective-permute-start.26) | collective-permute-done | bytes 196640 | tf_op jit(solution)/shard_map/mlpy_x1_4/ppermute | solution.py:774
  88.4 3.6 %mlp.1 = (bf16[256,768]{1,0:T(8,128)(2,1)S(1)}, bf16[256,768]{1,0:T(8,128)(2,1)S(1)}, f32[256,1536]{1,0:T(8,128)S(1)}, f32[128,768]{1,0:T(8,128)S(1)}, bf16[128,768]{1,0:T(8,128)(2,1)S(1)}) custom-call(s32[7]{0:T(128)S(1)} %copy-done.4, f32[1,1536]{1,0:T(1,128)S(1)} %get-tuple-element.149.bias, bf16[128,768]{1,0:T(8,128)(2,1)S(1)} %get-tuple-element.170.x0, ...), custom_call_target="tpu_custom_call" | custom-call | flops 1 | bytes 10500000 | tf_op jit(solution)/shard_map/mlp/pallas_call | solution.py:51
  94.1 4.9 %collective-permute-done.29.received = bf16[128,768]{1,0:T(8,128)(2,1)S(1)} collective-permute-done((bf16[128,768]{1,0:T(8,128)(2,1)S(1)}, bf16[128,768]{1,0:T(8,128)(2,1)S(1)}, u32[]{:S(2)}, u32[]{:S(2)}) %collective-permute-start.29) | collective-permute-done | bytes 196640 | tf_op jit(solution)/shard_map/mlpp_2/ppermute | solution.py:774
  104.5 3.3 %collective-permute-done.32.g2 = bf16[128,768]{1,0:T(8,128)(2,1)S(1)} collective-permute-done((bf16[128,768]{1,0:T(8,128)(2,1)S(1)}, bf16[128,768]{1,0:T(8,128)(2,1)S(1)}, u32[]{:S(2)}, u32[]{:S(2)}) %collective-permute-start.32) | collective-permute-done | bytes 196640 | tf_op jit(solution)/shard_map/mlpy_g1_4/ppermute | solution.py:774
  108.0 3.4 %mlp_back.1 = (bf16[256,768]{1,0:T(8,128)(2,1)S(1)}, bf16[256,768]{1,0:T(8,128)(2,1)S(1)}, f32[8,1536]{1,0:T(8,128)S(1)}, f32[128,768]{1,0:T(8,128)S(1)}, bf16[128,768]{1,0:T(8,128)(2,1)S(1)}) custom-call(s32[7]{0:T(128)S(1)} %copy-done.4, bf16[128,768]{1,0:T(8,128)(2,1)S(1)} %get-tuple-element.181.g0, bf16[128,768]{1,0:T(8,128)(2,1)S(1)} %collective-permute-done.31.g1, ...), custom_call_target="tpu_custom_call" | custom-call | flops 1 | bytes 10500000 | tf_op jit(solution)/shard_map/mlp_back/pallas_call | solution.py:51
  114.8 5.7 %collective-permute-done.34.received = bf16[128,768]{1,0:T(8,128)(2,1)S(1)} collective-permute-done((bf16[128,768]{1,0:T(8,128)(2,1)S(1)}, bf16[128,768]{1,0:T(8,128)(2,1)S(1)}, u32[]{:S(2)}, u32[]{:S(2)}) %collective-permute-start.34) | collective-permute-done | bytes 196640 | tf_op jit(solution)/shard_map/mlpb_2/ppermute | solution.py:774
  124.0 3.3 %mlp_grads.1 = (f32[4,192,768]{2,1,0:T(8,128)S(1)}, bf16[4,192,768]{2,1,0:T(8,128)(2,1)S(1)}) custom-call(s32[7]{0:T(128)S(1)} %copy-done.4, bf16[128,768]{1,0:T(8,128)(2,1)S(1)} %get-tuple-element.170.x0, bf16[128,768]{1,0:T(8,128)(2,1)S(1)} %collective-permute-done.25.x1, bf16[128,768]{1,0:T(8,128)(2,1)S(1)} %collective-permute-done.26.x2, ...), custom_call_target="tpu_custom_call" | custom-call | flops 1 | bytes 9900000 | tf_op jit(solution)/shard_map/mlp_grads/pallas_call | solution.py:51
  140.7 5.8 %attend_back.1 = (f32[512,384]{1,0:T(8,128)S(1)}, f32[512,384]{1,0:T(8,128)S(1)}, f32[512,384]{1,0:T(8,128)S(1)}, bf16[2,512,384]{2,1,0:T(8,128)(2,1)S(1)}) custom-call(bf16[64,384]{1,0:T(8,128)(2,1)S(1)} %get-tuple-element.211.gc0, bf16[64,384]{1,0:T(8,128)(2,1)S(1)} %collective-permute-done.36.gc1, bf16[64,384]{1,0:T(8,128)(2,1)S(1)} %collective-permute-done.37.gc2, ...), custom_call_target="tpu_custom_call" | custom-call | flops 1 | bytes 18000000 | tf_op jit(solution)/shard_map/attend_back/pallas_call | solution.py:375
  149.5 5.1 %qkv_grads.1 = (f32[128,768]{1,0:T(8,128)S(1)}, f32[128,768]{1,0:T(8,128)S(1)}, bf16[2,128,768]{2,1,0:T(8,128)(2,1)S(1)}, f32[4,296,384]{2,1,0:T(8,128)S(1)}, bf16[4,288,384]{2,1,0:T(8,128)(2,1)S(1)}) custom-call(s32[7]{0:T(128)S(1)} %copy-done.4, f32[16,128]{1,0:T(8,128)S(1)} %add_convert_fusion.meta, f32[512,384]{1,0:T(8,128)S(1)} %get-tuple-element.216.dq, ...), custom_call_target="tpu_custom_call" | custom-call | flops 1 | bytes 15000000 | tf_op jit(solution)/shard_map/qkv_grads/pallas_call | solution.py:51
  163.2 5.6 %collective-permute-done.46.received.near = bf16[2,128,768]{2,1,0:T(8,128)(2,1)S(1)} collective-permute-done((bf16[2,128,768]{2,1,0:T(8,128)(2,1)S(1)}, bf16[2,128,768]{2,1,0:T(8,128)(2,1)S(1)}, u32[]{:S(2)}, u32[]{:S(2)}) %collective-permute-start.46) | collective-permute-done | bytes 393248 | tf_op jit(solution)/shard_map/ig_2/ppermute | solution.py:774
  170.0 9.2 %collective-permute-done.51.received = bf16[344,384]{1,0:T(8,128)(2,1)S(1)} collective-permute-done((bf16[344,384]{1,0:T(8,128)(2,1)S(1)}, bf16[344,384]{1,0:T(8,128)(2,1)S(1)}, u32[]{:S(2)}, u32[]{:S(2)}) %collective-permute-start.51) | collective-permute-done | bytes 264224 | tf_op jit(solution)/shard_map/gq_z1/ppermute | solution.py:781
  188.5 2.8 %collective-permute-done.60.p3 = bf16[192,768]{1,0:T(8,128)(2,1)S(1)} collective-permute-done((bf16[192,768]{1,0:T(8,128)(2,1)S(1)}, bf16[192,768]{1,0:T(8,128)(2,1)S(1)}, u32[]{:S(2)}, u32[]{:S(2)}) %collective-permute-start.60) | collective-permute-done | bytes 294944 | tf_op jit(solution)/shard_map/gm_6/ppermute | solution.py:774
  191.3 4.6 %collective-permute-done.59.p2 = bf16[192,768]{1,0:T(8,128)(2,1)S(1)} collective-permute-done((bf16[192,768]{1,0:T(8,128)(2,1)S(1)}, bf16[192,768]{1,0:T(8,128)(2,1)S(1)}, u32[]{:S(2)}, u32[]{:S(2)}) %collective-permute-start.59) | collective-permute-done | bytes 294944 | tf_op jit(solution)/shard_map/gm_4/ppermute | solution.py:774
  202.5 6.7 %collective-permute-done.55.p3 = bf16[344,384]{1,0:T(8,128)(2,1)S(1)} collective-permute-done((bf16[344,384]{1,0:T(8,128)(2,1)S(1)}, bf16[344,384]{1,0:T(8,128)(2,1)S(1)}, u32[]{:S(2)}, u32[]{:S(2)}) %collective-permute-start.55) | collective-permute-done | bytes 264224 | tf_op jit(solution)/shard_map/gq_6/ppermute | solution.py:774
  209.2 5.2 %collective-permute-done.54.p2 = bf16[344,384]{1,0:T(8,128)(2,1)S(1)} collective-permute-done((bf16[344,384]{1,0:T(8,128)(2,1)S(1)}, bf16[344,384]{1,0:T(8,128)(2,1)S(1)}, u32[]{:S(2)}, u32[]{:S(2)}) %collective-permute-start.54) | collective-permute-done | bytes 264224 | tf_op jit(solution)/shard_map/gq_4/ppermute | solution.py:774
  214.5 3.3 %place_mlp.1 = (f32[192,3072]{1,0:T(8,128)}, f32[768,768]{1,0:T(8,128)}) custom-call(s32[7]{0:T(128)S(1)} %copy-done.4, bf16[192,768]{1,0:T(8,128)(2,1)S(1)} %sum_mlp.1.p0, bf16[192,768]{1,0:T(8,128)(2,1)S(1)} %collective-permute-done.58.p1, bf16[192,768]{1,0:T(8,128)(2,1)S(1)} %collective-permute-done.59.p2, ...), custom_call_target="tpu_custom_call" | custom-call | flops 1 | bytes 9000000 | tf_op jit(solution)/shard_map/place_mlp/pallas_call | solution.py:51
  217.9 2.6 %collective-permute-done.62.others = bf16[4,344,384]{2,1,0:T(8,128)(2,1)S(1)} collective-permute-done((bf16[4,344,384]{2,1,0:T(8,128)(2,1)S(1)}, bf16[4,344,384]{2,1,0:T(8,128)(2,1)S(1)}, u32[]{:S(2)}, u32[]{:S(2)}) %collective-permute-start.62) | collective-permute-done | bytes 1056800 | tf_op jit(solution)/shard_map/gq_1/ppermute | solution.py:774
  220.5 3.8 %place_qkv.1 = (f32[4,192,768]{2,1,0:T(8,128)}, f32[192,768]{1,0:T(8,128)}, f32[192,768]{1,0:T(8,128)}, f32[192,768]{1,0:T(8,128)}, f32[4,192]{1,0:T(4,128)}, /*...) custom-call(s32[7]{0:T(128)S(1)} %copy-done.4, ...), custom_call_target="tpu_custom_call" | custom-call | flops 1 | bytes 10500000 | tf_op jit(solution)/shard_map/place_qkv/pallas_call | solution.py:51
  (166 shorter events, 100.5 us)
Async XLA Ops:
  0.7 12.7 %collective-permute-start.2 = (bf16[128,768]{1,0:T(8,128)(2,1)}, bf16[128,768]{1,0:T(8,128)(2,1)S(1)}, u32[]{:S(2)}, u32[]{:S(2)}) collective-permute-start(bf16[128,768]{1,0:T(8,128)(2,1)} %bitcast.58), channel_id=1, source_target_pairs={{0,6},{1,7},{2,4},{3,5},{4,2},{5,3},{6,0},{7,1},{8,14},{9,15},{10,... | collective-permute-start | bytes 589832 | tf_op jit(solution)/shard_map/hid_6/ppermute | solution.py:774
  8.7 15.0 %collective-permute-start.5 = (bf16[392,384]{1,0:T(8,128)(2,1)}, bf16[392,384]{1,0:T(8,128)(2,1)}, u32[]{:S(2)}, u32[]{:S(2)}) collective-permute-start(bf16[392,384]{1,0:T(8,128)(2,1)} %get-tuple-element.141.mine), channel_id=1, source_target_pairs={{0,8},{8,0},{16,24},{24,16},{1,9},{9,1},{17,25},{25,17},{2,10},{10... | collective-permute-start | bytes 903176 | tf_op jit(solution)/shard_map/qkvw_z1/ppermute | solution.py:781
  10.7 15.6 %collective-permute-start.4 = (bf16[392,384]{1,0:T(8,128)(2,1)}, bf16[392,384]{1,0:T(8,128)(2,1)}, u32[]{:S(2)}, u32[]{:S(2)}) collective-permute-start(bf16[392,384]{1,0:T(8,128)(2,1)} %get-tuple-element.141.mine), channel_id=1, source_target_pairs={{0,16},{8,24},{16,0},{24,8},{1,17},{9,25},{17,1},{25,9},{2,18},{10... | collective-permute-start | bytes 903176 | tf_op jit(solution)/shard_map/qkvw_z2/ppermute | solution.py:781
  16.1 25.8 %collective-permute-start.3 = (bf16[4,128,768]{2,1,0:T(8,128)(2,1)S(1)}, bf16[4,128,768]{2,1,0:T(8,128)(2,1)}, u32[]{:S(2)}, u32[]{:S(2)}) collective-permute-start(bf16[4,128,768]{2,1,0:T(8,128)(2,1)S(1)} %pad_maximum_fusion.2.own_x.x), channel_id=1, source_target_pairs={{0,1},{1,0},{2,3},{3,2},{4,5},{5,4},{6,7},{7,6},{8,9},{9,8},{10,11... | collective-permute-start | bytes 2359304 | tf_op jit(solution)/shard_map/hid_1/ppermute | solution.py:774
  26.3 15.6 %collective-permute-start.6 = (bf16[392,384]{1,0:T(8,128)(2,1)}, bf16[392,384]{1,0:T(8,128)(2,1)}, u32[]{:S(2)}, u32[]{:S(2)}) collective-permute-start(bf16[392,384]{1,0:T(8,128)(2,1)} %collective-permute-done.4.refs_1_), channel_id=1, source_target_pairs={{0,8},{8,0},{16,24},{24,16},{1,9},{9,1},{17,25},{25,17},{2,10},{10... | collective-permute-start | bytes 903176 | tf_op jit(solution)/shard_map/qkvw_z1/ppermute | solution.py:781
  28.0 17.1 %collective-permute-start.11 = (bf16[192,768]{1,0:T(8,128)(2,1)}, bf16[192,768]{1,0:T(8,128)(2,1)}, u32[]{:S(2)}, u32[]{:S(2)}) collective-permute-start(bf16[192,768]{1,0:T(8,128)(2,1)} %prep_mlp.1), channel_id=1, source_target_pairs={{0,8},{8,0},{16,24},{24,16},{1,9},{9,1},{17,25},{25,17},{2,10},{10... | collective-permute-start | bytes 884744 | tf_op jit(solution)/shard_map/mlpw_z1/ppermute | solution.py:781
  29.7 15.4 %collective-permute-start.10 = (bf16[192,768]{1,0:T(8,128)(2,1)}, bf16[192,768]{1,0:T(8,128)(2,1)}, u32[]{:S(2)}, u32[]{:S(2)}) collective-permute-start(bf16[192,768]{1,0:T(8,128)(2,1)} %prep_mlp.1), channel_id=1, source_target_pairs={{0,16},{8,24},{16,0},{24,8},{1,17},{9,25},{17,1},{25,9},{2,18},{10... | collective-permute-start | bytes 884744 | tf_op jit(solution)/shard_map/mlpw_z2/ppermute | solution.py:781
  46.6 11.9 %collective-permute-start.22 = (bf16[192,768]{1,0:T(8,128)(2,1)}, bf16[192,768]{1,0:T(8,128)(2,1)S(1)}, u32[]{:S(2)}, u32[]{:S(2)}) collective-permute-start(bf16[192,768]{1,0:T(8,128)(2,1)} %collective-permute-done.10.refs_1_), channel_id=1, source_target_pairs={{0,4},{1,5},{2,6},{3,7},{4,0},{5,1},{6,2},{7,3},{8,12},{9,13},{10,... | collective-permute-start | bytes 884744 | tf_op jit(solution)/shard_map/mlpw_4/ppermute | solution.py:774
  47.2 11.3 %collective-permute-start.19 = (bf16[192,768]{1,0:T(8,128)(2,1)}, bf16[192,768]{1,0:T(8,128)(2,1)S(1)}, u32[]{:S(2)}, u32[]{:S(2)}) collective-permute-start(bf16[192,768]{1,0:T(8,128)(2,1)} %collective-permute-done.10.refs_1_), channel_id=1, source_target_pairs={{0,8},{8,0},{16,24},{24,16},{1,9},{9,1},{17,25},{25,17},{2,10},{10... | collective-permute-start | bytes 884744 | tf_op jit(solution)/shard_map/mlpw_z1/ppermute | solution.py:781
  71.7 13.6 %collective-permute-start.27 = (bf16[192,768]{1,0:T(8,128)(2,1)S(1)}, bf16[192,768]{1,0:T(8,128)(2,1)S(1)}, u32[]{:S(2)}, u32[]{:S(2)}) collective-permute-start(bf16[192,768]{1,0:T(8,128)(2,1)S(1)} %collective-permute-done.19.refs_2_), channel_id=1, source_target_pairs={{0,4},{1,5},{2,6},{3,7},{4,0},{5,1},{6,2},{7,3},{8,12},{9,13},{10,... | collective-permute-start | bytes 884744 | tf_op jit(solution)/shard_map/mlpw_4/ppermute | solution.py:774
  92.6 11.8 %collective-permute-start.33 = (bf16[256,768]{1,0:T(8,128)(2,1)S(1)}, bf16[256,768]{1,0:T(8,128)(2,1)S(1)}, u32[]{:S(2)}, u32[]{:S(2)}) collective-permute-start(bf16[256,768]{1,0:T(8,128)(2,1)S(1)} %get-tuple-element.182), channel_id=1, source_target_pairs={{0,4},{1,5},{2,6},{3,7},{4,0},{5,1},{6,2},{7,3},{8,12},{9,13},{10,... | collective-permute-start | bytes 1179656 | tf_op jit(solution)/shard_map/mlpy_a_4/ppermute | solution.py:774
  111.4 12.5 %collective-permute-start.39 = (bf16[256,768]{1,0:T(8,128)(2,1)S(1)}, bf16[256,768]{1,0:T(8,128)(2,1)S(1)}, u32[]{:S(2)}, u32[]{:S(2)}) collective-permute-start(bf16[256,768]{1,0:T(8,128)(2,1)S(1)} %get-tuple-element.200), channel_id=1, source_target_pairs={{0,4},{1,5},{2,6},{3,7},{4,0},{5,1},{6,2},{7,3},{8,12},{9,13},{10,... | collective-permute-start | bytes 1179656 | tf_op jit(solution)/shard_map/mlpy_l_4/ppermute | solution.py:774
  157.3 11.5 %collective-permute-start.46 = (bf16[2,128,768]{2,1,0:T(8,128)(2,1)S(1)}, bf16[2,128,768]{2,1,0:T(8,128)(2,1)S(1)}, u32[]{:S(2)}, u32[]{:S(2)}) collective-permute-start(bf16[2,128,768]{2,1,0:T(8,128)(2,1)S(1)} %get-tuple-element.231), channel_id=1, source_target_pairs={{0,2},{1,3},{2,0},{3,1},{4,6},{5,7},{6,4},{7,5},{8,10},{9,11},{10,... | collective-permute-start | bytes 1179656 | tf_op jit(solution)/shard_map/ig_2/ppermute | solution.py:774
  158.1 21.7 %collective-permute-start.56 = (bf16[192,768]{1,0:T(8,128)(2,1)S(1)}, bf16[192,768]{1,0:T(8,128)(2,1)S(1)}, u32[]{:S(2)}, u32[]{:S(2)}) collective-permute-start(bf16[192,768]{1,0:T(8,128)(2,1)S(1)} %get-tuple-element.203), channel_id=1, source_target_pairs={{0,8},{8,0},{16,24},{24,16},{1,9},{9,1},{17,25},{25,17},{2,10},{10... | collective-permute-start | bytes 884744 | tf_op jit(solution)/shard_map/gm_z1/ppermute | solution.py:781
  159.4 20.4 %collective-permute-start.57 = (bf16[192,768]{1,0:T(8,128)(2,1)S(1)}, bf16[192,768]{1,0:T(8,128)(2,1)S(1)}, u32[]{:S(2)}, u32[]{:S(2)}) collective-permute-start(bf16[192,768]{1,0:T(8,128)(2,1)S(1)} %relay.2), channel_id=1, source_target_pairs={{0,16},{8,24},{16,0},{24,8},{1,17},{9,25},{17,1},{25,9},{2,18},{10... | collective-permute-start | bytes 884744 | tf_op jit(solution)/shard_map/gm_z2/ppermute | solution.py:781
  162.0 17.1 %collective-permute-start.51 = (bf16[344,384]{1,0:T(8,128)(2,1)S(1)}, bf16[344,384]{1,0:T(8,128)(2,1)S(1)}, u32[]{:S(2)}, u32[]{:S(2)}) collective-permute-start(bf16[344,384]{1,0:T(8,128)(2,1)S(1)} %get-tuple-element.242), channel_id=1, source_target_pairs={{0,8},{8,0},{16,24},{24,16},{1,9},{9,1},{17,25},{25,17},{2,10},{10... | collective-permute-start | bytes 792584 | tf_op jit(solution)/shard_map/gq_z1/ppermute | solution.py:781
  169.4 15.9 %collective-permute-start.47 = (bf16[128,768]{1,0:T(8,128)(2,1)S(1)}, bf16[128,768]{1,0:T(8,128)(2,1)S(1)}, u32[]{:S(2)}, u32[]{:S(2)}) collective-permute-start(bf16[128,768]{1,0:T(8,128)(2,1)S(1)} %relay_ig.1), channel_id=1, source_target_pairs={{0,4},{1,5},{2,6},{3,7},{4,0},{5,1},{6,2},{7,3},{8,12},{9,13},{10,... | collective-permute-start | bytes 589832 | tf_op jit(solution)/shard_map/ig_4/ppermute | solution.py:774
  181.7 14.2 %collective-permute-start.59 = (bf16[192,768]{1,0:T(8,128)(2,1)S(1)}, bf16[192,768]{1,0:T(8,128)(2,1)S(1)}, u32[]{:S(2)}, u32[]{:S(2)}) collective-permute-start(bf16[192,768]{1,0:T(8,128)(2,1)S(1)} %sum_mlp.1.p0), channel_id=1, source_target_pairs={{0,4},{1,5},{2,6},{3,7},{4,0},{5,1},{6,2},{7,3},{8,12},{9,13},{10,... | collective-permute-start | bytes 884744 | tf_op jit(solution)/shard_map/gm_4/ppermute | solution.py:774
  183.2 12.6 %collective-permute-start.58 = (bf16[192,768]{1,0:T(8,128)(2,1)S(1)}, bf16[192,768]{1,0:T(8,128)(2,1)S(1)}, u32[]{:S(2)}, u32[]{:S(2)}) collective-permute-start(bf16[192,768]{1,0:T(8,128)(2,1)S(1)} %sum_mlp.1.p0), channel_id=1, source_target_pairs={{0,2},{1,3},{2,0},{3,1},{4,6},{5,7},{6,4},{7,5},{8,10},{9,11},{10,... | collective-permute-start | bytes 884744 | tf_op jit(solution)/shard_map/gm_2/ppermute | solution.py:774
  183.9 12.2 %collective-permute-start.50 = (bf16[344,384]{1,0:T(8,128)(2,1)S(1)}, bf16[344,384]{1,0:T(8,128)(2,1)S(1)}, u32[]{:S(2)}, u32[]{:S(2)}) collective-permute-start(bf16[344,384]{1,0:T(8,128)(2,1)S(1)} %get-tuple-element.240), channel_id=1, source_target_pairs={{0,8},{8,0},{16,24},{24,16},{1,9},{9,1},{17,25},{25,17},{2,10},{10... | collective-permute-start | bytes 792584 | tf_op jit(solution)/shard_map/gq_z1/ppermute | solution.py:781
  185.3 13.0 %collective-permute-start.52 = (bf16[344,384]{1,0:T(8,128)(2,1)S(1)}, bf16[344,384]{1,0:T(8,128)(2,1)S(1)}, u32[]{:S(2)}, u32[]{:S(2)}) collective-permute-start(bf16[344,384]{1,0:T(8,128)(2,1)S(1)} %relay.3), channel_id=1, source_target_pairs={{0,16},{8,24},{16,0},{24,8},{1,17},{9,25},{17,1},{25,9},{2,18},{10... | collective-permute-start | bytes 792584 | tf_op jit(solution)/shard_map/gq_z2/ppermute | solution.py:781
  198.3 16.2 %collective-permute-start.61 = (bf16[4,192,768]{2,1,0:T(8,128)(2,1)S(1)}, bf16[4,192,768]{2,1,0:T(8,128)(2,1)S(1)}, u32[]{:S(2)}, u32[]{:S(2)}) collective-permute-start(bf16[4,192,768]{2,1,0:T(8,128)(2,1)S(1)} %pad_maximum_fusion), channel_id=1, source_target_pairs={{0,1},{1,0},{2,3},{3,2},{4,5},{5,4},{6,7},{7,6},{8,9},{9,8},{10,11... | collective-permute-start | bytes 3538952 | tf_op jit(solution)/shard_map/gm_1/ppermute | solution.py:774
  200.3 14.1 %collective-permute-start.54 = (bf16[344,384]{1,0:T(8,128)(2,1)S(1)}, bf16[344,384]{1,0:T(8,128)(2,1)S(1)}, u32[]{:S(2)}, u32[]{:S(2)}) collective-permute-start(bf16[344,384]{1,0:T(8,128)(2,1)S(1)} %sum_qkv.1.p0), channel_id=1, source_target_pairs={{0,4},{1,5},{2,6},{3,7},{4,0},{5,1},{6,2},{7,3},{8,12},{9,13},{10,... | collective-permute-start | bytes 792584 | tf_op jit(solution)/shard_map/gq_4/ppermute | solution.py:774
  201.8 12.5 %collective-permute-start.53 = (bf16[344,384]{1,0:T(8,128)(2,1)S(1)}, bf16[344,384]{1,0:T(8,128)(2,1)S(1)}, u32[]{:S(2)}, u32[]{:S(2)}) collective-permute-start(bf16[344,384]{1,0:T(8,128)(2,1)S(1)} %sum_qkv.1.p0), channel_id=1, source_target_pairs={{0,2},{1,3},{2,0},{3,1},{4,6},{5,7},{6,4},{7,5},{8,10},{9,11},{10,... | collective-permute-start | bytes 792584 | tf_op jit(solution)/shard_map/gq_2/ppermute | solution.py:774
  (50 other events, 385.0 us)

commit v4 on v3

--- a/solution.py
+++ b/solution.py
@@ -520,6 +520,19 @@
 
 def relay_body(sc, value, received, out):
     out[...] = (value[...] + received[...].astype(F32)).astype(BF16)
+
+
+def relay_halves_body(sc, value, received, one, two):
+    half = one.shape[0]
+    one[...] = (value[0:half, :] + received[0:half, :].astype(F32)).astype(BF16)
+    two[...] = (value[half:, :] + received[half:, :].astype(F32)).astype(BF16)
+
+
+def sum_halves_body(sc, own, near, one, two, out):
+    half = one.shape[0]
+    value = own[...] + near[...].astype(F32)
+    out[0:half, :] = (value[0:half] + one[...].astype(F32)).astype(out.dtype)
+    out[half:, :] = (value[half:] + two[...].astype(F32)).astype(out.dtype)
 
 
 def relay_second_body(sc, value, received, out):
@@ -780,16 +793,19 @@
         with jax.named_scope(f"{name}_z{shift}"):
             return lax.ppermute(value, "shard", [(i, i ^ shift) for i in range(shards)])
 
-    def collect(value, name):
+    def first_two(value, name):
         far = turn(value, 2, name)
         far, near = lax.optimization_barrier((far, turn(value, 1, name)))
-        return [near, far, turn(far, 1, name)]
-
-    def reduce(parts, name, *others):
+        return [near, far]
+
+    def collect(pair, name):
+        return pair + [turn(pair[1], 1, name)]
+
+    def reduce(parts, name):
         _, near, far, last = parts
-        last = after(turn(last, 1, name), *others)
-        near = turn(near, 1, name)
+        last = turn(last, 1, name)
         far = run(relay_body, "relay", sds(far.shape, BF16), scalars, far, last)
+        near = turn(after(near, far), 1, name)
         return [near, turn(far, 2, name)], far
 
     def after(value, *others):
@@ -816,7 +832,7 @@
         down_bias, norm2_gain, norm2_bias, up_bias,
         vmem=60,
     )
-    own_w = collect(mine, "qkvw")
+    own_w = collect(first_two(mine, "qkvw"), "qkvw")
     quarter = rows // 4
     mlp_one = run(
         prep_mlp_body,
@@ -827,7 +843,7 @@
         lax.dynamic_slice_in_dim(down_weight, chip_x * side + spot * (side // 4), side // 4, 0),
     )
     own_x = jnp.stack([hid] + [chips(hid, rel, "hid") for rel in range(1, 4)])
-    mlp_z = collect(mlp_one, "mlpw")
+    mlp_z = collect(first_two(mlp_one, "mlpw"), "mlpw")
     other_x = across(own_x, 1, "hid")
     other_w = [across(after(piece, other_x), 1, "qkvw") for piece in own_w]
 
@@ -867,7 +883,7 @@
     probs, cx = attend(after(pq, mlp_core), pk, vv, valid, slots)
     cx = after(cx, out_far, mlp_far[0])
     cxs = [cx[0]] + [chips(cx[rel], rel, "cx") for rel in range(1, 4)]
-    mlp_core += [across(piece, 1, "mlpw") for piece in (mlp_z[2], mlp_far[0], mlp_far[1])]
+    mlp_core += [across(piece, 1, "mlpw") for piece in [mlp_z[2]] + mlp_far[:2]]
     cxs = after(cxs, mlp_core)
     *cxs, out_far = lax.optimization_barrier((*cxs, out_far))
     wo = run(
@@ -885,10 +901,10 @@
         vecs, *cxs, wo, hid,
     )
     low_two = chips(low_one, 1, "mlpx")
-    low_two, far_one = lax.optimization_barrier((low_two, across(low_one, 4, "mlpy_x1")))
-    far_two = chips(far_one, 1, "mlpy_x2")
+    far_one = across(low_one, 4, "mlpy_x1")
+    far_two = across(low_two, 4, "mlpy_x2")
+    mlp_core.append(across(after(mlp_far[2], low_two), 1, "mlpw"))
     pieces = mlp_z + mlp_far
-    mlp_core.append(across(after(mlp_far[2], low_two), 1, "mlpw"))
     wup, wdn = run(
         partial(assemble_mlp_body, shards),
         "assemble_mlp",
@@ -910,7 +926,9 @@
         scalars,
         up_shift, low_one, low_two, wup, wdn,
     )
-    received, far_two = lax.optimization_barrier((chips(send, 1, "mlpp"), far_two))
+    received, far_one, far_two = lax.optimization_barrier(
+        (chips(send, 1, "mlpp"), far_one, far_two)
+    )
     act_far = across(act_send, 4, "mlpy_a")
     output, gs, gs_low, sums_two = run(
         norm_two_body,
@@ -927,7 +945,6 @@
     gs_other, gs_far_one, act_far = lax.optimization_barrier(
         (chips(gs_low, 1, "mlpg"), across(gs_low, 4, "mlpy_g1"), act_far)
     )
-    gs_far_two = chips(gs_far_one, 1, "mlpy_g2")
     low_keep, low_send, sums_up, own, send = run(
         partial(mlp_back_body, 384),
         "mlp_back",
@@ -941,7 +958,8 @@
         scalars,
         gs_low, gs_other, slope, wup, wdn,
     )
-    received, gs_far_two = lax.optimization_barrier((chips(send, 1, "mlpb"), gs_far_two))
+    received = chips(send, 1, "mlpb")
+    gs_far_two = chips(after(gs_far_one, received), 1, "mlpy_g2")
     low_far = across(low_send, 4, "mlpy_l")
     gf, gf_low, gcx, sums_one = run(
         norm_one_back_body,
@@ -956,21 +974,21 @@
         vecs, own, received, gs, unit_one, rate_one, wo,
     )
     gcs = [gcx[0]] + [chips(gcx[rel], rel, "gcx") for rel in range(1, 4)]
+    keep_out, send_out = run(
+        out_grads_body,
+        "out_grads",
+        [sds((CHIPS, COLS, width // 2), F32), sds((CHIPS, COLS, width // 2), BF16)],
+        scalars,
+        *cxs,
+        gf_low,
+    )
     keep_mlp, send_mlp = run(
         partial(mlp_grads_body, shards),
         "mlp_grads",
         [sds((shards, rows, width), F32), sds((shards, rows, width), BF16)],
         scalars,
         low_one, low_two, far_one, far_two, gs_low, gs_other, gs_far_one, gs_far_two,
-        act, act_far, after(low_keep, gf_low), low_far,
-    )
-    keep_out, send_out = run(
-        out_grads_body,
-        "out_grads",
-        [sds((CHIPS, COLS, width // 2), F32), sds((CHIPS, COLS, width // 2), BF16)],
-        scalars,
-        *cxs,
-        after(gf_low, send_mlp),
+        act, act_far, after(low_keep, send_out), low_far,
     )
 
     kind = BF16 if groups == 1 else F32
@@ -1018,7 +1036,17 @@
         after(out_own, dq),
         *[chips(out_sends[rel - 1], rel, "go") for rel in range(1, 4)],
     )
-    dkv_rec = across(after(dkv, planes), 1, "dkv")
+    gm_far = run(
+        relay_halves_body,
+        "relay_mlp",
+        [sds((rows // 2, width), BF16)] * 2,
+        scalars,
+        mlp_parts[2],
+        after(turn(mlp_parts[3], 1, "gm"), dq),
+    )
+    gm_near = turn(mlp_parts[1], 1, "gm")
+    dkv_rec = across(after(dkv, planes, gm_far, gm_near), 1, "dkv")
+    gm_far = [turn(value, 2, "gm") for value in gm_far]
     own, own_far, send, keep_w, send_w = run(
         partial(qkv_grads_body, shards),
         "qkv_grads",
@@ -1033,7 +1061,6 @@
         meta, dq, dk_own, dv_own, dkv_rec, wall, sums_one, sums_two, sums_up, own_x,
         scratch=[pltpu.VMEM((2, 4 * slots, 2 * WIDE), BF16)],
     )
-    mlp_recs, gm_far = reduce(mlp_parts, "gm", own)
     size = main + small_rows + quarter
     qkv_parts = run(
         partial(qkv_fan_body, shards),
@@ -1041,7 +1068,7 @@
         fan((size, WIDE)),
         scalars,
         keep_w,
-        across(after(send_w, gm_far), 1, "gq"),
+        across(after(send_w, gm_far[0]), 1, "gq"),
         planes,
     )
     qkv_recs, gq_far = reduce(qkv_parts, "gq")
@@ -1058,9 +1085,9 @@
         gf, own, near, chips(far, 2, "ig"),
     )
 
-    mlp_recs = after(mlp_recs, gq_far, far)
+    mlp_recs = after([gm_near] + gm_far, gq_far, far)
     low = run(
-        gather_sum_body, "sum_mlp", sds((rows, width), kind), scalars, mlp_parts[0], *mlp_recs
+        sum_halves_body, "sum_mlp", sds((rows, width), kind), scalars, mlp_parts[0], *mlp_recs
     )
     done_mlp = spread(low, "gm", (input_grad, qkv_recs))
     ug, dg = run(
@@ -1074,7 +1101,7 @@
     low = run(
         gather_sum_body, "sum_qkv", sds((size, WIDE), kind), scalars, qkv_parts[0], *qkv_recs
     )
-    done_qkv = spread(low, "gq", (ug, dg))
+    done_qkv = spread(low, "gq")
 
     vec = sds((rows,), F32)
     qg, kg, vg, og, qbg, kbg, vbg, obg, g1g, b1g, dbg, g2g, b2g, ubg = run(

time: 225 us -> 214 us (0.951)
  waiting for transfers between devices: 99.6 us -> 82.9 us
  starting transfers between devices: 59.5 us -> 65.1 us
    ppermute x51, waiting for transfers between devices: 63 us -> 45.2 us  [across(): return lax.ppermute(value, 'ctx', [(i, i ^ mask) for i in range(lanes)])]
    ppermute x51, starting transfers between devices: 41.4 us -> 45.1 us  [across(): return lax.ppermute(value, 'ctx', [(i, i ^ mask) for i in range(lanes)])]
    ppermute x12 -> x13, starting transfers between devices: 18.1 us -> 20 us  [turn(): return lax.ppermute(value, 'shard', [(i, i ^ shift) for i in range(shards)])]
    ppermute x12 -> x13, waiting for transfers between devices: 36.6 us -> 37.7 us  [turn(): return lax.ppermute(value, 'shard', [(i, i ^ shift) for i in range(shards)])]
  transfers between devices with their start and end apart: 63 -> 64, of which waited for: 32 -> 30; matrix products, arithmetic and copies ran while one was open for 1% -> 1% of each run, Pallas kernels for 19% -> 22%
where the time goes in v4:
time: 214 us; the launch traced here: 213 us
  waiting for transfers between devices  82.9 us (39%)
  starting transfers between devices  65.1 us (30%)
  Pallas kernels  58.4 us (27%)
  local copies, waits for them, and re-layouts  3.41 us (2%)
    pallas_call x25, Pallas kernels, run(): pl.pallas_call(body, out_shape=outs, in_specs=[SMEM] + [VMEM] * len(array...  47.1 us
    ppermute x51, waiting for transfers between devices, across(): return lax.ppermute(value, 'ctx', [(i, i ^ mask) for i in range(lanes)])  45.2 us
    ppermute x51, starting transfers between devices, across(): return lax.ppermute(value, 'ctx', [(i, i ^ mask) for i in range(lanes)])  45.1 us
    ppermute x13, waiting for transfers between devices, turn(): return lax.ppermute(value, 'shard', [(i, i ^ shift) for i in range(shards)])  37.7 us
    ppermute x13, starting transfers between devices, turn(): return lax.ppermute(value, 'shard', [(i, i ^ shift) for i in range(shards)])  20 us
    pallas_call x1, Pallas kernels, attend_back(): pl.pallas_call(partial(attend_back_body, step, split), grid=(LOCAL_HEADS,...  5.85 us
    pallas_call x1, Pallas kernels, attend(): pl.pallas_call(partial(attend_body, step), grid=(LOCAL_HEADS,), in_specs=...  5.47 us
  transfers between devices with their start and end apart: 64, of which 30 were waited for; matrix products, arithmetic and copies ran while one was open for 1% of the time, Pallas kernels for 22%

profile of v4, /device:TPU:0, one launch (start us, length us, event | category | flops | bytes accessed | tf_op | source)
XLA Modules:
  0.0 213.4 jit_solution(2658473045704909069)
XLA Ops:
  0.7 4.0 %collective-permute-start.2 = (bf16[128,768]{1,0:T(8,128)(2,1)}, bf16[128,768]{1,0:T(8,128)(2,1)S(1)}, u32[]{:S(2)}, u32[]{:S(2)}) collective-permute-start(bf16[128,768]{1,0:T(8,128)(2,1)} %bitcast.58), channel_id=1, source_target_pairs={{0,6},{1,7},{2,4},{3,5},{4,2},{5,3},{6,0},{7,1},{8,14},{9,15},{10,... | collective-permute-start | bytes 589832 | tf_op jit(solution)/shard_map/hid_6/ppermute | solution.py:787
  16.9 6.7 %collective-permute-done.5.refs_0_ = bf16[392,384]{1,0:T(8,128)(2,1)} collective-permute-done((bf16[392,384]{1,0:T(8,128)(2,1)}, bf16[392,384]{1,0:T(8,128)(2,1)}, u32[]{:S(2)}, u32[]{:S(2)}) %collective-permute-start.5) | collective-permute-done | bytes 301088 | tf_op jit(solution)/shard_map/qkvw_z1/ppermute | solution.py:794
  30.7 11.2 %collective-permute-done.6.refs_2_ = bf16[392,384]{1,0:T(8,128)(2,1)} collective-permute-done((bf16[392,384]{1,0:T(8,128)(2,1)}, bf16[392,384]{1,0:T(8,128)(2,1)}, u32[]{:S(2)}, u32[]{:S(2)}) %collective-permute-start.6) | collective-permute-done | bytes 301088 | tf_op jit(solution)/shard_map/qkvw_z1/ppermute | solution.py:794
  50.6 4.8 %qkv.1 = (bf16[2,768,768]{2,1,0:T(8,128)(2,1)S(1)}, bf16[512,384]{1,0:T(8,128)(2,1)S(1)}, bf16[1024,384]{1,0:T(8,128)(2,1)S(1)}, bf16[1024,384]{1,0:T(8,128)(2,1...) custom-call(s32[7]{0:T(128)S(1)} %copy-done.4, ...), custom_call_target="tpu_custom_call" | custom-call | flops 1 | bytes 3000000 | tf_op jit(solution)/shard_map/qkv/pallas_call | solution.py:51
  59.0 5.5 %attend.1 = (bf16[3,512,1024]{2,1,0:T(8,128)(2,1)S(1)}, bf16[4,64,384]{2,1,0:T(8,128)(2,1)S(1)}) custom-call(bf16[512,384]{1,0:T(8,128)(2,1)S(1)} %get-tuple-element.154.pq, bf16[1024,384]{1,0:T(8,128)(2,1)S(1)} %get-tuple-element.155.pk, bf16[1024,384]{1,0:T(8,128)(2,1)S(1)} %get-tuple-element.156.vv, f32[1,1024]{1,0:T(1,128)S(1)} %bitcast.63), custom_call_target="tpu_custom_call" | custom-call | flops 1 | bytes 16500000 | tf_op jit(solution)/shard_map/attend/pallas_call | solution.py:290
  75.6 5.5 %collective-permute-done.26.refs_5_ = bf16[192,768]{1,0:T(8,128)(2,1)S(1)} collective-permute-done((bf16[192,768]{1,0:T(8,128)(2,1)S(1)}, bf16[192,768]{1,0:T(8,128)(2,1)S(1)}, u32[]{:S(2)}, u32[]{:S(2)}) %collective-permute-start.26) | collective-permute-done | bytes 294944 | tf_op jit(solution)/shard_map/mlpw_4/ppermute | solution.py:787
  85.6 3.6 %mlp.1 = (bf16[256,768]{1,0:T(8,128)(2,1)S(1)}, bf16[256,768]{1,0:T(8,128)(2,1)S(1)}, f32[256,1536]{1,0:T(8,128)S(1)}, f32[128,768]{1,0:T(8,128)S(1)}, bf16[128,768]{1,0:T(8,128)(2,1)S(1)}) custom-call(s32[7]{0:T(128)S(1)} %copy-done.4, f32[1,1536]{1,0:T(1,128)S(1)} %get-tuple-element.149.bias, bf16[128,768]{1,0:T(8,128)(2,1)S(1)} %get-tuple-element.170.x0, ...), custom_call_target="tpu_custom_call" | custom-call | flops 1 | bytes 10500000 | tf_op jit(solution)/shard_map/mlp/pallas_call | solution.py:51
  91.2 2.9 %collective-permute-done.30.x3 = bf16[128,768]{1,0:T(8,128)(2,1)S(1)} collective-permute-done((bf16[128,768]{1,0:T(8,128)(2,1)S(1)}, bf16[128,768]{1,0:T(8,128)(2,1)S(1)}, u32[]{:S(2)}, u32[]{:S(2)}) %collective-permute-start.30) | collective-permute-done | bytes 196640 | tf_op jit(solution)/shard_map/mlpy_x2_4/ppermute | solution.py:787
  99.6 2.9 %collective-permute-done.33.act_r = bf16[256,768]{1,0:T(8,128)(2,1)S(1)} collective-permute-done((bf16[256,768]{1,0:T(8,128)(2,1)S(1)}, bf16[256,768]{1,0:T(8,128)(2,1)S(1)}, u32[]{:S(2)}, u32[]{:S(2)}) %collective-permute-start.33) | collective-permute-done | bytes 393248 | tf_op jit(solution)/shard_map/mlpy_a_4/ppermute | solution.py:787
  102.5 3.8 %collective-permute-done.32.g2 = bf16[128,768]{1,0:T(8,128)(2,1)S(1)} collective-permute-done((bf16[128,768]{1,0:T(8,128)(2,1)S(1)}, bf16[128,768]{1,0:T(8,128)(2,1)S(1)}, u32[]{:S(2)}, u32[]{:S(2)}) %collective-permute-start.32) | collective-permute-done | bytes 196640 | tf_op jit(solution)/shard_map/mlpy_g1_4/ppermute | solution.py:787
  106.2 3.4 %mlp_back.1 = (bf16[256,768]{1,0:T(8,128)(2,1)S(1)}, bf16[256,768]{1,0:T(8,128)(2,1)S(1)}, f32[8,1536]{1,0:T(8,128)S(1)}, f32[128,768]{1,0:T(8,128)S(1)}, bf16[128,768]{1,0:T(8,128)(2,1)S(1)}) custom-call(s32[7]{0:T(128)S(1)} %copy-done.4, bf16[128,768]{1,0:T(8,128)(2,1)S(1)} %get-tuple-element.179.g0, bf16[128,768]{1,0:T(8,128)(2,1)S(1)} %collective-permute-done.31.g1, ...), custom_call_target="tpu_custom_call" | custom-call | flops 1 | bytes 10500000 | tf_op jit(solution)/shard_map/mlp_back/pallas_call | solution.py:51
  111.7 4.5 %collective-permute-done.34.received = bf16[128,768]{1,0:T(8,128)(2,1)S(1)} collective-permute-done((bf16[128,768]{1,0:T(8,128)(2,1)S(1)}, bf16[128,768]{1,0:T(8,128)(2,1)S(1)}, u32[]{:S(2)}, u32[]{:S(2)}) %collective-permute-start.34) | collective-permute-done | bytes 196640 | tf_op jit(solution)/shard_map/mlpb_2/ppermute | solution.py:787
  121.9 3.5 %mlp_grads.1 = (f32[4,192,768]{2,1,0:T(8,128)S(1)}, bf16[4,192,768]{2,1,0:T(8,128)(2,1)S(1)}) custom-call(s32[7]{0:T(128)S(1)} %copy-done.4, bf16[128,768]{1,0:T(8,128)(2,1)S(1)} %get-tuple-element.170.x0, bf16[128,768]{1,0:T(8,128)(2,1)S(1)} %collective-permute-done.25.x1, bf16[128,768]{1,0:T(8,128)(2,1)S(1)} %collective-permute-done.29.x2, ...), custom_call_target="tpu_custom_call" | custom-call | flops 1 | bytes 9900000 | tf_op jit(solution)/shard_map/mlp_grads/pallas_call | solution.py:51
  140.6 5.9 %attend_back.1 = (f32[512,384]{1,0:T(8,128)S(1)}, f32[512,384]{1,0:T(8,128)S(1)}, f32[512,384]{1,0:T(8,128)S(1)}, bf16[2,512,384]{2,1,0:T(8,128)(2,1)S(1)}) custom-call(bf16[64,384]{1,0:T(8,128)(2,1)S(1)} %get-tuple-element.208.gc0, bf16[64,384]{1,0:T(8,128)(2,1)S(1)} %collective-permute-done.35.gc1, bf16[64,384]{1,0:T(8,128)(2,1)S(1)} %collective-permute-done.36.gc2, ...), custom_call_target="tpu_custom_call" | custom-call | flops 1 | bytes 18000000 | tf_op jit(solution)/shard_map/attend_back/pallas_call | solution.py:375
  150.2 5.1 %qkv_grads.1 = (f32[128,768]{1,0:T(8,128)S(1)}, f32[128,768]{1,0:T(8,128)S(1)}, bf16[2,128,768]{2,1,0:T(8,128)(2,1)S(1)}, f32[4,296,384]{2,1,0:T(8,128)S(1)}, bf16[4,288,384]{2,1,0:T(8,128)(2,1)S(1)}) custom-call(s32[7]{0:T(128)S(1)} %copy-done.4, f32[16,128]{1,0:T(8,128)S(1)} %add_convert_fusion.meta, f32[512,384]{1,0:T(8,128)S(1)} %get-tuple-element.213.dq, ...), custom_call_target="tpu_custom_call" | custom-call | flops 1 | bytes 15000000 | tf_op jit(solution)/shard_map/qkv_grads/pallas_call | solution.py:51
  163.1 3.1 %collective-permute-start.59 = (bf16[96,768]{1,0:T(8,128)(2,1)S(1)}, bf16[96,768]{1,0:T(8,128)(2,1)S(1)}, u32[]{:S(2)}, u32[]{:S(2)}) collective-permute-start(bf16[96,768]{1,0:T(8,128)(2,1)S(1)} %get-tuple-element.226), channel_id=1, source_target_pairs={{0,16},{8,24},{16,0},{24,8},{1,17},{9,25},{17,1},{25,9},{2,18},{10... | collective-permute-start | bytes 442376 | tf_op jit(solution)/shard_map/gm_z2/ppermute | solution.py:794
  166.2 6.6 %collective-permute-done.52.received = bf16[344,384]{1,0:T(8,128)(2,1)S(1)} collective-permute-done((bf16[344,384]{1,0:T(8,128)(2,1)S(1)}, bf16[344,384]{1,0:T(8,128)(2,1)S(1)}, u32[]{:S(2)}, u32[]{:S(2)}) %collective-permute-start.52) | collective-permute-done | bytes 264224 | tf_op jit(solution)/shard_map/gq_z1/ppermute | solution.py:794
  177.4 3.2 %collective-permute-start.54 = (bf16[344,384]{1,0:T(8,128)(2,1)S(1)}, bf16[344,384]{1,0:T(8,128)(2,1)S(1)}, u32[]{:S(2)}, u32[]{:S(2)}) collective-permute-start(bf16[344,384]{1,0:T(8,128)(2,1)S(1)} %relay.1), channel_id=1, source_target_pairs={{0,16},{8,24},{16,0},{24,8},{1,17},{9,25},{17,1},{25,9},{2,18},{10... | collective-permute-start | bytes 792584 | tf_op jit(solution)/shard_map/gq_z2/ppermute | solution.py:794
  182.6 3.7 %collective-permute-start.60 = (bf16[192,768]{1,0:T(8,128)(2,1)S(1)}, bf16[192,768]{1,0:T(8,128)(2,1)S(1)}, u32[]{:S(2)}, u32[]{:S(2)}) collective-permute-start(bf16[192,768]{1,0:T(8,128)(2,1)S(1)} %sum_mlp.1.p0), channel_id=1, source_target_pairs={{0,2},{1,3},{2,0},{3,1},{4,6},{5,7},{6,4},{7,5},{8,10},{9,11},{10,... | collective-permute-start | bytes 884744 | tf_op jit(solution)/shard_map/gm_2/ppermute | solution.py:787
  186.3 5.1 %collective-permute-done.54.refs_1_ = bf16[344,384]{1,0:T(8,128)(2,1)S(1)} collective-permute-done((bf16[344,384]{1,0:T(8,128)(2,1)S(1)}, bf16[344,384]{1,0:T(8,128)(2,1)S(1)}, u32[]{:S(2)}, u32[]{:S(2)}) %collective-permute-start.54) | collective-permute-done | bytes 264224 | tf_op jit(solution)/shard_map/gq_z2/ppermute | solution.py:794
  198.6 3.7 %collective-permute-done.57.p3 = bf16[344,384]{1,0:T(8,128)(2,1)S(1)} collective-permute-done((bf16[344,384]{1,0:T(8,128)(2,1)S(1)}, bf16[344,384]{1,0:T(8,128)(2,1)S(1)}, u32[]{:S(2)}, u32[]{:S(2)}) %collective-permute-start.57) | collective-permute-done | bytes 264224 | tf_op jit(solution)/shard_map/gq_6/ppermute | solution.py:787
  202.3 3.5 %collective-permute-done.56.p2 = bf16[344,384]{1,0:T(8,128)(2,1)S(1)} collective-permute-done((bf16[344,384]{1,0:T(8,128)(2,1)S(1)}, bf16[344,384]{1,0:T(8,128)(2,1)S(1)}, u32[]{:S(2)}, u32[]{:S(2)}) %collective-permute-start.56) | collective-permute-done | bytes 264224 | tf_op jit(solution)/shard_map/gq_4/ppermute | solution.py:787
  206.1 3.3 %place_mlp.1 = (f32[192,3072]{1,0:T(8,128)}, f32[768,768]{1,0:T(8,128)}) custom-call(s32[7]{0:T(128)S(1)} %copy-done.4, bf16[192,768]{1,0:T(8,128)(2,1)S(1)} %sum_mlp.1.p0, bf16[192,768]{1,0:T(8,128)(2,1)S(1)} %collective-permute-done.60.p1, bf16[192,768]{1,0:T(8,128)(2,1)S(1)} %collective-permute-done.61.p2, ...), custom_call_target="tpu_custom_call" | custom-call | flops 1 | bytes 9000000 | tf_op jit(solution)/shard_map/place_mlp/pallas_call | solution.py:51
  209.4 3.8 %place_qkv.1 = (f32[4,192,768]{2,1,0:T(8,128)}, f32[192,768]{1,0:T(8,128)}, f32[192,768]{1,0:T(8,128)}, f32[192,768]{1,0:T(8,128)}, f32[4,192]{1,0:T(4,128)}, /*...) custom-call(s32[7]{0:T(128)S(1)} %copy-done.4, ...), custom_call_target="tpu_custom_call" | custom-call | flops 1 | bytes 10500000 | tf_op jit(solution)/shard_map/place_qkv/pallas_call | solution.py:51
  (168 shorter events, 102.0 us)
Async XLA Ops:
  0.7 12.7 %collective-permute-start.2 = (bf16[128,768]{1,0:T(8,128)(2,1)}, bf16[128,768]{1,0:T(8,128)(2,1)S(1)}, u32[]{:S(2)}, u32[]{:S(2)}) collective-permute-start(bf16[128,768]{1,0:T(8,128)(2,1)} %bitcast.58), channel_id=1, source_target_pairs={{0,6},{1,7},{2,4},{3,5},{4,2},{5,3},{6,0},{7,1},{8,14},{9,15},{10,... | collective-permute-start | bytes 589832 | tf_op jit(solution)/shard_map/hid_6/ppermute | solution.py:787
  8.7 15.0 %collective-permute-start.5 = (bf16[392,384]{1,0:T(8,128)(2,1)}, bf16[392,384]{1,0:T(8,128)(2,1)}, u32[]{:S(2)}, u32[]{:S(2)}) collective-permute-start(bf16[392,384]{1,0:T(8,128)(2,1)} %get-tuple-element.141.mine), channel_id=1, source_target_pairs={{0,8},{8,0},{16,24},{24,16},{1,9},{9,1},{17,25},{25,17},{2,10},{10... | collective-permute-start | bytes 903176 | tf_op jit(solution)/shard_map/qkvw_z1/ppermute | solution.py:794
  10.7 15.6 %collective-permute-start.4 = (bf16[392,384]{1,0:T(8,128)(2,1)}, bf16[392,384]{1,0:T(8,128)(2,1)}, u32[]{:S(2)}, u32[]{:S(2)}) collective-permute-start(bf16[392,384]{1,0:T(8,128)(2,1)} %get-tuple-element.141.mine), channel_id=1, source_target_pairs={{0,16},{8,24},{16,0},{24,8},{1,17},{9,25},{17,1},{25,9},{2,18},{10... | collective-permute-start | bytes 903176 | tf_op jit(solution)/shard_map/qkvw_z2/ppermute | solution.py:794
  16.1 25.8 %collective-permute-start.3 = (bf16[4,128,768]{2,1,0:T(8,128)(2,1)S(1)}, bf16[4,128,768]{2,1,0:T(8,128)(2,1)}, u32[]{:S(2)}, u32[]{:S(2)}) collective-permute-start(bf16[4,128,768]{2,1,0:T(8,128)(2,1)S(1)} %pad_maximum_fusion.2.own_x.x), channel_id=1, source_target_pairs={{0,1},{1,0},{2,3},{3,2},{4,5},{5,4},{6,7},{7,6},{8,9},{9,8},{10,11... | collective-permute-start | bytes 2359304 | tf_op jit(solution)/shard_map/hid_1/ppermute | solution.py:787
  26.3 15.6 %collective-permute-start.6 = (bf16[392,384]{1,0:T(8,128)(2,1)}, bf16[392,384]{1,0:T(8,128)(2,1)}, u32[]{:S(2)}, u32[]{:S(2)}) collective-permute-start(bf16[392,384]{1,0:T(8,128)(2,1)} %collective-permute-done.4.refs_1_), channel_id=1, source_target_pairs={{0,8},{8,0},{16,24},{24,16},{1,9},{9,1},{17,25},{25,17},{2,10},{10... | collective-permute-start | bytes 903176 | tf_op jit(solution)/shard_map/qkvw_z1/ppermute | solution.py:794
  28.0 17.1 %collective-permute-start.11 = (bf16[192,768]{1,0:T(8,128)(2,1)}, bf16[192,768]{1,0:T(8,128)(2,1)}, u32[]{:S(2)}, u32[]{:S(2)}) collective-permute-start(bf16[192,768]{1,0:T(8,128)(2,1)} %prep_mlp.1), channel_id=1, source_target_pairs={{0,8},{8,0},{16,24},{24,16},{1,9},{9,1},{17,25},{25,17},{2,10},{10... | collective-permute-start | bytes 884744 | tf_op jit(solution)/shard_map/mlpw_z1/ppermute | solution.py:794
  29.7 15.4 %collective-permute-start.10 = (bf16[192,768]{1,0:T(8,128)(2,1)}, bf16[192,768]{1,0:T(8,128)(2,1)}, u32[]{:S(2)}, u32[]{:S(2)}) collective-permute-start(bf16[192,768]{1,0:T(8,128)(2,1)} %prep_mlp.1), channel_id=1, source_target_pairs={{0,16},{8,24},{16,0},{24,8},{1,17},{9,25},{17,1},{25,9},{2,18},{10... | collective-permute-start | bytes 884744 | tf_op jit(solution)/shard_map/mlpw_z2/ppermute | solution.py:794
  46.6 10.6 %collective-permute-start.12 = (bf16[192,768]{1,0:T(8,128)(2,1)}, bf16[192,768]{1,0:T(8,128)(2,1)S(1)}, u32[]{:S(2)}, u32[]{:S(2)}) collective-permute-start(bf16[192,768]{1,0:T(8,128)(2,1)} %collective-permute-done.11.refs_0_), channel_id=1, source_target_pairs={{0,1},{1,0},{2,3},{3,2},{4,5},{5,4},{6,7},{7,6},{8,9},{9,8},{10,11... | collective-permute-start | bytes 884744 | tf_op jit(solution)/shard_map/mlpw_1/ppermute | solution.py:787
  46.6 11.9 %collective-permute-start.22 = (bf16[192,768]{1,0:T(8,128)(2,1)}, bf16[192,768]{1,0:T(8,128)(2,1)S(1)}, u32[]{:S(2)}, u32[]{:S(2)}) collective-permute-start(bf16[192,768]{1,0:T(8,128)(2,1)} %collective-permute-done.10.refs_1_), channel_id=1, source_target_pairs={{0,4},{1,5},{2,6},{3,7},{4,0},{5,1},{6,2},{7,3},{8,12},{9,13},{10,... | collective-permute-start | bytes 884744 | tf_op jit(solution)/shard_map/mlpw_4/ppermute | solution.py:787
  47.2 11.3 %collective-permute-start.19 = (bf16[192,768]{1,0:T(8,128)(2,1)}, bf16[192,768]{1,0:T(8,128)(2,1)S(1)}, u32[]{:S(2)}, u32[]{:S(2)}) collective-permute-start(bf16[192,768]{1,0:T(8,128)(2,1)} %collective-permute-done.10.refs_1_), channel_id=1, source_target_pairs={{0,8},{8,0},{16,24},{24,16},{1,9},{9,1},{17,25},{25,17},{2,10},{10... | collective-permute-start | bytes 884744 | tf_op jit(solution)/shard_map/mlpw_z1/ppermute | solution.py:794
  83.5 10.6 %collective-permute-start.30 = (bf16[128,768]{1,0:T(8,128)(2,1)S(1)}, bf16[128,768]{1,0:T(8,128)(2,1)S(1)}, u32[]{:S(2)}, u32[]{:S(2)}) collective-permute-start(bf16[128,768]{1,0:T(8,128)(2,1)S(1)} %collective-permute-done.25.x1), channel_id=1, source_target_pairs={{0,4},{1,5},{2,6},{3,7},{4,0},{5,1},{6,2},{7,3},{8,12},{9,13},{10,... | collective-permute-start | bytes 589832 | tf_op jit(solution)/shard_map/mlpy_x2_4/ppermute | solution.py:787
  89.8 12.7 %collective-permute-start.33 = (bf16[256,768]{1,0:T(8,128)(2,1)S(1)}, bf16[256,768]{1,0:T(8,128)(2,1)S(1)}, u32[]{:S(2)}, u32[]{:S(2)}) collective-permute-start(bf16[256,768]{1,0:T(8,128)(2,1)S(1)} %get-tuple-element.180), channel_id=1, source_target_pairs={{0,4},{1,5},{2,6},{3,7},{4,0},{5,1},{6,2},{7,3},{8,12},{9,13},{10,... | collective-permute-start | bytes 1179656 | tf_op jit(solution)/shard_map/mlpy_a_4/ppermute | solution.py:787
  129.0 18.1 %collective-permute-start.45 = (bf16[192,768]{1,0:T(8,128)(2,1)S(1)}, bf16[192,768]{1,0:T(8,128)(2,1)S(1)}, u32[]{:S(2)}, u32[]{:S(2)}) collective-permute-start(bf16[192,768]{1,0:T(8,128)(2,1)S(1)} %get-tuple-element.223), channel_id=1, source_target_pairs={{0,8},{8,0},{16,24},{24,16},{1,9},{9,1},{17,25},{25,17},{2,10},{10... | collective-permute-start | bytes 884744 | tf_op jit(solution)/shard_map/gm_z1/ppermute | solution.py:794
  130.4 17.3 %collective-permute-start.46 = (bf16[192,768]{1,0:T(8,128)(2,1)S(1)}, bf16[192,768]{1,0:T(8,128)(2,1)S(1)}, u32[]{:S(2)}, u32[]{:S(2)}) collective-permute-start(bf16[192,768]{1,0:T(8,128)(2,1)S(1)} %get-tuple-element.202), channel_id=1, source_target_pairs={{0,8},{8,0},{16,24},{24,16},{1,9},{9,1},{17,25},{25,17},{2,10},{10... | collective-permute-start | bytes 884744 | tf_op jit(solution)/shard_map/gm_z1/ppermute | solution.py:794
  161.3 11.6 %collective-permute-start.52 = (bf16[344,384]{1,0:T(8,128)(2,1)S(1)}, bf16[344,384]{1,0:T(8,128)(2,1)S(1)}, u32[]{:S(2)}, u32[]{:S(2)}) collective-permute-start(bf16[344,384]{1,0:T(8,128)(2,1)S(1)} %get-tuple-element.241), channel_id=1, source_target_pairs={{0,8},{8,0},{16,24},{24,16},{1,9},{9,1},{17,25},{25,17},{2,10},{10... | collective-permute-start | bytes 792584 | tf_op jit(solution)/shard_map/gq_z1/ppermute | solution.py:794
  161.3 12.2 %collective-permute-start.48 = (bf16[2,128,768]{2,1,0:T(8,128)(2,1)S(1)}, bf16[2,128,768]{2,1,0:T(8,128)(2,1)S(1)}, u32[]{:S(2)}, u32[]{:S(2)}) collective-permute-start(bf16[2,128,768]{2,1,0:T(8,128)(2,1)S(1)} %get-tuple-element.233), channel_id=1, source_target_pairs={{0,2},{1,3},{2,0},{3,1},{4,6},{5,7},{6,4},{7,5},{8,10},{9,11},{10,... | collective-permute-start | bytes 1179656 | tf_op jit(solution)/shard_map/ig_2/ppermute | solution.py:787
  163.1 11.1 %collective-permute-start.59 = (bf16[96,768]{1,0:T(8,128)(2,1)S(1)}, bf16[96,768]{1,0:T(8,128)(2,1)S(1)}, u32[]{:S(2)}, u32[]{:S(2)}) collective-permute-start(bf16[96,768]{1,0:T(8,128)(2,1)S(1)} %get-tuple-element.226), channel_id=1, source_target_pairs={{0,16},{8,24},{16,0},{24,8},{1,17},{9,25},{17,1},{25,9},{2,18},{10... | collective-permute-start | bytes 442376 | tf_op jit(solution)/shard_map/gm_z2/ppermute | solution.py:794
  174.8 18.9 %collective-permute-start.62 = (bf16[192,768]{1,0:T(8,128)(2,1)S(1)}, bf16[192,768]{1,0:T(8,128)(2,1)S(1)}, u32[]{:S(2)}, u32[]{:S(2)}) collective-permute-start(bf16[192,768]{1,0:T(8,128)(2,1)S(1)} %sum_mlp.1.p0), channel_id=1, source_target_pairs={{0,6},{1,7},{2,4},{3,5},{4,2},{5,3},{6,0},{7,1},{8,14},{9,15},{10,... | collective-permute-start | bytes 884744 | tf_op jit(solution)/shard_map/gm_6/ppermute | solution.py:787
  177.4 14.1 %collective-permute-start.54 = (bf16[344,384]{1,0:T(8,128)(2,1)S(1)}, bf16[344,384]{1,0:T(8,128)(2,1)S(1)}, u32[]{:S(2)}, u32[]{:S(2)}) collective-permute-start(bf16[344,384]{1,0:T(8,128)(2,1)S(1)} %relay.1), channel_id=1, source_target_pairs={{0,16},{8,24},{16,0},{24,8},{1,17},{9,25},{17,1},{25,9},{2,18},{10... | collective-permute-start | bytes 792584 | tf_op jit(solution)/shard_map/gq_z2/ppermute | solution.py:794
  180.6 12.0 %collective-permute-start.49 = (bf16[128,768]{1,0:T(8,128)(2,1)S(1)}, bf16[128,768]{1,0:T(8,128)(2,1)S(1)}, u32[]{:S(2)}, u32[]{:S(2)}) collective-permute-start(bf16[128,768]{1,0:T(8,128)(2,1)S(1)} %relay_ig.1), channel_id=1, source_target_pairs={{0,4},{1,5},{2,6},{3,7},{4,0},{5,1},{6,2},{7,3},{8,12},{9,13},{10,... | collective-permute-start | bytes 589832 | tf_op jit(solution)/shard_map/ig_4/ppermute | solution.py:787
  181.2 17.1 %collective-permute-start.61 = (bf16[192,768]{1,0:T(8,128)(2,1)S(1)}, bf16[192,768]{1,0:T(8,128)(2,1)S(1)}, u32[]{:S(2)}, u32[]{:S(2)}) collective-permute-start(bf16[192,768]{1,0:T(8,128)(2,1)S(1)} %sum_mlp.1.p0), channel_id=1, source_target_pairs={{0,4},{1,5},{2,6},{3,7},{4,0},{5,1},{6,2},{7,3},{8,12},{9,13},{10,... | collective-permute-start | bytes 884744 | tf_op jit(solution)/shard_map/gm_4/ppermute | solution.py:787
  182.6 15.7 %collective-permute-start.60 = (bf16[192,768]{1,0:T(8,128)(2,1)S(1)}, bf16[192,768]{1,0:T(8,128)(2,1)S(1)}, u32[]{:S(2)}, u32[]{:S(2)}) collective-permute-start(bf16[192,768]{1,0:T(8,128)(2,1)S(1)} %sum_mlp.1.p0), channel_id=1, source_target_pairs={{0,2},{1,3},{2,0},{3,1},{4,6},{5,7},{6,4},{7,5},{8,10},{9,11},{10,... | collective-permute-start | bytes 884744 | tf_op jit(solution)/shard_map/gm_2/ppermute | solution.py:787
  192.6 13.2 %collective-permute-start.56 = (bf16[344,384]{1,0:T(8,128)(2,1)S(1)}, bf16[344,384]{1,0:T(8,128)(2,1)S(1)}, u32[]{:S(2)}, u32[]{:S(2)}) collective-permute-start(bf16[344,384]{1,0:T(8,128)(2,1)S(1)} %sum_qkv.1.p0), channel_id=1, source_target_pairs={{0,4},{1,5},{2,6},{3,7},{4,0},{5,1},{6,2},{7,3},{8,12},{9,13},{10,... | collective-permute-start | bytes 792584 | tf_op jit(solution)/shard_map/gq_4/ppermute | solution.py:787
  193.7 12.1 %collective-permute-start.55 = (bf16[344,384]{1,0:T(8,128)(2,1)S(1)}, bf16[344,384]{1,0:T(8,128)(2,1)S(1)}, u32[]{:S(2)}, u32[]{:S(2)}) collective-permute-start(bf16[344,384]{1,0:T(8,128)(2,1)S(1)} %sum_qkv.1.p0), channel_id=1, source_target_pairs={{0,2},{1,3},{2,0},{3,1},{4,6},{5,7},{6,4},{7,5},{8,10},{9,11},{10,... | collective-permute-start | bytes 792584 | tf_op jit(solution)/shard_map/gq_2/ppermute | solution.py:787
  (51 other events, 383.7 us)

commit v5 on v4

--- a/solution.py
+++ b/solution.py
@@ -843,7 +843,7 @@
         lax.dynamic_slice_in_dim(down_weight, chip_x * side + spot * (side // 4), side // 4, 0),
     )
     own_x = jnp.stack([hid] + [chips(hid, rel, "hid") for rel in range(1, 4)])
-    mlp_z = collect(first_two(mlp_one, "mlpw"), "mlpw")
+    mlp_pair = first_two(after(mlp_one, own_w[2]), "mlpw")
     other_x = across(own_x, 1, "hid")
     other_w = [across(after(piece, other_x), 1, "qkvw") for piece in own_w]
 
@@ -878,13 +878,14 @@
         gather = partial(lax.all_gather, axis_name="ctx", axis_index_groups=sets, tiled=True)
         pk, vv = gather(pk, axis=0), gather(vv, axis=0)
         valid = gather(valid, axis=1)
+    mlp_z = collect(after(mlp_pair, out_far), "mlpw")
     mlp_far = [across(piece, 4, "mlpw") for piece in mlp_z]
+    probs, cx = attend(after(pq, mlp_z[:2]), pk, vv, valid, slots)
+    cx = after(cx, mlp_far[0])
     mlp_core = [across(piece, 1, "mlpw") for piece in mlp_z[:2]]
-    probs, cx = attend(after(pq, mlp_core), pk, vv, valid, slots)
-    cx = after(cx, out_far, mlp_far[0])
     cxs = [cx[0]] + [chips(cx[rel], rel, "cx") for rel in range(1, 4)]
     mlp_core += [across(piece, 1, "mlpw") for piece in [mlp_z[2]] + mlp_far[:2]]
-    cxs = after(cxs, mlp_core)
+    cxs = after(cxs, mlp_far[1])
     *cxs, out_far = lax.optimization_barrier((*cxs, out_far))
     wo = run(
         partial(assemble_out_body, shards),

time: 214 us -> 211 us (0.986)
  waiting for transfers between devices: 82.9 us -> 91.1 us
  starting transfers between devices: 65.1 us -> 57.5 us
    ppermute x13, waiting for transfers between devices: 37.7 us -> 43.7 us  [turn(): return lax.ppermute(value, 'shard', [(i, i ^ shift) for i in range(shards)])]
    ppermute x51, starting transfers between devices: 45.1 us -> 40.5 us  [across(): return lax.ppermute(value, 'ctx', [(i, i ^ mask) for i in range(lanes)])]
    ppermute x13, starting transfers between devices: 20 us -> 17 us  [turn(): return lax.ppermute(value, 'shard', [(i, i ^ shift) for i in range(shards)])]
    ppermute x51, waiting for transfers between devices: 45.2 us -> 47.4 us  [across(): return lax.ppermute(value, 'ctx', [(i, i ^ mask) for i in range(lanes)])]
  transfers between devices with their start and end apart: 64 -> 64, of which waited for: 30 -> 32; matrix products, arithmetic and copies ran while one was open for 1% -> 1% of each run, Pallas kernels for 22% -> 22%
where the time goes in v5:
time: 211 us; the launch traced here: 210 us
  waiting for transfers between devices  91.1 us (43%)
  starting transfers between devices  57.5 us (27%)
  Pallas kernels  56.9 us (27%)
    ppermute x51, waiting for transfers between devices, across(): return lax.ppermute(value, 'ctx', [(i, i ^ mask) for i in range(lanes)])  47.4 us
    pallas_call x25, Pallas kernels, run(): pl.pallas_call(body, out_shape=outs, in_specs=[SMEM] + [VMEM] * len(array...  45.6 us
    ppermute x13, waiting for transfers between devices, turn(): return lax.ppermute(value, 'shard', [(i, i ^ shift) for i in range(shards)])  43.7 us
    ppermute x51, starting transfers between devices, across(): return lax.ppermute(value, 'ctx', [(i, i ^ mask) for i in range(lanes)])  40.5 us
    ppermute x13, starting transfers between devices, turn(): return lax.ppermute(value, 'shard', [(i, i ^ shift) for i in range(shards)])  17 us
    pallas_call x1, Pallas kernels, attend_back(): pl.pallas_call(partial(attend_back_body, step, split), grid=(LOCAL_HEADS,...  5.85 us
    pallas_call x1, Pallas kernels, attend(): pl.pallas_call(partial(attend_body, step), grid=(LOCAL_HEADS,), in_specs=...  5.44 us
  transfers between devices with their start and end apart: 64, of which 32 were waited for; matrix products, arithmetic and copies ran while one was open for 1% of the time, Pallas kernels for 22%

profile of v5, /device:TPU:0, one launch (start us, length us, event | category | flops | bytes accessed | tf_op | source)
XLA Modules:
  0.0 210.4 jit_solution(4634754142828897840)
XLA Ops:
  0.7 4.0 %collective-permute-start.2 = (bf16[128,768]{1,0:T(8,128)(2,1)}, bf16[128,768]{1,0:T(8,128)(2,1)S(1)}, u32[]{:S(2)}, u32[]{:S(2)}) collective-permute-start(bf16[128,768]{1,0:T(8,128)(2,1)} %bitcast.58), channel_id=1, source_target_pairs={{0,6},{1,7},{2,4},{3,5},{4,2},{5,3},{6,0},{7,1},{8,14},{9,15},{10,... | collective-permute-start | bytes 589832 | tf_op jit(solution)/shard_map/hid_6/ppermute | solution.py:787
  16.4 7.3 %collective-permute-done.5.refs_0_ = bf16[392,384]{1,0:T(8,128)(2,1)} collective-permute-done((bf16[392,384]{1,0:T(8,128)(2,1)}, bf16[392,384]{1,0:T(8,128)(2,1)}, u32[]{:S(2)}, u32[]{:S(2)}) %collective-permute-start.5) | collective-permute-done | bytes 301088 | tf_op jit(solution)/shard_map/qkvw_z1/ppermute | solution.py:794
  26.7 6.6 %collective-permute-done.6.refs_2_ = bf16[392,384]{1,0:T(8,128)(2,1)S(1)} collective-permute-done((bf16[392,384]{1,0:T(8,128)(2,1)}, bf16[392,384]{1,0:T(8,128)(2,1)S(1)}, u32[]{:S(2)}, u32[]{:S(2)}) %collective-permute-start.6) | collective-permute-done | bytes 301088 | tf_op jit(solution)/shard_map/qkvw_z1/ppermute | solution.py:794
  37.6 4.5 %qkv.1 = (bf16[2,768,768]{2,1,0:T(8,128)(2,1)S(1)}, bf16[512,384]{1,0:T(8,128)(2,1)S(1)}, bf16[1024,384]{1,0:T(8,128)(2,1)S(1)}, bf16[1024,384]{1,0:T(8,128)(2,1...) custom-call(s32[7]{0:T(128)S(1)} %copy-done.4, ...), custom_call_target="tpu_custom_call" | custom-call | flops 1 | bytes 3000000 | tf_op jit(solution)/shard_map/qkv/pallas_call | solution.py:51
  43.9 5.9 %collective-permute-done.11.refs_0_ = bf16[192,768]{1,0:T(8,128)(2,1)S(1)} collective-permute-done((bf16[192,768]{1,0:T(8,128)(2,1)S(1)}, bf16[192,768]{1,0:T(8,128)(2,1)S(1)}, u32[]{:S(2)}, u32[]{:S(2)}) %collective-permute-start.11) | collective-permute-done | bytes 294944 | tf_op jit(solution)/shard_map/mlpw_z1/ppermute | solution.py:794
  53.7 5.4 %attend.1 = (bf16[3,512,1024]{2,1,0:T(8,128)(2,1)S(1)}, bf16[4,64,384]{2,1,0:T(8,128)(2,1)S(1)}) custom-call(bf16[512,384]{1,0:T(8,128)(2,1)S(1)} %get-tuple-element.161.pq, bf16[1024,384]{1,0:T(8,128)(2,1)S(1)} %get-tuple-element.162.pk, bf16[1024,384]{1,0:T(8,128)(2,1)S(1)} %get-tuple-element.163.vv, f32[1,1024]{1,0:T(1,128)S(1)} %bitcast.63), custom_call_target="tpu_custom_call" | custom-call | flops 1 | bytes 16500000 | tf_op jit(solution)/shard_map/attend/pallas_call | solution.py:290
  73.2 4.8 %collective-permute-done.21.refs_5_ = bf16[192,768]{1,0:T(8,128)(2,1)S(1)} collective-permute-done((bf16[192,768]{1,0:T(8,128)(2,1)S(1)}, bf16[192,768]{1,0:T(8,128)(2,1)S(1)}, u32[]{:S(2)}, u32[]{:S(2)}) %collective-permute-start.21) | collective-permute-done | bytes 294944 | tf_op jit(solution)/shard_map/mlpw_4/ppermute | solution.py:787
  82.9 3.6 %mlp.1 = (bf16[256,768]{1,0:T(8,128)(2,1)S(1)}, bf16[256,768]{1,0:T(8,128)(2,1)S(1)}, f32[256,1536]{1,0:T(8,128)S(1)}, f32[128,768]{1,0:T(8,128)S(1)}, bf16[128,768]{1,0:T(8,128)(2,1)S(1)}) custom-call(s32[7]{0:T(128)S(1)} %copy-done.4, f32[1,1536]{1,0:T(1,128)S(1)} %get-tuple-element.152.bias, bf16[128,768]{1,0:T(8,128)(2,1)S(1)} %get-tuple-element.176.x0, ...), custom_call_target="tpu_custom_call" | custom-call | flops 1 | bytes 10500000 | tf_op jit(solution)/shard_map/mlp/pallas_call | solution.py:51
  88.2 3.7 %collective-permute-done.30.x3 = bf16[128,768]{1,0:T(8,128)(2,1)S(1)} collective-permute-done((bf16[128,768]{1,0:T(8,128)(2,1)S(1)}, bf16[128,768]{1,0:T(8,128)(2,1)S(1)}, u32[]{:S(2)}, u32[]{:S(2)}) %collective-permute-start.30) | collective-permute-done | bytes 196640 | tf_op jit(solution)/shard_map/mlpy_x2_4/ppermute | solution.py:787
  96.2 4.1 %collective-permute-done.33.act_r = bf16[256,768]{1,0:T(8,128)(2,1)S(1)} collective-permute-done((bf16[256,768]{1,0:T(8,128)(2,1)S(1)}, bf16[256,768]{1,0:T(8,128)(2,1)S(1)}, u32[]{:S(2)}, u32[]{:S(2)}) %collective-permute-start.33) | collective-permute-done | bytes 393248 | tf_op jit(solution)/shard_map/mlpy_a_4/ppermute | solution.py:787
  100.3 3.3 %collective-permute-done.32.g2 = bf16[128,768]{1,0:T(8,128)(2,1)S(1)} collective-permute-done((bf16[128,768]{1,0:T(8,128)(2,1)S(1)}, bf16[128,768]{1,0:T(8,128)(2,1)S(1)}, u32[]{:S(2)}, u32[]{:S(2)}) %collective-permute-start.32) | collective-permute-done | bytes 196640 | tf_op jit(solution)/shard_map/mlpy_g1_4/ppermute | solution.py:787
  103.6 3.4 %mlp_back.1 = (bf16[256,768]{1,0:T(8,128)(2,1)S(1)}, bf16[256,768]{1,0:T(8,128)(2,1)S(1)}, f32[8,1536]{1,0:T(8,128)S(1)}, f32[128,768]{1,0:T(8,128)S(1)}, bf16[128,768]{1,0:T(8,128)(2,1)S(1)}) custom-call(s32[7]{0:T(128)S(1)} %copy-done.4, bf16[128,768]{1,0:T(8,128)(2,1)S(1)} %get-tuple-element.185.g0, bf16[128,768]{1,0:T(8,128)(2,1)S(1)} %collective-permute-done.31.g1, ...), custom_call_target="tpu_custom_call" | custom-call | flops 1 | bytes 10500000 | tf_op jit(solution)/shard_map/mlp_back/pallas_call | solution.py:51
  108.7 4.4 %collective-permute-done.34.received = bf16[128,768]{1,0:T(8,128)(2,1)S(1)} collective-permute-done((bf16[128,768]{1,0:T(8,128)(2,1)S(1)}, bf16[128,768]{1,0:T(8,128)(2,1)S(1)}, u32[]{:S(2)}, u32[]{:S(2)}) %collective-permute-start.34) | collective-permute-done | bytes 196640 | tf_op jit(solution)/shard_map/mlpb_2/ppermute | solution.py:787
  118.8 3.5 %mlp_grads.1 = (f32[4,192,768]{2,1,0:T(8,128)S(1)}, bf16[4,192,768]{2,1,0:T(8,128)(2,1)S(1)}) custom-call(s32[7]{0:T(128)S(1)} %copy-done.4, bf16[128,768]{1,0:T(8,128)(2,1)S(1)} %get-tuple-element.176.x0, bf16[128,768]{1,0:T(8,128)(2,1)S(1)} %collective-permute-done.19.x1, bf16[128,768]{1,0:T(8,128)(2,1)S(1)} %collective-permute-done.29.x2, ...), custom_call_target="tpu_custom_call" | custom-call | flops 1 | bytes 9900000 | tf_op jit(solution)/shard_map/mlp_grads/pallas_call | solution.py:51
  137.7 5.9 %attend_back.1 = (f32[512,384]{1,0:T(8,128)S(1)}, f32[512,384]{1,0:T(8,128)S(1)}, f32[512,384]{1,0:T(8,128)S(1)}, bf16[2,512,384]{2,1,0:T(8,128)(2,1)S(1)}) custom-call(bf16[64,384]{1,0:T(8,128)(2,1)S(1)} %get-tuple-element.214.gc0, bf16[64,384]{1,0:T(8,128)(2,1)S(1)} %collective-permute-done.35.gc1, bf16[64,384]{1,0:T(8,128)(2,1)S(1)} %collective-permute-done.36.gc2, ...), custom_call_target="tpu_custom_call" | custom-call | flops 1 | bytes 18000000 | tf_op jit(solution)/shard_map/attend_back/pallas_call | solution.py:375
  147.1 5.1 %qkv_grads.1 = (f32[128,768]{1,0:T(8,128)S(1)}, f32[128,768]{1,0:T(8,128)S(1)}, bf16[2,128,768]{2,1,0:T(8,128)(2,1)S(1)}, f32[4,296,384]{2,1,0:T(8,128)S(1)}, bf16[4,288,384]{2,1,0:T(8,128)(2,1)S(1)}) custom-call(s32[7]{0:T(128)S(1)} %copy-done.4, f32[16,128]{1,0:T(8,128)S(1)} %add_convert_fusion.meta, f32[512,384]{1,0:T(8,128)S(1)} %get-tuple-element.219.dq, ...), custom_call_target="tpu_custom_call" | custom-call | flops 1 | bytes 15000000 | tf_op jit(solution)/shard_map/qkv_grads/pallas_call | solution.py:51
  152.3 2.9 %collective-permute-done.50.one = bf16[96,768]{1,0:T(8,128)(2,1)S(1)} collective-permute-done((bf16[96,768]{1,0:T(8,128)(2,1)S(1)}, bf16[96,768]{1,0:T(8,128)(2,1)S(1)}, u32[]{:S(2)}, u32[]{:S(2)}) %collective-permute-start.50) | collective-permute-done | bytes 147488 | tf_op jit(solution)/shard_map/gm_z2/ppermute | solution.py:794
  162.2 7.8 %collective-permute-done.52.received = bf16[344,384]{1,0:T(8,128)(2,1)S(1)} collective-permute-done((bf16[344,384]{1,0:T(8,128)(2,1)S(1)}, bf16[344,384]{1,0:T(8,128)(2,1)S(1)}, u32[]{:S(2)}, u32[]{:S(2)}) %collective-permute-start.52) | collective-permute-done | bytes 264224 | tf_op jit(solution)/shard_map/gq_z1/ppermute | solution.py:794
  178.2 2.9 %collective-permute-done.53.refs_0_ = bf16[344,384]{1,0:T(8,128)(2,1)S(1)} collective-permute-done((bf16[344,384]{1,0:T(8,128)(2,1)S(1)}, bf16[344,384]{1,0:T(8,128)(2,1)S(1)}, u32[]{:S(2)}, u32[]{:S(2)}) %collective-permute-start.53) | collective-permute-done | bytes 264224 | tf_op jit(solution)/shard_map/gq_z1/ppermute | solution.py:794
  181.8 5.8 %collective-permute-done.54.refs_1_ = bf16[344,384]{1,0:T(8,128)(2,1)S(1)} collective-permute-done((bf16[344,384]{1,0:T(8,128)(2,1)S(1)}, bf16[344,384]{1,0:T(8,128)(2,1)S(1)}, u32[]{:S(2)}, u32[]{:S(2)}) %collective-permute-start.54) | collective-permute-done | bytes 264224 | tf_op jit(solution)/shard_map/gq_z2/ppermute | solution.py:794
  193.1 3.2 %collective-permute-done.61.p2 = bf16[192,768]{1,0:T(8,128)(2,1)S(1)} collective-permute-done((bf16[192,768]{1,0:T(8,128)(2,1)S(1)}, bf16[192,768]{1,0:T(8,128)(2,1)S(1)}, u32[]{:S(2)}, u32[]{:S(2)}) %collective-permute-start.61) | collective-permute-done | bytes 294944 | tf_op jit(solution)/shard_map/gm_4/ppermute | solution.py:787
  198.4 4.5 %collective-permute-done.56.p2 = bf16[344,384]{1,0:T(8,128)(2,1)S(1)} collective-permute-done((bf16[344,384]{1,0:T(8,128)(2,1)S(1)}, bf16[344,384]{1,0:T(8,128)(2,1)S(1)}, u32[]{:S(2)}, u32[]{:S(2)}) %collective-permute-start.56) | collective-permute-done | bytes 264224 | tf_op jit(solution)/shard_map/gq_4/ppermute | solution.py:787
  203.2 3.3 %place_mlp.1 = (f32[192,3072]{1,0:T(8,128)}, f32[768,768]{1,0:T(8,128)}) custom-call(s32[7]{0:T(128)S(1)} %copy-done.4, bf16[192,768]{1,0:T(8,128)(2,1)S(1)} %sum_mlp.1.p0, bf16[192,768]{1,0:T(8,128)(2,1)S(1)} %collective-permute-done.60.p1, bf16[192,768]{1,0:T(8,128)(2,1)S(1)} %collective-permute-done.61.p2, ...), custom_call_target="tpu_custom_call" | custom-call | flops 1 | bytes 9000000 | tf_op jit(solution)/shard_map/place_mlp/pallas_call | solution.py:51
  206.5 3.8 %place_qkv.1 = (f32[4,192,768]{2,1,0:T(8,128)}, f32[192,768]{1,0:T(8,128)}, f32[192,768]{1,0:T(8,128)}, f32[192,768]{1,0:T(8,128)}, f32[4,192]{1,0:T(4,128)}, /*...) custom-call(s32[7]{0:T(128)S(1)} %copy-done.4, ...), custom_call_target="tpu_custom_call" | custom-call | flops 1 | bytes 10500000 | tf_op jit(solution)/shard_map/place_qkv/pallas_call | solution.py:51
  (168 shorter events, 98.7 us)
Async XLA Ops:
  0.7 13.4 %collective-permute-start.2 = (bf16[128,768]{1,0:T(8,128)(2,1)}, bf16[128,768]{1,0:T(8,128)(2,1)S(1)}, u32[]{:S(2)}, u32[]{:S(2)}) collective-permute-start(bf16[128,768]{1,0:T(8,128)(2,1)} %bitcast.58), channel_id=1, source_target_pairs={{0,6},{1,7},{2,4},{3,5},{4,2},{5,3},{6,0},{7,1},{8,14},{9,15},{10,... | collective-permute-start | bytes 589832 | tf_op jit(solution)/shard_map/hid_6/ppermute | solution.py:787
  8.7 15.0 %collective-permute-start.5 = (bf16[392,384]{1,0:T(8,128)(2,1)}, bf16[392,384]{1,0:T(8,128)(2,1)}, u32[]{:S(2)}, u32[]{:S(2)}) collective-permute-start(bf16[392,384]{1,0:T(8,128)(2,1)} %get-tuple-element.144.mine), channel_id=1, source_target_pairs={{0,8},{8,0},{16,24},{24,16},{1,9},{9,1},{17,25},{25,17},{2,10},{10... | collective-permute-start | bytes 903176 | tf_op jit(solution)/shard_map/qkvw_z1/ppermute | solution.py:794
  10.7 15.6 %collective-permute-start.4 = (bf16[392,384]{1,0:T(8,128)(2,1)}, bf16[392,384]{1,0:T(8,128)(2,1)}, u32[]{:S(2)}, u32[]{:S(2)}) collective-permute-start(bf16[392,384]{1,0:T(8,128)(2,1)} %get-tuple-element.144.mine), channel_id=1, source_target_pairs={{0,16},{8,24},{16,0},{24,8},{1,17},{9,25},{17,1},{25,9},{2,18},{10... | collective-permute-start | bytes 903176 | tf_op jit(solution)/shard_map/qkvw_z2/ppermute | solution.py:794
  16.1 17.2 %collective-permute-start.3 = (bf16[4,128,768]{2,1,0:T(8,128)(2,1)S(1)}, bf16[4,128,768]{2,1,0:T(8,128)(2,1)}, u32[]{:S(2)}, u32[]{:S(2)}) collective-permute-start(bf16[4,128,768]{2,1,0:T(8,128)(2,1)S(1)} %pad_maximum_fusion.2.own_x.x), channel_id=1, source_target_pairs={{0,1},{1,0},{2,3},{3,2},{4,5},{5,4},{6,7},{7,6},{8,9},{9,8},{10,11... | collective-permute-start | bytes 2359304 | tf_op jit(solution)/shard_map/hid_1/ppermute | solution.py:787
  34.5 15.2 %collective-permute-start.11 = (bf16[192,768]{1,0:T(8,128)(2,1)S(1)}, bf16[192,768]{1,0:T(8,128)(2,1)S(1)}, u32[]{:S(2)}, u32[]{:S(2)}) collective-permute-start(bf16[192,768]{1,0:T(8,128)(2,1)S(1)} %prep_mlp.1), channel_id=1, source_target_pairs={{0,8},{8,0},{16,24},{24,16},{1,9},{9,1},{17,25},{25,17},{2,10},{10... | collective-permute-start | bytes 884744 | tf_op jit(solution)/shard_map/mlpw_z1/ppermute | solution.py:794
  35.2 16.4 %collective-permute-start.10 = (bf16[192,768]{1,0:T(8,128)(2,1)S(1)}, bf16[192,768]{1,0:T(8,128)(2,1)S(1)}, u32[]{:S(2)}, u32[]{:S(2)}) collective-permute-start(bf16[192,768]{1,0:T(8,128)(2,1)S(1)} %prep_mlp.1), channel_id=1, source_target_pairs={{0,16},{8,24},{16,0},{24,8},{1,17},{9,25},{17,1},{25,9},{2,18},{10... | collective-permute-start | bytes 884744 | tf_op jit(solution)/shard_map/mlpw_z2/ppermute | solution.py:794
  53.2 12.5 %collective-permute-start.17 = (bf16[192,768]{1,0:T(8,128)(2,1)S(1)}, bf16[192,768]{1,0:T(8,128)(2,1)S(1)}, u32[]{:S(2)}, u32[]{:S(2)}) collective-permute-start(bf16[192,768]{1,0:T(8,128)(2,1)S(1)} %collective-permute-done.10.refs_1_), channel_id=1, source_target_pairs={{0,4},{1,5},{2,6},{3,7},{4,0},{5,1},{6,2},{7,3},{8,12},{9,13},{10,... | collective-permute-start | bytes 884744 | tf_op jit(solution)/shard_map/mlpw_4/ppermute | solution.py:787
  53.7 14.9 %collective-permute-start.20 = (bf16[192,768]{1,0:T(8,128)(2,1)S(1)}, bf16[192,768]{1,0:T(8,128)(2,1)S(1)}, u32[]{:S(2)}, u32[]{:S(2)}) collective-permute-start(bf16[192,768]{1,0:T(8,128)(2,1)S(1)} %collective-permute-done.10.refs_1_), channel_id=1, source_target_pairs={{0,8},{8,0},{16,24},{24,16},{1,9},{9,1},{17,25},{25,17},{2,10},{10... | collective-permute-start | bytes 884744 | tf_op jit(solution)/shard_map/mlpw_z1/ppermute | solution.py:794
  81.0 10.9 %collective-permute-start.30 = (bf16[128,768]{1,0:T(8,128)(2,1)S(1)}, bf16[128,768]{1,0:T(8,128)(2,1)S(1)}, u32[]{:S(2)}, u32[]{:S(2)}) collective-permute-start(bf16[128,768]{1,0:T(8,128)(2,1)S(1)} %collective-permute-done.19.x1), channel_id=1, source_target_pairs={{0,4},{1,5},{2,6},{3,7},{4,0},{5,1},{6,2},{7,3},{8,12},{9,13},{10,... | collective-permute-start | bytes 589832 | tf_op jit(solution)/shard_map/mlpy_x2_4/ppermute | solution.py:787
  87.1 13.2 %collective-permute-start.33 = (bf16[256,768]{1,0:T(8,128)(2,1)S(1)}, bf16[256,768]{1,0:T(8,128)(2,1)S(1)}, u32[]{:S(2)}, u32[]{:S(2)}) collective-permute-start(bf16[256,768]{1,0:T(8,128)(2,1)S(1)} %get-tuple-element.186), channel_id=1, source_target_pairs={{0,4},{1,5},{2,6},{3,7},{4,0},{5,1},{6,2},{7,3},{8,12},{9,13},{10,... | collective-permute-start | bytes 1179656 | tf_op jit(solution)/shard_map/mlpy_a_4/ppermute | solution.py:787
  107.6 11.2 %collective-permute-start.39 = (bf16[256,768]{1,0:T(8,128)(2,1)S(1)}, bf16[256,768]{1,0:T(8,128)(2,1)S(1)}, u32[]{:S(2)}, u32[]{:S(2)}) collective-permute-start(bf16[256,768]{1,0:T(8,128)(2,1)S(1)} %get-tuple-element.205), channel_id=1, source_target_pairs={{0,4},{1,5},{2,6},{3,7},{4,0},{5,1},{6,2},{7,3},{8,12},{9,13},{10,... | collective-permute-start | bytes 1179656 | tf_op jit(solution)/shard_map/mlpy_l_4/ppermute | solution.py:787
  126.0 18.2 %collective-permute-start.45 = (bf16[192,768]{1,0:T(8,128)(2,1)S(1)}, bf16[192,768]{1,0:T(8,128)(2,1)S(1)}, u32[]{:S(2)}, u32[]{:S(2)}) collective-permute-start(bf16[192,768]{1,0:T(8,128)(2,1)S(1)} %get-tuple-element.229), channel_id=1, source_target_pairs={{0,8},{8,0},{16,24},{24,16},{1,9},{9,1},{17,25},{25,17},{2,10},{10... | collective-permute-start | bytes 884744 | tf_op jit(solution)/shard_map/gm_z1/ppermute | solution.py:794
  126.3 18.5 %collective-permute-start.46 = (bf16[192,768]{1,0:T(8,128)(2,1)S(1)}, bf16[192,768]{1,0:T(8,128)(2,1)S(1)}, u32[]{:S(2)}, u32[]{:S(2)}) collective-permute-start(bf16[192,768]{1,0:T(8,128)(2,1)S(1)} %get-tuple-element.208), channel_id=1, source_target_pairs={{0,8},{8,0},{16,24},{24,16},{1,9},{9,1},{17,25},{25,17},{2,10},{10... | collective-permute-start | bytes 884744 | tf_op jit(solution)/shard_map/gm_z1/ppermute | solution.py:794
  158.3 11.6 %collective-permute-start.52 = (bf16[344,384]{1,0:T(8,128)(2,1)S(1)}, bf16[344,384]{1,0:T(8,128)(2,1)S(1)}, u32[]{:S(2)}, u32[]{:S(2)}) collective-permute-start(bf16[344,384]{1,0:T(8,128)(2,1)S(1)} %get-tuple-element.247), channel_id=1, source_target_pairs={{0,8},{8,0},{16,24},{24,16},{1,9},{9,1},{17,25},{25,17},{2,10},{10... | collective-permute-start | bytes 792584 | tf_op jit(solution)/shard_map/gq_z1/ppermute | solution.py:794
  158.4 12.2 %collective-permute-start.48 = (bf16[2,128,768]{2,1,0:T(8,128)(2,1)S(1)}, bf16[2,128,768]{2,1,0:T(8,128)(2,1)S(1)}, u32[]{:S(2)}, u32[]{:S(2)}) collective-permute-start(bf16[2,128,768]{2,1,0:T(8,128)(2,1)S(1)} %get-tuple-element.239), channel_id=1, source_target_pairs={{0,2},{1,3},{2,0},{3,1},{4,6},{5,7},{6,4},{7,5},{8,10},{9,11},{10,... | collective-permute-start | bytes 1179656 | tf_op jit(solution)/shard_map/ig_2/ppermute | solution.py:787
  159.7 11.5 %collective-permute-start.59 = (bf16[96,768]{1,0:T(8,128)(2,1)S(1)}, bf16[96,768]{1,0:T(8,128)(2,1)S(1)}, u32[]{:S(2)}, u32[]{:S(2)}) collective-permute-start(bf16[96,768]{1,0:T(8,128)(2,1)S(1)} %get-tuple-element.232), channel_id=1, source_target_pairs={{0,16},{8,24},{16,0},{24,8},{1,17},{9,25},{17,1},{25,9},{2,18},{10... | collective-permute-start | bytes 442376 | tf_op jit(solution)/shard_map/gm_z2/ppermute | solution.py:794
  170.6 10.6 %collective-permute-start.53 = (bf16[344,384]{1,0:T(8,128)(2,1)S(1)}, bf16[344,384]{1,0:T(8,128)(2,1)S(1)}, u32[]{:S(2)}, u32[]{:S(2)}) collective-permute-start(bf16[344,384]{1,0:T(8,128)(2,1)S(1)} %get-tuple-element.248), channel_id=1, source_target_pairs={{0,8},{8,0},{16,24},{24,16},{1,9},{9,1},{17,25},{25,17},{2,10},{10... | collective-permute-start | bytes 792584 | tf_op jit(solution)/shard_map/gq_z1/ppermute | solution.py:794
  171.9 18.9 %collective-permute-start.62 = (bf16[192,768]{1,0:T(8,128)(2,1)S(1)}, bf16[192,768]{1,0:T(8,128)(2,1)S(1)}, u32[]{:S(2)}, u32[]{:S(2)}) collective-permute-start(bf16[192,768]{1,0:T(8,128)(2,1)S(1)} %sum_mlp.1.p0), channel_id=1, source_target_pairs={{0,6},{1,7},{2,4},{3,5},{4,2},{5,3},{6,0},{7,1},{8,14},{9,15},{10,... | collective-permute-start | bytes 884744 | tf_op jit(solution)/shard_map/gm_6/ppermute | solution.py:787
  173.7 13.9 %collective-permute-start.54 = (bf16[344,384]{1,0:T(8,128)(2,1)S(1)}, bf16[344,384]{1,0:T(8,128)(2,1)S(1)}, u32[]{:S(2)}, u32[]{:S(2)}) collective-permute-start(bf16[344,384]{1,0:T(8,128)(2,1)S(1)} %relay.1), channel_id=1, source_target_pairs={{0,16},{8,24},{16,0},{24,8},{1,17},{9,25},{17,1},{25,9},{2,18},{10... | collective-permute-start | bytes 792584 | tf_op jit(solution)/shard_map/gq_z2/ppermute | solution.py:794
  176.2 13.6 %collective-permute-start.49 = (bf16[128,768]{1,0:T(8,128)(2,1)S(1)}, bf16[128,768]{1,0:T(8,128)(2,1)S(1)}, u32[]{:S(2)}, u32[]{:S(2)}) collective-permute-start(bf16[128,768]{1,0:T(8,128)(2,1)S(1)} %relay_ig.1), channel_id=1, source_target_pairs={{0,4},{1,5},{2,6},{3,7},{4,0},{5,1},{6,2},{7,3},{8,12},{9,13},{10,... | collective-permute-start | bytes 589832 | tf_op jit(solution)/shard_map/ig_4/ppermute | solution.py:787
  177.2 19.1 %collective-permute-start.61 = (bf16[192,768]{1,0:T(8,128)(2,1)S(1)}, bf16[192,768]{1,0:T(8,128)(2,1)S(1)}, u32[]{:S(2)}, u32[]{:S(2)}) collective-permute-start(bf16[192,768]{1,0:T(8,128)(2,1)S(1)} %sum_mlp.1.p0), channel_id=1, source_target_pairs={{0,4},{1,5},{2,6},{3,7},{4,0},{5,1},{6,2},{7,3},{8,12},{9,13},{10,... | collective-permute-start | bytes 884744 | tf_op jit(solution)/shard_map/gm_4/ppermute | solution.py:787
  181.2 15.2 %collective-permute-start.60 = (bf16[192,768]{1,0:T(8,128)(2,1)S(1)}, bf16[192,768]{1,0:T(8,128)(2,1)S(1)}, u32[]{:S(2)}, u32[]{:S(2)}) collective-permute-start(bf16[192,768]{1,0:T(8,128)(2,1)S(1)} %sum_mlp.1.p0), channel_id=1, source_target_pairs={{0,2},{1,3},{2,0},{3,1},{4,6},{5,7},{6,4},{7,5},{8,10},{9,11},{10,... | collective-permute-start | bytes 884744 | tf_op jit(solution)/shard_map/gm_2/ppermute | solution.py:787
  189.8 13.2 %collective-permute-start.56 = (bf16[344,384]{1,0:T(8,128)(2,1)S(1)}, bf16[344,384]{1,0:T(8,128)(2,1)S(1)}, u32[]{:S(2)}, u32[]{:S(2)}) collective-permute-start(bf16[344,384]{1,0:T(8,128)(2,1)S(1)} %sum_qkv.1.p0), channel_id=1, source_target_pairs={{0,4},{1,5},{2,6},{3,7},{4,0},{5,1},{6,2},{7,3},{8,12},{9,13},{10,... | collective-permute-start | bytes 792584 | tf_op jit(solution)/shard_map/gq_4/ppermute | solution.py:787
  190.8 12.2 %collective-permute-start.55 = (bf16[344,384]{1,0:T(8,128)(2,1)S(1)}, bf16[344,384]{1,0:T(8,128)(2,1)S(1)}, u32[]{:S(2)}, u32[]{:S(2)}) collective-permute-start(bf16[344,384]{1,0:T(8,128)(2,1)S(1)} %sum_qkv.1.p0), channel_id=1, source_target_pairs={{0,2},{1,3},{2,0},{3,1},{4,6},{5,7},{6,4},{7,5},{8,10},{9,11},{10,... | collective-permute-start | bytes 792584 | tf_op jit(solution)/shard_map/gq_2/ppermute | solution.py:787
  (51 other events, 389.2 us)
